TPU v7x, 256 devices: a whole 4x4x8 slice. The times are simulated.
256 devices in a mesh: gx: 64 (over z, y, core), gy: 4 (over x).
Axes of the slice: x: 4, y: 4, z: 8, core: 2. Of those that a mesh axis runs over, the one named last changes fastest.
Arguments:
- anomalies: float32 [131072, 1024], P(('gx', 'gy')), may hold values from -50 to 50
- obs_rows: int32 [64, 256], replicated, may hold values from 0 to 6143
- obs_var: float32 [64, 256], P('gx'), may hold values from 0.5 to 20
- taper_level: int32 [64, 3, 4], replicated, may hold values from 0 to 3
Outputs:
- posterior: float32 [131072, 1024], P(('gx', 'gy'))
All inputs are finite; a program needn't handle non-finite values.
Results may differ from a plain program's by a relative error of at most 0.035.
The roundings to bfloat16 on the way count: a program that leaves them out, or rounds other values in their place, can miss the bound.
Values may be sent and summed in bfloat16 or wider, within the bound.
No kernel may reach another device: no remote copies, remote signals or barrier semaphores. Data moves between devices by JAX's collectives and lax.ppermute only.
A program may use at most 64 MiB of HBM per device.

v0:
```python
import functools

import jax
import jax.numpy as jnp
from jax import lax
from jax.experimental import pallas as pl
from jax.experimental.pallas import tpu as pltpu
from jax.sharding import PartitionSpec as P

NCOL = 4
NS_STEPS = 12
AXES = ("gx", "gy")
VMEM_LIMIT = 20 << 20
INTERPRET = False
F32 = jnp.float32
BF16 = jnp.bfloat16


def kernel_call(body, out, args, name, flops, smem=(), scratch=()):
    whole = pl.BlockSpec(memory_space=pltpu.VMEM)
    scalar = pl.BlockSpec(memory_space=pltpu.SMEM)
    leaves = [*args, *jax.tree.leaves(out)]
    return pl.pallas_call(
        body,
        out_shape=out,
        in_specs=[scalar if n in smem else whole for n in range(len(args))],
        out_specs=jax.tree.map(lambda _: whole, out),
        scratch_shapes=scratch,
        name=name,
        interpret=INTERPRET,
        cost_estimate=pl.CostEstimate(
            flops=flops,
            bytes_accessed=sum(leaf.size * leaf.dtype.itemsize for leaf in leaves),
            transcendentals=0,
        ),
        compiler_params=pltpu.CompilerParams(vmem_limit_bytes=VMEM_LIMIT),
    )(*args)


def dot(left, right):
    return jnp.dot(left, right, preferred_element_type=F32)


def dot_nt(left, right):
    return lax.dot_general(
        left, right, (((1,), (1,)), ((), ())), preferred_element_type=F32
    )


def halves(value):
    high = value.astype(BF16)
    return high, (value - high.astype(F32)).astype(BF16)


def mat_prod(left, right):
    return dot(left[0], right[0]) + (dot(left[0], right[1]) + dot(left[1], right[0]))


def standing(col, colour, columns):
    offset = lax.rem(col + (NCOL - colour), NCOL)
    slot = jnp.where(offset == 1, 2, jnp.where(offset == 3, 0, 1))
    return slot, offset != 2, lax.rem(col - slot + 1 + columns, columns)


def pick_kernel(colours, state, obs, place, *refs):
    outs, scratch = refs[:-1], refs[-1]
    tiles = len(outs)
    tile_rows = state.shape[0]
    columns, size = obs.shape
    share = size // tiles
    col, tile = place[0, 0], place[0, 1]
    band = state.shape[1] // tiles
    for n, colour in enumerate(colours):
        slot, active, batch = standing(col, colour, columns)
        first = jnp.where(active, (slot * tiles + tile) * tile_rows, -(1 << 20))
        local = obs[pl.ds(batch, 1), :] - first
        row = lax.broadcasted_iota(jnp.int32, (size, size), 0)
        same = row == lax.broadcasted_iota(jnp.int32, (size, size), 1)
        wanted = jnp.sum(jnp.where(same, local.astype(F32), 0.0), axis=1, keepdims=True)
        spots = lax.broadcasted_iota(jnp.int32, (size, tile_rows), 1)
        chosen = jnp.where(spots == wanted.astype(jnp.int32), 1.0, 0.0).astype(BF16)

        def pick_band(m, _):
            lanes = pl.ds(pl.multiple_of(m * band, band), band)
            rest = state[:, lanes]
            high = rest.astype(BF16)
            picked = dot(chosen, high)
            if scratch.dtype == F32:
                rest = rest - high.astype(F32)
                middle = rest.astype(BF16)
                picked = picked + dot(chosen, middle)
                picked = picked + dot(chosen, (rest - middle.astype(F32)).astype(BF16))
            scratch[:, lanes] = picked.astype(scratch.dtype)
            return 0

        lax.fori_loop(0, tiles, pick_band, 0)
        for step, out in enumerate(outs):
            start = pl.multiple_of(lax.rem(tile + step, tiles) * share, share)
            out[n * share : (n + 1) * share, :] = scratch[pl.ds(start, share), :]


def setup_kernel(pairs, tiles, tile_rows, obs, levels, place, own, left, right, *outs):
    columns, size = obs.shape
    share = size // tiles
    col, tile = place[0, 0], place[0, 1]
    members = place[0, 2].astype(F32)
    lane = lax.broadcasted_iota(jnp.int32, (share, size), 1)
    mine = lane == lax.broadcasted_iota(jnp.int32, (share, size), 0) + tile * share

    def factor(source, which):
        slot, active, batch = standing(col, source, columns)
        level = levels[batch, slot * tiles + which].astype(F32) / 3.0
        return jnp.where(active, level, 0.0)

    for (targets, source), out in zip(pairs, outs):
        for n, target in enumerate(targets):
            slot, _, batch = standing(col, target, columns)
            inside = obs[pl.ds(batch, 1), :] - slot * (tiles * tile_rows)
            row = jnp.zeros((1, size), F32)
            for which in range(tiles):
                hit = (inside >= which * tile_rows) & (inside < (which + 1) * tile_rows)
                row = jnp.where(hit, factor(source, which), row)
            column = jnp.sum(jnp.where(mine, row, 0.0), axis=1, keepdims=True)
            out[n * share : (n + 1) * share, :] = column / members
    for colour in range(NCOL):
        outs[len(pairs) + colour][...] = jnp.full((1, 1), factor(colour, tile)) / members
        slot, active, _ = standing(col, colour, columns)
        value = jnp.where(
            active & (slot == 2), left[...], jnp.where(active & (slot == 0), right[...], own[...])
        )
        pieces = [value[:, n * share : (n + 1) * share] for n in range(tiles)]
        ordered = []
        for step in range(tiles):
            source = lax.rem(tile + tiles - step, tiles)
            piece = pieces[0]
            for n in range(1, tiles):
                piece = jnp.where(source == n, pieces[n], piece)
            ordered.append(piece)
        outs[len(pairs) + NCOL + colour][...] = jnp.concatenate(ordered, axis=1)


def root_kernel(*refs):
    *pieces, variance, out = refs
    observed = jnp.concatenate([piece[...] for piece in pieces], axis=0)
    size, members = observed.shape
    row = lax.broadcasted_iota(jnp.int32, (size, size), 0)
    column = lax.broadcasted_iota(jnp.int32, (size, size), 1)
    eye = jnp.where(row == column, 1.0, 0.0).astype(F32)
    gram = dot_nt(observed, observed) / (members - 1) + eye * variance[...]
    trace = jnp.sum(jnp.sum(gram * eye, axis=1, keepdims=True), axis=0, keepdims=True)
    left = gram / trace
    right_h = halves(1.5 * eye - 0.5 * left)
    left_h = halves(mat_prod(halves(left), right_h))

    def next_term(left_h, right_h):
        return halves(1.5 * eye - 0.5 * mat_prod(right_h, left_h))

    def step(_, pair):
        left_h, right_h = pair
        term_h = next_term(left_h, right_h)
        return halves(mat_prod(left_h, term_h)), halves(mat_prod(term_h, right_h))

    left_h, right_h = lax.fori_loop(1, NS_STEPS - 1, step, (left_h, right_h))
    right = mat_prod(next_term(left_h, right_h), right_h)
    inverse_half = (right / jnp.sqrt(trace)).astype(BF16)
    out[...] = dot(inverse_half, observed).astype(BF16)


def summed(parts):
    total = parts[0][...]
    for part in parts[1:]:
        total = total + part[...]
    return total


def rows_kernel(count, *refs):
    *pairs, out = refs[count:]
    rows = summed(refs[:count])
    for transformed, factor in zip(pairs[::2], pairs[1::2]):
        source = transformed[...]
        projected = dot_nt(rows.astype(BF16), source).astype(BF16)
        rows = rows - factor[...] * dot(projected, source)
    out[...] = rows.astype(out.dtype)


def tile_kernel(state, transformed, factor, out):
    value = state[...]
    source = transformed[...]
    projected = dot_nt(value.astype(BF16), source).astype(BF16)
    out[...] = value - factor[...] * dot(projected, source)


def sum_kernel(*refs):
    *parts, out = refs
    out[...] = summed(parts)


def on_device(anomalies, obs_rows, obs_var, taper_level):
    tile_rows, members = anomalies.shape
    batches, size = obs_rows.shape
    columns = lax.axis_size("gx")
    tiles = lax.axis_size("gy")
    share = size // tiles
    col = lax.axis_index("gx")
    tile = lax.axis_index("gy")
    place = jnp.stack([col, tile, jnp.int32(members - 1)]).astype(jnp.int32).reshape(1, 3)
    levels = taper_level.reshape(batches, 3 * tiles)
    everywhere = list(range(columns))

    def hop(value, pairs):
        flat = [
            ((a % columns) * tiles + b % tiles, (c % columns) * tiles + d % tiles)
            for (a, b), (c, d) in pairs
        ]
        return lax.ppermute(value, AXES, flat)

    def along_gy(value, step):
        return hop(value, [((c, n), (c, n + step)) for c in everywhere for n in range(tiles)])

    def along_gx(value, colour, step):
        trio = (-1, 0, 1)
        pairs = [
            ((b + trio[m], n), (b + trio[(m + step) % 3], n))
            for b in range(colour, columns, NCOL)
            for m in range(3)
            for n in range(tiles)
        ]
        pairs += [
            ((b + 2, n), (b + 2, n + 1 - 2 * (n % 2)))
            for b in range(colour, columns, NCOL)
            for n in range(tiles)
        ]
        return hop(value, pairs)

    def beside(value, step):
        return hop(value, [((c, n), (c + step, n)) for c in everywhere for n in range(tiles)])

    def pick(colours, dtype, state):
        shape = jax.ShapeDtypeStruct((len(colours) * share, members), dtype)
        return kernel_call(
            functools.partial(pick_kernel, colours),
            [shape] * tiles,
            [state, obs_rows, place],
            "pick",
            2 * size * tile_rows * members * len(colours) * (1 if dtype == BF16 else 3),
            smem=(2,),
            scratch=[pltpu.VMEM((size, members), dtype)],
        )

    def scattered(parts):
        return [parts[0], *[along_gy(parts[n], n) for n in range(1, tiles)]]

    def added(parts):
        shape = jax.ShapeDtypeStruct(parts[0].shape, parts[0].dtype)
        return kernel_call(sum_kernel, shape, parts, "sum", 1_000_000)

    def joined(rows, colour):
        first, second = (along_gx(rows, colour, step) for step in (1, 2))
        return added([rows, first, second])

    def spread(whole):
        return [whole, *[along_gy(whole, step) for step in range(1, tiles)]]

    def transform(pieces, variance):
        return kernel_call(
            root_kernel,
            jax.ShapeDtypeStruct((size, members), BF16),
            [*pieces, variance],
            "root",
            8_000_000_000,
        )

    def move_tile(state, transformed, factor):
        blocks = 4
        some = pl.BlockSpec((tile_rows // blocks, members), lambda n: (n, 0))
        return pl.pallas_call(
            tile_kernel,
            out_shape=jax.ShapeDtypeStruct(state.shape, F32),
            grid=(blocks,),
            in_specs=[
                some,
                pl.BlockSpec((size, members), lambda n: (0, 0)),
                pl.BlockSpec((1, 1), lambda n: (0, 0)),
            ],
            out_specs=some,
            name="tile",
            interpret=INTERPRET,
            cost_estimate=pl.CostEstimate(
                flops=4 * tile_rows * size * members,
                bytes_accessed=2 * state.size * 4,
                transcendentals=0,
            ),
            compiler_params=pltpu.CompilerParams(vmem_limit_bytes=VMEM_LIMIT),
        )(state, transformed, factor)

    def move(parts, sources, dtype):
        rows = share
        return kernel_call(
            functools.partial(rows_kernel, len(parts)),
            jax.ShapeDtypeStruct((rows, members), dtype),
            [*parts, *[ref for pair in sources for ref in pair]],
            "rows",
            4 * rows * size * members * len(sources),
        )

    together = lax.optimization_barrier
    total0 = added(scattered(pick((0,), BF16, anomalies)))
    picked = [None, *[pick((colour,), F32, anomalies) for colour in range(1, NCOL)]]

    pairs = [((target,), source) for target in range(1, NCOL) for source in range(target)]
    prepared = kernel_call(
        functools.partial(setup_kernel, pairs, tiles, tile_rows),
        [jax.ShapeDtypeStruct((len(t) * share, 1), F32) for t, _ in pairs]
        + [jax.ShapeDtypeStruct((1, 1), F32)] * NCOL
        + [jax.ShapeDtypeStruct((1, size), F32)] * NCOL,
        [obs_rows, levels, place, obs_var, beside(obs_var, 1), beside(obs_var, -1)],
        "setup",
        1_000_000,
        smem=(1, 2),
    )
    row_factor = {(t[0], source): out for (t, source), out in zip(pairs, prepared)}
    tile_factor = prepared[len(pairs) : len(pairs) + NCOL]
    variance = prepared[len(pairs) + NCOL :]

    state = anomalies
    rows = total0
    done = []
    for colour in range(NCOL):
        whole = joined(rows, colour)
        pieces = spread(whole)
        if colour < NCOL - 1:
            coming, _ = together((picked[colour + 1], whole))
            parts = scattered(coming)
        var, state = together((variance[colour], state))
        done.append(transform(pieces, var))
        if colour < NCOL - 1:
            sources = [(done[n], row_factor[colour + 1, n]) for n in range(colour + 1)]
            rows = move(parts, sources, BF16)
        state = move_tile(state, done[colour], tile_factor[colour])
    return state


def solution(mesh):
    in_specs = (P(AXES, None), P(), P("gx", None), P())
    return jax.shard_map(
        on_device,
        mesh=mesh,
        in_specs=in_specs,
        out_specs=P(AXES, None),
        check_vma=False,
    )
```

profile of v0, /device:TPU:6, one launch (start us, length us, event | category | flops | bytes accessed | tf_op | source)
XLA Modules:
  0.0 151.5 jit_solution(8256762079770660071)
XLA Ops:
  0.1 1.6 %copy-done = f32[512,1024]{1,0:T(8,128)S(1)} copy-done((f32[512,1024]{1,0:T(8,128)S(1)}, f32[512,1024]{1,0:T(8,128)}, u32[]{:S(2)}) %copy-start) | copy-done | bytes 2097176
  1.7 0.8 copy-done.2
  2.5 1.7 %pick.4 = (bf16[64,1024]{1,0:T(8,128)(2,1)S(1)}, bf16[64,1024]{1,0:T(8,128)(2,1)S(1)}, bf16[64,1024]{1,0:T(8,128)(2,1)S(1)}, bf16[64,1024]{1,0:T(8,128)(2,1)S(1)}) custom-call(f32[512,1024]{1,0:T(8,128)S(1)} %copy-done, s32[64,256]{1,0:T(8,128)S(1)} %copy-done.2, s32[1,3]{1,0:T(1,128)S(1)} %add_bitcast_fusion.place), custom_call_target="tpu_custom_call" | custom-call | flops 268435456 | bytes 2686988 | tf_op jit(solution)/shard_map/pick/pallas_call | solution.py:23
  4.2 2.3 %collective-permute-start.2 = (bf16[64,1024]{1,0:T(8,128)(2,1)S(1)}, bf16[64,1024]{1,0:T(8,128)(2,1)S(1)}, u32[]{:S(2)}, u32[]{:S(2)}) collective-permute-start(bf16[64,1024]{1,0:T(8,128)(2,1)S(1)} %get-tuple-element.61), channel_id=1, source_target_pairs={{0,1},{1,2},{2,3},{3,0},{4,5},{5,6},{6,7},{7,4},{8,9},{9,10},{10,1... | collective-permute-start | bytes 393224 | tf_op jit(solution)/shard_map/ppermute | solution.py:215
  6.5 0.7 collective-permute-start.3
  7.5 4.3 %collective-permute-done.2.refs_1_ = bf16[64,1024]{1,0:T(8,128)(2,1)S(1)} collective-permute-done((bf16[64,1024]{1,0:T(8,128)(2,1)S(1)}, bf16[64,1024]{1,0:T(8,128)(2,1)S(1)}, u32[]{:S(2)}, u32[]{:S(2)}) %collective-permute-start.2) | collective-permute-done | bytes 131104 | tf_op jit(solution)/shard_map/ppermute | solution.py:215
  11.7 1.5 collective-permute-done.3.refs_2_
  13.2 1.3 collective-permute-done.4.refs_3_
  14.6 6.7 %collective-permute-start.6 = (bf16[64,1024]{1,0:T(8,128)(2,1)S(1)}, bf16[64,1024]{1,0:T(8,128)(2,1)S(1)}, u32[]{:S(2)}, u32[]{:S(2)}) collective-permute-start(bf16[64,1024]{1,0:T(8,128)(2,1)S(1)} %sum.5.refs_0_), channel_id=1, source_target_pairs={{252,4},{253,5},{254,6},{255,7},{0,252},{1,253},{2,254},{3,255},{4... | collective-permute-start | bytes 393224 | tf_op jit(solution)/shard_map/ppermute | solution.py:215
  21.3 2.6 %collective-permute-done.5.refs_1_ = bf16[64,1024]{1,0:T(8,128)(2,1)S(1)} collective-permute-done((bf16[64,1024]{1,0:T(8,128)(2,1)S(1)}, bf16[64,1024]{1,0:T(8,128)(2,1)S(1)}, u32[]{:S(2)}, u32[]{:S(2)}) %collective-permute-start.5) | collective-permute-done | bytes 131104 | tf_op jit(solution)/shard_map/ppermute | solution.py:215
  23.9 0.7 collective-permute-done.6.refs_2_
  24.6 0.8 collective-permute-start.7
  25.4 1.5 collective-permute-start.8
  26.9 0.8 collective-permute-start.9
  27.7 3.1 %collective-permute-start = (f32[1,256]{1,0:T(1,128)S(1)}, f32[1,256]{1,0:T(1,128)S(1)}, u32[]{:S(2)}, u32[]{:S(2)}) collective-permute-start(f32[1,256]{1,0:T(1,128)S(1)} %copy-done.4), channel_id=1, source_target_pairs={{0,4},{1,5},{2,6},{3,7},{4,8},{5,9},{6,10},{7,11},{8,12},{9,13},{1... | collective-permute-start | bytes 3080 | tf_op jit(solution)/shard_map/ppermute | solution.py:215
  30.8 2.0 %collective-permute-start.1 = (f32[1,256]{1,0:T(1,128)S(1)}, f32[1,256]{1,0:T(1,128)S(1)}, u32[]{:S(2)}, u32[]{:S(2)}) collective-permute-start(f32[1,256]{1,0:T(1,128)S(1)} %copy-done.4), channel_id=1, source_target_pairs={{0,252},{1,253},{2,254},{3,255},{4,0},{5,1},{6,2},{7,3},{8,4},{9,5... | collective-permute-start | bytes 3080 | tf_op jit(solution)/shard_map/ppermute | solution.py:215
  32.8 2.4 %pick.5 = (f32[64,1024]{1,0:T(8,128)S(1)}, f32[64,1024]{1,0:T(8,128)S(1)}, f32[64,1024]{1,0:T(8,128)S(1)}, f32[64,1024]{1,0:T(8,128)S(1)}) custom-call(f32[512,1024]{1,0:T(8,128)S(1)} %copy-done.1, s32[64,256]{1,0:T(8,128)S(1)} %copy-done.2, s32[1,3]{1,0:T(1,128)S(1)} %add_bitcast_fusion.place), custom_call_target="tpu_custom_call" | custom-call | flops 805306368 | bytes 3211276 | tf_op jit(solution)/shard_map/pick/pallas_call | solution.py:23
  35.3 1.9 %setup.1 = (f32[64,1]{1,0:T(8,128)S(1)}, f32[64,1]{1,0:T(8,128)S(1)}, f32[64,1]{1,0:T(8,128)S(1)}, f32[64,1]{1,0:T(8,128)S(1)}, f32[64,1]{1,0:T(8,128)S(1)}, /*i...) custom-call(s32[64,256]{1,0:T(8,128)S(1)} %copy-done.3, ...), custom_call_target="tpu_custom_call" | custom-call | flops 1000000 | bytes 77340 | tf_op jit(solution)/shard_map/setup/pallas_call | solution.py:23
  37.2 2.4 %collective-permute-start.10 = (f32[64,1024]{1,0:T(8,128)S(1)}, f32[64,1024]{1,0:T(8,128)S(1)}, u32[]{:S(2)}, u32[]{:S(2)}) collective-permute-start(f32[64,1024]{1,0:T(8,128)S(1)} %get-tuple-element.72), channel_id=1, source_target_pairs={{0,1},{1,2},{2,3},{3,0},{4,5},{5,6},{6,7},{7,4},{8,9},{9,10},{10,1... | collective-permute-start | bytes 786440 | tf_op jit(solution)/shard_map/ppermute | solution.py:215
  39.6 0.8 collective-permute-start.11
  40.5 1.3 collective-permute-start.12
  41.7 9.1 %root.4.transformed.refs_4_ = bf16[256,1024]{1,0:T(8,128)(2,1)S(1)} custom-call(bf16[64,1024]{1,0:T(8,128)(2,1)S(1)} %sum.6.refs_0_, bf16[64,1024]{1,0:T(8,128)(2,1)S(1)} %collective-permute-done.7.refs_1_, bf16[64,1024]{1,0:T(8,128)(2,1)} %collective-permute-done.8.refs_2_, bf16[64,1024]{1,0:T(8,128)(2,1)} %collective-permute-done.9.refs_3_, ...), custom_call_target="tpu_custom_call" | custom-call | flops 8000000000 | bytes 1049600 | tf_op jit(solution)/shard_map/root/pallas_call | solution.py:23
  50.9 2.6 %collective-permute-done.12.refs_3_ = f32[64,1024]{1,0:T(8,128)S(1)} collective-permute-done((f32[64,1024]{1,0:T(8,128)S(1)}, f32[64,1024]{1,0:T(8,128)S(1)}, u32[]{:S(2)}, u32[]{:S(2)}) %collective-permute-start.12) | collective-permute-done | bytes 262176 | tf_op jit(solution)/shard_map/ppermute | solution.py:215
  53.5 0.6 rows.3.refs_0_
  54.2 2.0 %collective-permute-start.14 = (bf16[64,1024]{1,0:T(8,128)(2,1)S(1)}, bf16[64,1024]{1,0:T(8,128)(2,1)S(1)}, u32[]{:S(2)}, u32[]{:S(2)}) collective-permute-start(bf16[64,1024]{1,0:T(8,128)(2,1)S(1)} %rows.3.refs_0_), channel_id=1, source_target_pairs={{0,8},{1,9},{2,10},{3,11},{4,0},{5,1},{6,2},{7,3},{8,4},{9,5},{10,... | collective-permute-start | bytes 393224 | tf_op jit(solution)/shard_map/ppermute | solution.py:215
  56.2 2.9 %collective-permute-done.13.refs_1_ = bf16[64,1024]{1,0:T(8,128)(2,1)S(1)} collective-permute-done((bf16[64,1024]{1,0:T(8,128)(2,1)S(1)}, bf16[64,1024]{1,0:T(8,128)(2,1)S(1)}, u32[]{:S(2)}, u32[]{:S(2)}) %collective-permute-start.13) | collective-permute-done | bytes 131104 | tf_op jit(solution)/shard_map/ppermute | solution.py:215
  59.1 0.7 collective-permute-start.15
  59.8 1.0 collective-permute-start.16
  60.8 0.8 collective-permute-start.17
  61.6 2.4 %pick.6 = (f32[64,1024]{1,0:T(8,128)S(1)}, f32[64,1024]{1,0:T(8,128)S(1)}, f32[64,1024]{1,0:T(8,128)S(1)}, f32[64,1024]{1,0:T(8,128)S(1)}) custom-call(f32[512,1024]{1,0:T(8,128)S(1)} %copy-done.1, s32[64,256]{1,0:T(8,128)S(1)} %copy-done.3, s32[1,3]{1,0:T(1,128)S(1)} %add_bitcast_fusion.place), custom_call_target="tpu_custom_call" | custom-call | flops 805306368 | bytes 3211276 | tf_op jit(solution)/shard_map/pick/pallas_call | solution.py:23
  64.0 3.1 %tile.4.state = f32[512,1024]{1,0:T(8,128)S(1)} custom-call(f32[512,1024]{1,0:T(8,128)S(1)} %copy-done.1, bf16[256,1024]{1,0:T(8,128)(2,1)S(1)} %root.4.transformed.refs_4_, f32[1,1]{1,0:T(1,128)} %get-tuple-element.65.factor), custom_call_target="tpu_custom_call" | custom-call | flops 536870912 | bytes 4194304 | tf_op jit(solution)/shard_map/tile/pallas_call | solution.py:276
  67.1 2.5 %collective-permute-start.18 = (f32[64,1024]{1,0:T(8,128)S(1)}, f32[64,1024]{1,0:T(8,128)S(1)}, u32[]{:S(2)}, u32[]{:S(2)}) collective-permute-start(f32[64,1024]{1,0:T(8,128)S(1)} %get-tuple-element.84), channel_id=1, source_target_pairs={{0,1},{1,2},{2,3},{3,0},{4,5},{5,6},{6,7},{7,4},{8,9},{9,10},{10,1... | collective-permute-start | bytes 786440 | tf_op jit(solution)/shard_map/ppermute | solution.py:215
  69.6 1.5 collective-permute-start.19
  71.1 1.3 collective-permute-start.20
  72.4 8.2 %root.5.transformed.refs_6_ = bf16[256,1024]{1,0:T(8,128)(2,1)S(1)} custom-call(bf16[64,1024]{1,0:T(8,128)(2,1)S(1)} %sum.7.refs_0_, bf16[64,1024]{1,0:T(8,128)(2,1)S(1)} %collective-permute-done.15.refs_1_, bf16[64,1024]{1,0:T(8,128)(2,1)S(1)} %collective-permute-done.16.refs_2_, bf16[64,1024]{1,0:T(8,128)(2,1)S(1)} %collective-permute-done.17.refs_3_, ...), custom_call_target="tpu_custom_call" | custom-call | flops 8000000000 | bytes 1049600 | tf_op jit(solution)/shard_map/root/pallas_call | solution.py:23
  80.6 1.0 collective-permute-done.18.refs_1_
  81.5 3.7 %collective-permute-done.20.refs_3_ = f32[64,1024]{1,0:T(8,128)S(1)} collective-permute-done((f32[64,1024]{1,0:T(8,128)S(1)}, f32[64,1024]{1,0:T(8,128)S(1)}, u32[]{:S(2)}, u32[]{:S(2)}) %collective-permute-start.20) | collective-permute-done | bytes 262176 | tf_op jit(solution)/shard_map/ppermute | solution.py:215
  85.2 1.1 rows.4.refs_0_
  86.5 1.9 %collective-permute-start.22 = (bf16[64,1024]{1,0:T(8,128)(2,1)S(1)}, bf16[64,1024]{1,0:T(8,128)(2,1)S(1)}, u32[]{:S(2)}, u32[]{:S(2)}) collective-permute-start(bf16[64,1024]{1,0:T(8,128)(2,1)S(1)} %rows.4.refs_0_), channel_id=1, source_target_pairs={{4,12},{5,13},{6,14},{7,15},{8,4},{9,5},{10,6},{11,7},{12,8},{13,9... | collective-permute-start | bytes 393224 | tf_op jit(solution)/shard_map/ppermute | solution.py:215
  88.4 2.9 %collective-permute-done.21.refs_1_ = bf16[64,1024]{1,0:T(8,128)(2,1)S(1)} collective-permute-done((bf16[64,1024]{1,0:T(8,128)(2,1)S(1)}, bf16[64,1024]{1,0:T(8,128)(2,1)S(1)}, u32[]{:S(2)}, u32[]{:S(2)}) %collective-permute-start.21) | collective-permute-done | bytes 131104 | tf_op jit(solution)/shard_map/ppermute | solution.py:215
  91.4 1.4 collective-permute-done.22.refs_2_
  92.8 0.8 collective-permute-start.23
  93.6 2.0 %collective-permute-start.24 = (bf16[64,1024]{1,0:T(8,128)(2,1)S(1)}, bf16[64,1024]{1,0:T(8,128)(2,1)S(1)}, u32[]{:S(2)}, u32[]{:S(2)}) collective-permute-start(bf16[64,1024]{1,0:T(8,128)(2,1)S(1)} %sum.8.refs_0_), channel_id=1, source_target_pairs={{0,2},{1,3},{2,0},{3,1},{4,6},{5,7},{6,4},{7,5},{8,10},{9,11},{10,... | collective-permute-start | bytes 393224 | tf_op jit(solution)/shard_map/ppermute | solution.py:215
  95.6 0.3 collective-permute-start.25
  95.9 2.4 %pick.7 = (f32[64,1024]{1,0:T(8,128)S(1)}, f32[64,1024]{1,0:T(8,128)S(1)}, f32[64,1024]{1,0:T(8,128)S(1)}, f32[64,1024]{1,0:T(8,128)S(1)}) custom-call(f32[512,1024]{1,0:T(8,128)S(1)} %copy-done.1, s32[64,256]{1,0:T(8,128)S(1)} %copy-done.3, s32[1,3]{1,0:T(1,128)S(1)} %add_bitcast_fusion.place), custom_call_target="tpu_custom_call" | custom-call | flops 805306368 | bytes 3211276 | tf_op jit(solution)/shard_map/pick/pallas_call | solution.py:23
  98.2 3.0 %tile.5.state = f32[512,1024]{1,0:T(8,128)S(1)} custom-call(f32[512,1024]{1,0:T(8,128)S(1)} %tile.4.state, bf16[256,1024]{1,0:T(8,128)(2,1)S(1)} %root.5.transformed.refs_6_, f32[1,1]{1,0:T(1,128)} %get-tuple-element.77.factor), custom_call_target="tpu_custom_call" | custom-call | flops 536870912 | bytes 4194304 | tf_op jit(solution)/shard_map/tile/pallas_call | solution.py:276
  101.2 3.0 %collective-permute-start.26 = (f32[64,1024]{1,0:T(8,128)S(1)}, f32[64,1024]{1,0:T(8,128)S(1)}, u32[]{:S(2)}, u32[]{:S(2)}) collective-permute-start(f32[64,1024]{1,0:T(8,128)S(1)} %get-tuple-element.97), channel_id=1, source_target_pairs={{0,1},{1,2},{2,3},{3,0},{4,5},{5,6},{6,7},{7,4},{8,9},{9,10},{10,1... | collective-permute-start | bytes 786440 | tf_op jit(solution)/shard_map/ppermute | solution.py:215
  104.3 0.3 collective-permute-start.27
  104.6 1.3 collective-permute-start.28
  105.9 8.2 %root.6.transformed.refs_8_ = bf16[256,1024]{1,0:T(8,128)(2,1)S(1)} custom-call(bf16[64,1024]{1,0:T(8,128)(2,1)S(1)} %sum.8.refs_0_, bf16[64,1024]{1,0:T(8,128)(2,1)S(1)} %collective-permute-done.23.refs_1_, bf16[64,1024]{1,0:T(8,128)(2,1)S(1)} %collective-permute-done.24.refs_2_, bf16[64,1024]{1,0:T(8,128)(2,1)S(1)} %collective-permute-done.25.refs_3_, ...), custom_call_target="tpu_custom_call" | custom-call | flops 8000000000 | bytes 1049600 | tf_op jit(solution)/shard_map/root/pallas_call | solution.py:23
  114.2 2.7 %collective-permute-done.28.refs_3_ = f32[64,1024]{1,0:T(8,128)S(1)} collective-permute-done((f32[64,1024]{1,0:T(8,128)S(1)}, f32[64,1024]{1,0:T(8,128)S(1)}, u32[]{:S(2)}, u32[]{:S(2)}) %collective-permute-start.28) | collective-permute-done | bytes 262176 | tf_op jit(solution)/shard_map/ppermute | solution.py:215
  116.9 1.6 %rows.5.refs_0_ = bf16[64,1024]{1,0:T(8,128)(2,1)S(1)} custom-call(f32[64,1024]{1,0:T(8,128)S(1)} %get-tuple-element.96.refs_0_, f32[64,1024]{1,0:T(8,128)S(1)} %collective-permute-done.26.refs_1_, f32[64,1024]{1,0:T(8,128)S(1)} %collective-permute-done.27.refs_2_, f32[64,1024]{1,0:T(8,128)S(1)} %collective-permute-done.28.refs_3_, ...), custom_call_target="tpu_custom_call" | custom-call | flops 201326592 | bytes 2753280 | tf_op jit(solution)/shard_map/rows/pallas_call | solution.py:23
  118.5 3.9 %collective-permute-start.29 = (bf16[64,1024]{1,0:T(8,128)(2,1)S(1)}, bf16[64,1024]{1,0:T(8,128)(2,1)S(1)}, u32[]{:S(2)}, u32[]{:S(2)}) collective-permute-start(bf16[64,1024]{1,0:T(8,128)(2,1)S(1)} %rows.5.refs_0_), channel_id=1, source_target_pairs={{8,12},{9,13},{10,14},{11,15},{12,16},{13,17},{14,18},{15,19},{16,... | collective-permute-start | bytes 393224 | tf_op jit(solution)/shard_map/ppermute | solution.py:215
  122.4 1.3 collective-permute-start.30
  123.6 2.6 %collective-permute-done.29.refs_1_ = bf16[64,1024]{1,0:T(8,128)(2,1)S(1)} collective-permute-done((bf16[64,1024]{1,0:T(8,128)(2,1)S(1)}, bf16[64,1024]{1,0:T(8,128)(2,1)S(1)}, u32[]{:S(2)}, u32[]{:S(2)}) %collective-permute-start.29) | collective-permute-done | bytes 131104 | tf_op jit(solution)/shard_map/ppermute | solution.py:215
  126.3 4.4 %collective-permute-done.30.refs_2_ = bf16[64,1024]{1,0:T(8,128)(2,1)S(1)} collective-permute-done((bf16[64,1024]{1,0:T(8,128)(2,1)S(1)}, bf16[64,1024]{1,0:T(8,128)(2,1)S(1)}, u32[]{:S(2)}, u32[]{:S(2)}) %collective-permute-start.30) | collective-permute-done | bytes 131104 | tf_op jit(solution)/shard_map/ppermute | solution.py:215
  130.7 0.7 collective-permute-start.31
  131.4 1.5 collective-permute-start.32
  132.9 0.8 collective-permute-start.33
  133.7 3.0 %tile.6.state = f32[512,1024]{1,0:T(8,128)S(1)} custom-call(f32[512,1024]{1,0:T(8,128)S(1)} %tile.5.state, bf16[256,1024]{1,0:T(8,128)(2,1)S(1)} %root.6.transformed.refs_8_, f32[1,1]{1,0:T(1,128)} %get-tuple-element.90.factor), custom_call_target="tpu_custom_call" | custom-call | flops 536870912 | bytes 4194304 | tf_op jit(solution)/shard_map/tile/pallas_call | solution.py:276
  136.7 1.2 collective-permute-done.32.refs_2_
  137.8 1.4 collective-permute-done.33.refs_3_
  139.2 8.2 %root.7.transformed = bf16[256,1024]{1,0:T(8,128)(2,1)S(1)} custom-call(bf16[64,1024]{1,0:T(8,128)(2,1)S(1)} %sum.9.refs_0_, bf16[64,1024]{1,0:T(8,128)(2,1)S(1)} %collective-permute-done.31.refs_1_, bf16[64,1024]{1,0:T(8,128)(2,1)S(1)} %collective-permute-done.32.refs_2_, bf16[64,1024]{1,0:T(8,128)(2,1)S(1)} %collective-permute-done.33.refs_3_, ...), custom_call_target="tpu_custom_call" | custom-call | flops 8000000000 | bytes 1049600 | tf_op jit(solution)/shard_map/root/pallas_call | solution.py:23
  147.4 4.1 %tile.7 = f32[512,1024]{1,0:T(8,128)} custom-call(f32[512,1024]{1,0:T(8,128)S(1)} %tile.6.state, bf16[256,1024]{1,0:T(8,128)(2,1)S(1)} %root.7.transformed, f32[1,1]{1,0:T(1,128)} %get-tuple-element.104.factor), custom_call_target="tpu_custom_call" | custom-call | flops 536870912 | bytes 4194304 | tf_op jit(solution)/shard_map/tile/pallas_call | solution.py:276
  (40 shorter events, 1.1 us)
Async XLA Ops:
  0.0 27.7 %copy-start.4 = (f32[1,256]{1,0:T(1,128)S(1)}, f32[1,256]{1,0:T(1,128)}, u32[]{:S(2)}) copy-start(f32[1,256]{1,0:T(1,128)} %own.1) | copy-start | bytes 3076
  0.1 1.6 %copy-start = (f32[512,1024]{1,0:T(8,128)S(1)}, f32[512,1024]{1,0:T(8,128)}, u32[]{:S(2)}) copy-start(f32[512,1024]{1,0:T(8,128)} %state.8) | copy-start | bytes 6291460
  1.7 0.8 copy-start.2
  2.5 30.3 %copy-start.1 = (f32[512,1024]{1,0:T(8,128)S(1)}, f32[512,1024]{1,0:T(8,128)}, u32[]{:S(2)}) copy-start(f32[512,1024]{1,0:T(8,128)} %state.8) | copy-start | bytes 6291460
  4.2 31.0 %copy-start.5 = (s32[64,3,4]{0,2,1:T(4,128)S(1)}, s32[64,3,4]{0,2,1:T(4,128)}, u32[]{:S(2)}) copy-start(s32[64,3,4]{0,2,1:T(4,128)} %param.7) | copy-start | bytes 9220
  4.2 7.5 %collective-permute-start.2 = (bf16[64,1024]{1,0:T(8,128)(2,1)S(1)}, bf16[64,1024]{1,0:T(8,128)(2,1)S(1)}, u32[]{:S(2)}, u32[]{:S(2)}) collective-permute-start(bf16[64,1024]{1,0:T(8,128)(2,1)S(1)} %get-tuple-element.61), channel_id=1, source_target_pairs={{0,1},{1,2},{2,3},{3,0},{4,5},{5,6},{6,7},{7,4},{8,9},{9,10},{10,1... | collective-permute-start | bytes 393224 | tf_op jit(solution)/shard_map/ppermute | solution.py:215
  6.5 6.7 %collective-permute-start.3 = (bf16[64,1024]{1,0:T(8,128)(2,1)S(1)}, bf16[64,1024]{1,0:T(8,128)(2,1)S(1)}, u32[]{:S(2)}, u32[]{:S(2)}) collective-permute-start(bf16[64,1024]{1,0:T(8,128)(2,1)S(1)} %get-tuple-element.62), channel_id=1, source_target_pairs={{0,2},{1,3},{2,0},{3,1},{4,6},{5,7},{6,4},{7,5},{8,10},{9,11},{10,... | collective-permute-start | bytes 393224 | tf_op jit(solution)/shard_map/ppermute | solution.py:215
  7.2 7.3 %collective-permute-start.4 = (bf16[64,1024]{1,0:T(8,128)(2,1)S(1)}, bf16[64,1024]{1,0:T(8,128)(2,1)S(1)}, u32[]{:S(2)}, u32[]{:S(2)}) collective-permute-start(bf16[64,1024]{1,0:T(8,128)(2,1)S(1)} %get-tuple-element.63), channel_id=1, source_target_pairs={{0,3},{1,0},{2,1},{3,2},{4,7},{5,4},{6,5},{7,6},{8,11},{9,8},{10,9... | collective-permute-start | bytes 393224 | tf_op jit(solution)/shard_map/ppermute | solution.py:215
  14.5 20.8 %copy-start.3 = (s32[64,256]{1,0:T(8,128)S(1)}, s32[64,256]{1,0:T(8,128)}, u32[]{:S(2)}) copy-start(s32[64,256]{1,0:T(8,128)} %obs.9) | copy-start | bytes 196612
  14.5 9.4 %collective-permute-start.5 = (bf16[64,1024]{1,0:T(8,128)(2,1)S(1)}, bf16[64,1024]{1,0:T(8,128)(2,1)S(1)}, u32[]{:S(2)}, u32[]{:S(2)}) collective-permute-start(bf16[64,1024]{1,0:T(8,128)(2,1)S(1)} %sum.5.refs_0_), channel_id=1, source_target_pairs={{252,0},{253,1},{254,2},{255,3},{0,4},{1,5},{2,6},{3,7},{4,252},{5... | collective-permute-start | bytes 393224 | tf_op jit(solution)/shard_map/ppermute | solution.py:215
  14.6 9.9 %collective-permute-start.6 = (bf16[64,1024]{1,0:T(8,128)(2,1)S(1)}, bf16[64,1024]{1,0:T(8,128)(2,1)S(1)}, u32[]{:S(2)}, u32[]{:S(2)}) collective-permute-start(bf16[64,1024]{1,0:T(8,128)(2,1)S(1)} %sum.5.refs_0_), channel_id=1, source_target_pairs={{252,4},{253,5},{254,6},{255,7},{0,252},{1,253},{2,254},{3,255},{4... | collective-permute-start | bytes 393224 | tf_op jit(solution)/shard_map/ppermute | solution.py:215
  24.6 15.9 %collective-permute-start.7 = (bf16[64,1024]{1,0:T(8,128)(2,1)S(1)}, bf16[64,1024]{1,0:T(8,128)(2,1)S(1)}, u32[]{:S(2)}, u32[]{:S(2)}) collective-permute-start(bf16[64,1024]{1,0:T(8,128)(2,1)S(1)} %sum.6.refs_0_), channel_id=1, source_target_pairs={{0,1},{1,2},{2,3},{3,0},{4,5},{5,6},{6,7},{7,4},{8,9},{9,10},{10,1... | collective-permute-start | bytes 393224 | tf_op jit(solution)/shard_map/ppermute | solution.py:215
  25.4 16.3 %collective-permute-start.8 = (bf16[64,1024]{1,0:T(8,128)(2,1)S(1)}, bf16[64,1024]{1,0:T(8,128)(2,1)}, u32[]{:S(2)}, u32[]{:S(2)}) collective-permute-start(bf16[64,1024]{1,0:T(8,128)(2,1)S(1)} %sum.6.refs_0_), channel_id=1, source_target_pairs={{0,2},{1,3},{2,0},{3,1},{4,6},{5,7},{6,4},{7,5},{8,10},{9,11},{10,... | collective-permute-start | bytes 393224 | tf_op jit(solution)/shard_map/ppermute | solution.py:215
  26.9 14.8 %collective-permute-start.9 = (bf16[64,1024]{1,0:T(8,128)(2,1)S(1)}, bf16[64,1024]{1,0:T(8,128)(2,1)}, u32[]{:S(2)}, u32[]{:S(2)}) collective-permute-start(bf16[64,1024]{1,0:T(8,128)(2,1)S(1)} %sum.6.refs_0_), channel_id=1, source_target_pairs={{0,3},{1,0},{2,1},{3,2},{4,7},{5,4},{6,5},{7,6},{8,11},{9,8},{10,9... | collective-permute-start | bytes 393224 | tf_op jit(solution)/shard_map/ppermute | solution.py:215
  27.7 7.6 %collective-permute-start = (f32[1,256]{1,0:T(1,128)S(1)}, f32[1,256]{1,0:T(1,128)S(1)}, u32[]{:S(2)}, u32[]{:S(2)}) collective-permute-start(f32[1,256]{1,0:T(1,128)S(1)} %copy-done.4), channel_id=1, source_target_pairs={{0,4},{1,5},{2,6},{3,7},{4,8},{5,9},{6,10},{7,11},{8,12},{9,13},{1... | collective-permute-start | bytes 3080 | tf_op jit(solution)/shard_map/ppermute | solution.py:215
  30.8 4.5 %collective-permute-start.1 = (f32[1,256]{1,0:T(1,128)S(1)}, f32[1,256]{1,0:T(1,128)S(1)}, u32[]{:S(2)}, u32[]{:S(2)}) collective-permute-start(f32[1,256]{1,0:T(1,128)S(1)} %copy-done.4), channel_id=1, source_target_pairs={{0,252},{1,253},{2,254},{3,255},{4,0},{5,1},{6,2},{7,3},{8,4},{9,5... | collective-permute-start | bytes 3080 | tf_op jit(solution)/shard_map/ppermute | solution.py:215
  37.2 13.7 %collective-permute-start.10 = (f32[64,1024]{1,0:T(8,128)S(1)}, f32[64,1024]{1,0:T(8,128)S(1)}, u32[]{:S(2)}, u32[]{:S(2)}) collective-permute-start(f32[64,1024]{1,0:T(8,128)S(1)} %get-tuple-element.72), channel_id=1, source_target_pairs={{0,1},{1,2},{2,3},{3,0},{4,5},{5,6},{6,7},{7,4},{8,9},{9,10},{10,1... | collective-permute-start | bytes 786440 | tf_op jit(solution)/shard_map/ppermute | solution.py:215
  39.6 11.3 %collective-permute-start.11 = (f32[64,1024]{1,0:T(8,128)S(1)}, f32[64,1024]{1,0:T(8,128)S(1)}, u32[]{:S(2)}, u32[]{:S(2)}) collective-permute-start(f32[64,1024]{1,0:T(8,128)S(1)} %get-tuple-element.73), channel_id=1, source_target_pairs={{0,2},{1,3},{2,0},{3,1},{4,6},{5,7},{6,4},{7,5},{8,10},{9,11},{10,... | collective-permute-start | bytes 786440 | tf_op jit(solution)/shard_map/ppermute | solution.py:215
  40.5 13.0 %collective-permute-start.12 = (f32[64,1024]{1,0:T(8,128)S(1)}, f32[64,1024]{1,0:T(8,128)S(1)}, u32[]{:S(2)}, u32[]{:S(2)}) collective-permute-start(f32[64,1024]{1,0:T(8,128)S(1)} %get-tuple-element.74), channel_id=1, source_target_pairs={{0,3},{1,0},{2,1},{3,2},{4,7},{5,4},{6,5},{7,6},{8,11},{9,8},{10,9... | collective-permute-start | bytes 786440 | tf_op jit(solution)/shard_map/ppermute | solution.py:215
  54.1 5.0 %collective-permute-start.13 = (bf16[64,1024]{1,0:T(8,128)(2,1)S(1)}, bf16[64,1024]{1,0:T(8,128)(2,1)S(1)}, u32[]{:S(2)}, u32[]{:S(2)}) collective-permute-start(bf16[64,1024]{1,0:T(8,128)(2,1)S(1)} %rows.3.refs_0_), channel_id=1, source_target_pairs={{0,4},{1,5},{2,6},{3,7},{4,8},{5,9},{6,10},{7,11},{8,0},{9,1},{10,... | collective-permute-start | bytes 393224 | tf_op jit(solution)/shard_map/ppermute | solution.py:215
  54.2 5.0 %collective-permute-start.14 = (bf16[64,1024]{1,0:T(8,128)(2,1)S(1)}, bf16[64,1024]{1,0:T(8,128)(2,1)S(1)}, u32[]{:S(2)}, u32[]{:S(2)}) collective-permute-start(bf16[64,1024]{1,0:T(8,128)(2,1)S(1)} %rows.3.refs_0_), channel_id=1, source_target_pairs={{0,8},{1,9},{2,10},{3,11},{4,0},{5,1},{6,2},{7,3},{8,4},{9,5},{10,... | collective-permute-start | bytes 393224 | tf_op jit(solution)/shard_map/ppermute | solution.py:215
  59.1 11.9 %collective-permute-start.15 = (bf16[64,1024]{1,0:T(8,128)(2,1)S(1)}, bf16[64,1024]{1,0:T(8,128)(2,1)S(1)}, u32[]{:S(2)}, u32[]{:S(2)}) collective-permute-start(bf16[64,1024]{1,0:T(8,128)(2,1)S(1)} %sum.7.refs_0_), channel_id=1, source_target_pairs={{0,1},{1,2},{2,3},{3,0},{4,5},{5,6},{6,7},{7,4},{8,9},{9,10},{10,1... | collective-permute-start | bytes 393224 | tf_op jit(solution)/shard_map/ppermute | solution.py:215
  59.8 12.6 %collective-permute-start.16 = (bf16[64,1024]{1,0:T(8,128)(2,1)S(1)}, bf16[64,1024]{1,0:T(8,128)(2,1)S(1)}, u32[]{:S(2)}, u32[]{:S(2)}) collective-permute-start(bf16[64,1024]{1,0:T(8,128)(2,1)S(1)} %sum.7.refs_0_), channel_id=1, source_target_pairs={{0,2},{1,3},{2,0},{3,1},{4,6},{5,7},{6,4},{7,5},{8,10},{9,11},{10,... | collective-permute-start | bytes 393224 | tf_op jit(solution)/shard_map/ppermute | solution.py:215
  60.8 11.6 %collective-permute-start.17 = (bf16[64,1024]{1,0:T(8,128)(2,1)S(1)}, bf16[64,1024]{1,0:T(8,128)(2,1)S(1)}, u32[]{:S(2)}, u32[]{:S(2)}) collective-permute-start(bf16[64,1024]{1,0:T(8,128)(2,1)S(1)} %sum.7.refs_0_), channel_id=1, source_target_pairs={{0,3},{1,0},{2,1},{3,2},{4,7},{5,4},{6,5},{7,6},{8,11},{9,8},{10,9... | collective-permute-start | bytes 393224 | tf_op jit(solution)/shard_map/ppermute | solution.py:215
  67.1 14.4 %collective-permute-start.18 = (f32[64,1024]{1,0:T(8,128)S(1)}, f32[64,1024]{1,0:T(8,128)S(1)}, u32[]{:S(2)}, u32[]{:S(2)}) collective-permute-start(f32[64,1024]{1,0:T(8,128)S(1)} %get-tuple-element.84), channel_id=1, source_target_pairs={{0,1},{1,2},{2,3},{3,0},{4,5},{5,6},{6,7},{7,4},{8,9},{9,10},{10,1... | collective-permute-start | bytes 786440 | tf_op jit(solution)/shard_map/ppermute | solution.py:215
  69.6 11.9 %collective-permute-start.19 = (f32[64,1024]{1,0:T(8,128)S(1)}, f32[64,1024]{1,0:T(8,128)S(1)}, u32[]{:S(2)}, u32[]{:S(2)}) collective-permute-start(f32[64,1024]{1,0:T(8,128)S(1)} %get-tuple-element.85), channel_id=1, source_target_pairs={{0,2},{1,3},{2,0},{3,1},{4,6},{5,7},{6,4},{7,5},{8,10},{9,11},{10,... | collective-permute-start | bytes 786440 | tf_op jit(solution)/shard_map/ppermute | solution.py:215
  71.1 14.1 %collective-permute-start.20 = (f32[64,1024]{1,0:T(8,128)S(1)}, f32[64,1024]{1,0:T(8,128)S(1)}, u32[]{:S(2)}, u32[]{:S(2)}) collective-permute-start(f32[64,1024]{1,0:T(8,128)S(1)} %get-tuple-element.86), channel_id=1, source_target_pairs={{0,3},{1,0},{2,1},{3,2},{4,7},{5,4},{6,5},{7,6},{8,11},{9,8},{10,9... | collective-permute-start | bytes 786440 | tf_op jit(solution)/shard_map/ppermute | solution.py:215
  86.3 5.0 %collective-permute-start.21 = (bf16[64,1024]{1,0:T(8,128)(2,1)S(1)}, bf16[64,1024]{1,0:T(8,128)(2,1)S(1)}, u32[]{:S(2)}, u32[]{:S(2)}) collective-permute-start(bf16[64,1024]{1,0:T(8,128)(2,1)S(1)} %rows.4.refs_0_), channel_id=1, source_target_pairs={{4,8},{5,9},{6,10},{7,11},{8,12},{9,13},{10,14},{11,15},{12,4},{13... | collective-permute-start | bytes 393224 | tf_op jit(solution)/shard_map/ppermute | solution.py:215
  86.5 6.3 %collective-permute-start.22 = (bf16[64,1024]{1,0:T(8,128)(2,1)S(1)}, bf16[64,1024]{1,0:T(8,128)(2,1)S(1)}, u32[]{:S(2)}, u32[]{:S(2)}) collective-permute-start(bf16[64,1024]{1,0:T(8,128)(2,1)S(1)} %rows.4.refs_0_), channel_id=1, source_target_pairs={{4,12},{5,13},{6,14},{7,15},{8,4},{9,5},{10,6},{11,7},{12,8},{13,9... | collective-permute-start | bytes 393224 | tf_op jit(solution)/shard_map/ppermute | solution.py:215
  92.8 11.8 %collective-permute-start.23 = (bf16[64,1024]{1,0:T(8,128)(2,1)S(1)}, bf16[64,1024]{1,0:T(8,128)(2,1)S(1)}, u32[]{:S(2)}, u32[]{:S(2)}) collective-permute-start(bf16[64,1024]{1,0:T(8,128)(2,1)S(1)} %sum.8.refs_0_), channel_id=1, source_target_pairs={{0,1},{1,2},{2,3},{3,0},{4,5},{5,6},{6,7},{7,4},{8,9},{9,10},{10,1... | collective-permute-start | bytes 393224 | tf_op jit(solution)/shard_map/ppermute | solution.py:215
  93.6 12.3 %collective-permute-start.24 = (bf16[64,1024]{1,0:T(8,128)(2,1)S(1)}, bf16[64,1024]{1,0:T(8,128)(2,1)S(1)}, u32[]{:S(2)}, u32[]{:S(2)}) collective-permute-start(bf16[64,1024]{1,0:T(8,128)(2,1)S(1)} %sum.8.refs_0_), channel_id=1, source_target_pairs={{0,2},{1,3},{2,0},{3,1},{4,6},{5,7},{6,4},{7,5},{8,10},{9,11},{10,... | collective-permute-start | bytes 393224 | tf_op jit(solution)/shard_map/ppermute | solution.py:215
  95.6 10.3 %collective-permute-start.25 = (bf16[64,1024]{1,0:T(8,128)(2,1)S(1)}, bf16[64,1024]{1,0:T(8,128)(2,1)S(1)}, u32[]{:S(2)}, u32[]{:S(2)}) collective-permute-start(bf16[64,1024]{1,0:T(8,128)(2,1)S(1)} %sum.8.refs_0_), channel_id=1, source_target_pairs={{0,3},{1,0},{2,1},{3,2},{4,7},{5,4},{6,5},{7,6},{8,11},{9,8},{10,9... | collective-permute-start | bytes 393224 | tf_op jit(solution)/shard_map/ppermute | solution.py:215
  101.2 12.9 %collective-permute-start.26 = (f32[64,1024]{1,0:T(8,128)S(1)}, f32[64,1024]{1,0:T(8,128)S(1)}, u32[]{:S(2)}, u32[]{:S(2)}) collective-permute-start(f32[64,1024]{1,0:T(8,128)S(1)} %get-tuple-element.97), channel_id=1, source_target_pairs={{0,1},{1,2},{2,3},{3,0},{4,5},{5,6},{6,7},{7,4},{8,9},{9,10},{10,1... | collective-permute-start | bytes 786440 | tf_op jit(solution)/shard_map/ppermute | solution.py:215
  104.3 9.9 %collective-permute-start.27 = (f32[64,1024]{1,0:T(8,128)S(1)}, f32[64,1024]{1,0:T(8,128)S(1)}, u32[]{:S(2)}, u32[]{:S(2)}) collective-permute-start(f32[64,1024]{1,0:T(8,128)S(1)} %get-tuple-element.98), channel_id=1, source_target_pairs={{0,2},{1,3},{2,0},{3,1},{4,6},{5,7},{6,4},{7,5},{8,10},{9,11},{10,... | collective-permute-start | bytes 786440 | tf_op jit(solution)/shard_map/ppermute | solution.py:215
  104.6 12.3 %collective-permute-start.28 = (f32[64,1024]{1,0:T(8,128)S(1)}, f32[64,1024]{1,0:T(8,128)S(1)}, u32[]{:S(2)}, u32[]{:S(2)}) collective-permute-start(f32[64,1024]{1,0:T(8,128)S(1)} %get-tuple-element.99), channel_id=1, source_target_pairs={{0,3},{1,0},{2,1},{3,2},{4,7},{5,4},{6,5},{7,6},{8,11},{9,8},{10,9... | collective-permute-start | bytes 786440 | tf_op jit(solution)/shard_map/ppermute | solution.py:215
  118.5 7.8 %collective-permute-start.29 = (bf16[64,1024]{1,0:T(8,128)(2,1)S(1)}, bf16[64,1024]{1,0:T(8,128)(2,1)S(1)}, u32[]{:S(2)}, u32[]{:S(2)}) collective-permute-start(bf16[64,1024]{1,0:T(8,128)(2,1)S(1)} %rows.5.refs_0_), channel_id=1, source_target_pairs={{8,12},{9,13},{10,14},{11,15},{12,16},{13,17},{14,18},{15,19},{16,... | collective-permute-start | bytes 393224 | tf_op jit(solution)/shard_map/ppermute | solution.py:215
  122.4 8.3 %collective-permute-start.30 = (bf16[64,1024]{1,0:T(8,128)(2,1)S(1)}, bf16[64,1024]{1,0:T(8,128)(2,1)S(1)}, u32[]{:S(2)}, u32[]{:S(2)}) collective-permute-start(bf16[64,1024]{1,0:T(8,128)(2,1)S(1)} %rows.5.refs_0_), channel_id=1, source_target_pairs={{8,16},{9,17},{10,18},{11,19},{12,8},{13,9},{14,10},{15,11},{16,12... | collective-permute-start | bytes 393224 | tf_op jit(solution)/shard_map/ppermute | solution.py:215
  130.7 6.0 %collective-permute-start.31 = (bf16[64,1024]{1,0:T(8,128)(2,1)S(1)}, bf16[64,1024]{1,0:T(8,128)(2,1)S(1)}, u32[]{:S(2)}, u32[]{:S(2)}) collective-permute-start(bf16[64,1024]{1,0:T(8,128)(2,1)S(1)} %sum.9.refs_0_), channel_id=1, source_target_pairs={{0,1},{1,2},{2,3},{3,0},{4,5},{5,6},{6,7},{7,4},{8,9},{9,10},{10,1... | collective-permute-start | bytes 393224 | tf_op jit(solution)/shard_map/ppermute | solution.py:215
  131.4 6.5 %collective-permute-start.32 = (bf16[64,1024]{1,0:T(8,128)(2,1)S(1)}, bf16[64,1024]{1,0:T(8,128)(2,1)S(1)}, u32[]{:S(2)}, u32[]{:S(2)}) collective-permute-start(bf16[64,1024]{1,0:T(8,128)(2,1)S(1)} %sum.9.refs_0_), channel_id=1, source_target_pairs={{0,2},{1,3},{2,0},{3,1},{4,6},{5,7},{6,4},{7,5},{8,10},{9,11},{10,... | collective-permute-start | bytes 393224 | tf_op jit(solution)/shard_map/ppermute | solution.py:215
  132.9 6.4 %collective-permute-start.33 = (bf16[64,1024]{1,0:T(8,128)(2,1)S(1)}, bf16[64,1024]{1,0:T(8,128)(2,1)S(1)}, u32[]{:S(2)}, u32[]{:S(2)}) collective-permute-start(bf16[64,1024]{1,0:T(8,128)(2,1)S(1)} %sum.9.refs_0_), channel_id=1, source_target_pairs={{0,3},{1,0},{2,1},{3,2},{4,7},{5,4},{6,5},{7,6},{8,11},{9,8},{10,9... | collective-permute-start | bytes 393224 | tf_op jit(solution)/shard_map/ppermute | solution.py:215
where the time goes:
time: 152 us
  Pallas kernels  60.9 us (40%)
  starting transfers between devices  50.6 us (33%)
  waiting for transfers between devices  37.1 us (24%)
  local copies, waits for them, and re-layouts  2.55 us (2%)
    ppermute x34, starting transfers between devices, hop(): return lax.ppermute(value, AXES, flat)  50.6 us
    pallas_call x17, Pallas kernels, kernel_call(): pl.pallas_call(body, out_shape=out, in_specs=[scalar if n in smem else wh...  47.7 us
    ppermute x34, waiting for transfers between devices, hop(): return lax.ppermute(value, AXES, flat)  37.1 us
    pallas_call x4, Pallas kernels, move_tile(): pl.pallas_call(tile_kernel, out_shape=jax.ShapeDtypeStruct(state.shape, F...  13.1 us
  transfers between devices with their start and end apart: 34, of which 17 were waited for; matrix products, arithmetic and copies ran while one was open for 0% of the time, Pallas kernels for 29%

commit v1 on v0

--- a/solution.py
+++ b/solution.py
@@ -254,9 +254,10 @@
         shape = jax.ShapeDtypeStruct(parts[0].shape, parts[0].dtype)
         return kernel_call(sum_kernel, shape, parts, "sum", 1_000_000)
 
-    def joined(rows, colour):
+    def joined(rows, colour, beside_it):
         first, second = (along_gx(rows, colour, step) for step in (1, 2))
-        return added([rows, first, second])
+        second, beside_it = lax.optimization_barrier((second, beside_it))
+        return added([rows, first, second]), beside_it
 
     def spread(whole):
         return [whole, *[along_gy(whole, step) for step in range(1, tiles)]]
@@ -270,8 +271,7 @@
             8_000_000_000,
         )
 
-    def move_tile(state, transformed, factor):
-        blocks = 4
+    def move_tile(state, transformed, factor, blocks):
         some = pl.BlockSpec((tile_rows // blocks, members), lambda n: (n, 0))
         return pl.pallas_call(
             tile_kernel,
@@ -304,8 +304,11 @@
         )
 
     together = lax.optimization_barrier
-    total0 = added(scattered(pick((0,), BF16, anomalies)))
+    parts = scattered(pick((0,), BF16, anomalies))
     picked = [None, *[pick((colour,), F32, anomalies) for colour in range(1, NCOL)]]
+    sides = [beside(obs_var, 1), beside(obs_var, -1)]
+    parts[-1], picked[1], sides = together((parts[-1], picked[1], sides))
+    total0 = added(parts)
 
     pairs = [((target,), source) for target in range(1, NCOL) for source in range(target)]
     prepared = kernel_call(
@@ -313,30 +316,32 @@
         [jax.ShapeDtypeStruct((len(t) * share, 1), F32) for t, _ in pairs]
         + [jax.ShapeDtypeStruct((1, 1), F32)] * NCOL
         + [jax.ShapeDtypeStruct((1, size), F32)] * NCOL,
-        [obs_rows, levels, place, obs_var, beside(obs_var, 1), beside(obs_var, -1)],
+        [obs_rows, levels, place, obs_var, *sides],
         "setup",
         1_000_000,
         smem=(1, 2),
     )
-    row_factor = {(t[0], source): out for (t, source), out in zip(pairs, prepared)}
-    tile_factor = prepared[len(pairs) : len(pairs) + NCOL]
-    variance = prepared[len(pairs) + NCOL :]
-
     state = anomalies
     rows = total0
     done = []
     for colour in range(NCOL):
-        whole = joined(rows, colour)
+        ahead = prepared if colour == 0 else [state, *picked[colour + 1 : colour + 2]]
+        whole, ahead = joined(rows, colour, ahead)
+        if colour == 0:
+            row_factor = {(t[0], source): out for (t, source), out in zip(pairs, ahead)}
+            tile_factor = ahead[len(pairs) : len(pairs) + NCOL]
+            variance = ahead[len(pairs) + NCOL :]
+        else:
+            state, picked[colour + 1 : colour + 2] = ahead[0], ahead[1:]
         pieces = spread(whole)
         if colour < NCOL - 1:
             coming, _ = together((picked[colour + 1], whole))
             parts = scattered(coming)
-        var, state = together((variance[colour], state))
-        done.append(transform(pieces, var))
+        done.append(transform(pieces, variance[colour]))
         if colour < NCOL - 1:
             sources = [(done[n], row_factor[colour + 1, n]) for n in range(colour + 1)]
             rows = move(parts, sources, BF16)
-        state = move_tile(state, done[colour], tile_factor[colour])
+        state = move_tile(state, done[colour], tile_factor[colour], 4)
     return state
 
 

time: 152 us -> 144 us (0.947)
  waiting for transfers between devices: 37.1 us -> 32.2 us
  starting transfers between devices: 50.6 us -> 47.6 us
    ppermute x34, waiting for transfers between devices: 37.1 us -> 32.2 us  [hop(): return lax.ppermute(value, AXES, flat)]
    ppermute x34, starting transfers between devices: 50.6 us -> 47.6 us  [hop(): return lax.ppermute(value, AXES, flat)]
  transfers between devices with their start and end apart: 34 -> 34, of which waited for: 17 -> 13; matrix products, arithmetic and copies ran while one was open for 0% -> 0% of each run, Pallas kernels for 29% -> 30%
where the time goes in v1:
time: 144 us; the launch traced here: 143 us
  Pallas kernels  59.9 us (42%)
  starting transfers between devices  47.6 us (33%)
  waiting for transfers between devices  32.2 us (22%)
  local copies, waits for them, and re-layouts  2.56 us (2%)
    ppermute x34, starting transfers between devices, hop(): return lax.ppermute(value, AXES, flat)  47.6 us
    pallas_call x17, Pallas kernels, kernel_call(): pl.pallas_call(body, out_shape=out, in_specs=[scalar if n in smem else wh...  46.8 us
    ppermute x34, waiting for transfers between devices, hop(): return lax.ppermute(value, AXES, flat)  32.2 us
    pallas_call x4, Pallas kernels, move_tile(): pl.pallas_call(tile_kernel, out_shape=jax.ShapeDtypeStruct(state.shape, F...  13.2 us
  transfers between devices with their start and end apart: 34, of which 13 were waited for; matrix products, arithmetic and copies ran while one was open for 0% of the time, Pallas kernels for 30%

profile of v1, /device:TPU:6, one launch (start us, length us, event | category | flops | bytes accessed | tf_op | source)
XLA Modules:
  0.0 142.7 jit_solution(7552167833325978673)
XLA Ops:
  0.0 0.1 add_bitcast_fusion.place
  0.1 1.6 %copy-done = f32[512,1024]{1,0:T(8,128)S(1)} copy-done((f32[512,1024]{1,0:T(8,128)S(1)}, f32[512,1024]{1,0:T(8,128)}, u32[]{:S(2)}) %copy-start) | copy-done | bytes 2097176
  1.7 0.8 copy-done.2
  2.5 1.7 %pick.4 = (bf16[64,1024]{1,0:T(8,128)(2,1)S(1)}, bf16[64,1024]{1,0:T(8,128)(2,1)S(1)}, bf16[64,1024]{1,0:T(8,128)(2,1)S(1)}, bf16[64,1024]{1,0:T(8,128)(2,1)S(1)}) custom-call(f32[512,1024]{1,0:T(8,128)S(1)} %copy-done, s32[64,256]{1,0:T(8,128)S(1)} %copy-done.2, s32[1,3]{1,0:T(1,128)S(1)} %add_bitcast_fusion.place), custom_call_target="tpu_custom_call" | custom-call | flops 268435456 | bytes 2686988 | tf_op jit(solution)/shard_map/pick/pallas_call | solution.py:23
  4.2 0.0 copy-start.3
  4.2 0.9 collective-permute-start
  5.1 2.4 %collective-permute-start.3 = (bf16[64,1024]{1,0:T(8,128)(2,1)S(1)}, bf16[64,1024]{1,0:T(8,128)(2,1)S(1)}, u32[]{:S(2)}, u32[]{:S(2)}) collective-permute-start(bf16[64,1024]{1,0:T(8,128)(2,1)S(1)} %get-tuple-element.93), channel_id=1, source_target_pairs={{0,1},{1,2},{2,3},{3,0},{4,5},{5,6},{6,7},{7,4},{8,9},{9,10},{10,1... | collective-permute-start | bytes 393224 | tf_op jit(solution)/shard_map/ppermute | solution.py:215
  7.5 0.4 collective-permute-start.4
  8.0 6.8 %collective-permute-start.2 = (f32[1,256]{1,0:T(1,128)S(1)}, f32[1,256]{1,0:T(1,128)S(1)}, u32[]{:S(2)}, u32[]{:S(2)}) collective-permute-start(f32[1,256]{1,0:T(1,128)S(1)} %copy-done.4), channel_id=1, source_target_pairs={{0,252},{1,253},{2,254},{3,255},{4,0},{5,1},{6,2},{7,3},{8,4},{9,5... | collective-permute-start | bytes 3080 | tf_op jit(solution)/shard_map/ppermute | solution.py:215
  14.8 2.4 %pick.5 = (f32[64,1024]{1,0:T(8,128)S(1)}, f32[64,1024]{1,0:T(8,128)S(1)}, f32[64,1024]{1,0:T(8,128)S(1)}, f32[64,1024]{1,0:T(8,128)S(1)}) custom-call(f32[512,1024]{1,0:T(8,128)S(1)} %copy-done, s32[64,256]{1,0:T(8,128)S(1)} %copy-done.2, s32[1,3]{1,0:T(1,128)S(1)} %add_bitcast_fusion.place), custom_call_target="tpu_custom_call" | custom-call | flops 805306368 | bytes 3211276 | tf_op jit(solution)/shard_map/pick/pallas_call | solution.py:23
  17.3 4.0 %collective-permute-start.6 = (bf16[64,1024]{1,0:T(8,128)(2,1)S(1)}, bf16[64,1024]{1,0:T(8,128)(2,1)S(1)}, u32[]{:S(2)}, u32[]{:S(2)}) collective-permute-start(bf16[64,1024]{1,0:T(8,128)(2,1)S(1)} %sum.5.refs_0_), channel_id=1, source_target_pairs={{252,4},{253,5},{254,6},{255,7},{0,252},{1,253},{2,254},{3,255},{4... | collective-permute-start | bytes 393224 | tf_op jit(solution)/shard_map/ppermute | solution.py:215
  21.3 0.1 copy.6.levels
  21.4 1.9 %setup.1 = (f32[64,1]{1,0:T(8,128)S(1)}, f32[64,1]{1,0:T(8,128)S(1)}, f32[64,1]{1,0:T(8,128)S(1)}, f32[64,1]{1,0:T(8,128)S(1)}, f32[64,1]{1,0:T(8,128)S(1)}, /*i...) custom-call(s32[64,256]{1,0:T(8,128)S(1)} %copy-done.3, ...), custom_call_target="tpu_custom_call" | custom-call | flops 1000000 | bytes 77340 | tf_op jit(solution)/shard_map/setup/pallas_call | solution.py:23
  23.2 1.4 collective-permute-done.6.refs_2_
  24.7 4.3 %collective-permute-done.5.refs_1_ = bf16[64,1024]{1,0:T(8,128)(2,1)S(1)} collective-permute-done((bf16[64,1024]{1,0:T(8,128)(2,1)S(1)}, bf16[64,1024]{1,0:T(8,128)(2,1)S(1)}, u32[]{:S(2)}, u32[]{:S(2)}) %collective-permute-start.5) | collective-permute-done | bytes 131104 | tf_op jit(solution)/shard_map/ppermute | solution.py:215
  29.0 2.0 %collective-permute-start.10 = (bf16[64,1024]{1,0:T(8,128)(2,1)S(1)}, bf16[64,1024]{1,0:T(8,128)(2,1)S(1)}, u32[]{:S(2)}, u32[]{:S(2)}) collective-permute-start(bf16[64,1024]{1,0:T(8,128)(2,1)S(1)} %sum.6.refs_0_), channel_id=1, source_target_pairs={{0,1},{1,2},{2,3},{3,0},{4,5},{5,6},{6,7},{7,4},{8,9},{9,10},{10,1... | collective-permute-start | bytes 393224 | tf_op jit(solution)/shard_map/ppermute | solution.py:215
  31.0 1.3 collective-permute-start.11
  32.4 1.3 collective-permute-start.12
  33.7 1.9 %collective-permute-start.7 = (f32[64,1024]{1,0:T(8,128)S(1)}, f32[64,1024]{1,0:T(8,128)S(1)}, u32[]{:S(2)}, u32[]{:S(2)}) collective-permute-start(f32[64,1024]{1,0:T(8,128)S(1)} %get-tuple-element.114), channel_id=1, source_target_pairs={{0,1},{1,2},{2,3},{3,0},{4,5},{5,6},{6,7},{7,4},{8,9},{9,10},{10,1... | collective-permute-start | bytes 786440 | tf_op jit(solution)/shard_map/ppermute | solution.py:215
  35.6 1.0 collective-permute-start.8
  36.6 2.0 %collective-permute-done.10.refs_1_ = bf16[64,1024]{1,0:T(8,128)(2,1)S(1)} collective-permute-done((bf16[64,1024]{1,0:T(8,128)(2,1)S(1)}, bf16[64,1024]{1,0:T(8,128)(2,1)S(1)}, u32[]{:S(2)}, u32[]{:S(2)}) %collective-permute-start.10) | collective-permute-done | bytes 131104 | tf_op jit(solution)/shard_map/ppermute | solution.py:215
  38.6 0.4 collective-permute-done.11.refs_2_
  39.0 2.4 %collective-permute-done.12.refs_3_ = bf16[64,1024]{1,0:T(8,128)(2,1)S(1)} collective-permute-done((bf16[64,1024]{1,0:T(8,128)(2,1)S(1)}, bf16[64,1024]{1,0:T(8,128)(2,1)S(1)}, u32[]{:S(2)}, u32[]{:S(2)}) %collective-permute-start.12) | collective-permute-done | bytes 131104 | tf_op jit(solution)/shard_map/ppermute | solution.py:215
  41.4 8.2 %root.4.refs_4_.transformed = bf16[256,1024]{1,0:T(8,128)(2,1)S(1)} custom-call(bf16[64,1024]{1,0:T(8,128)(2,1)S(1)} %sum.6.refs_0_, bf16[64,1024]{1,0:T(8,128)(2,1)S(1)} %collective-permute-done.10.refs_1_, bf16[64,1024]{1,0:T(8,128)(2,1)S(1)} %collective-permute-done.11.refs_2_, bf16[64,1024]{1,0:T(8,128)(2,1)S(1)} %collective-permute-done.12.refs_3_, ...), custom_call_target="tpu_custom_call" | custom-call | flops 8000000000 | bytes 1049600 | tf_op jit(solution)/shard_map/root/pallas_call | solution.py:23
  49.6 0.6 rows.3.refs_0_
  50.2 0.1 collective-permute-start.13
  50.3 0.5 collective-permute-start.14
  50.8 2.4 %pick.6 = (f32[64,1024]{1,0:T(8,128)S(1)}, f32[64,1024]{1,0:T(8,128)S(1)}, f32[64,1024]{1,0:T(8,128)S(1)}, f32[64,1024]{1,0:T(8,128)S(1)}) custom-call(f32[512,1024]{1,0:T(8,128)S(1)} %copy-done.1, s32[64,256]{1,0:T(8,128)S(1)} %copy-done.3, s32[1,3]{1,0:T(1,128)S(1)} %add_bitcast_fusion.place), custom_call_target="tpu_custom_call" | custom-call | flops 805306368 | bytes 3211276 | tf_op jit(solution)/shard_map/pick/pallas_call | solution.py:23
  53.1 3.1 %tile.4.state = f32[512,1024]{1,0:T(8,128)S(1)} custom-call(f32[512,1024]{1,0:T(8,128)S(1)} %copy-done.1, bf16[256,1024]{1,0:T(8,128)(2,1)S(1)} %root.4.refs_4_.transformed, f32[1,1]{1,0:T(1,128)} %get-tuple-element.119.factor), custom_call_target="tpu_custom_call" | custom-call | flops 536870912 | bytes 4194304 | tf_op jit(solution)/shard_map/tile/pallas_call | solution.py:276
  56.3 1.1 collective-permute-start.18
  57.4 1.6 %collective-permute-start.19 = (bf16[64,1024]{1,0:T(8,128)(2,1)S(1)}, bf16[64,1024]{1,0:T(8,128)(2,1)S(1)}, u32[]{:S(2)}, u32[]{:S(2)}) collective-permute-start(bf16[64,1024]{1,0:T(8,128)(2,1)S(1)} %sum.7.refs_0_), channel_id=1, source_target_pairs={{0,2},{1,3},{2,0},{3,1},{4,6},{5,7},{6,4},{7,5},{8,10},{9,11},{10,... | collective-permute-start | bytes 393224 | tf_op jit(solution)/shard_map/ppermute | solution.py:215
  59.0 1.3 collective-permute-start.20
  60.3 1.9 %collective-permute-start.15 = (f32[64,1024]{1,0:T(8,128)S(1)}, f32[64,1024]{1,0:T(8,128)S(1)}, u32[]{:S(2)}, u32[]{:S(2)}) collective-permute-start(f32[64,1024]{1,0:T(8,128)S(1)} %get-tuple-element.130), channel_id=1, source_target_pairs={{0,1},{1,2},{2,3},{3,0},{4,5},{5,6},{6,7},{7,4},{8,9},{9,10},{10,1... | collective-permute-start | bytes 786440 | tf_op jit(solution)/shard_map/ppermute | solution.py:215
  62.2 0.8 collective-permute-start.16
  63.0 1.0 collective-permute-start.17
  63.9 1.4 collective-permute-done.19.refs_2_
  65.3 6.9 %collective-permute-done.20.refs_3_ = bf16[64,1024]{1,0:T(8,128)(2,1)S(1)} collective-permute-done((bf16[64,1024]{1,0:T(8,128)(2,1)S(1)}, bf16[64,1024]{1,0:T(8,128)(2,1)S(1)}, u32[]{:S(2)}, u32[]{:S(2)}) %collective-permute-start.20) | collective-permute-done | bytes 131104 | tf_op jit(solution)/shard_map/ppermute | solution.py:215
  72.2 8.2 %root.5.refs_6_.transformed = bf16[256,1024]{1,0:T(8,128)(2,1)S(1)} custom-call(bf16[64,1024]{1,0:T(8,128)(2,1)S(1)} %sum.7.refs_0_, bf16[64,1024]{1,0:T(8,128)(2,1)S(1)} %collective-permute-done.18.refs_1_, bf16[64,1024]{1,0:T(8,128)(2,1)S(1)} %collective-permute-done.19.refs_2_, bf16[64,1024]{1,0:T(8,128)(2,1)S(1)} %collective-permute-done.20.refs_3_, ...), custom_call_target="tpu_custom_call" | custom-call | flops 8000000000 | bytes 1049600 | tf_op jit(solution)/shard_map/root/pallas_call | solution.py:23
  80.4 1.2 rows.4.refs_0_
  81.6 0.1 collective-permute-start.21
  81.7 2.0 %collective-permute-start.22 = (bf16[64,1024]{1,0:T(8,128)(2,1)S(1)}, bf16[64,1024]{1,0:T(8,128)(2,1)S(1)}, u32[]{:S(2)}, u32[]{:S(2)}) collective-permute-start(bf16[64,1024]{1,0:T(8,128)(2,1)S(1)} %rows.4.refs_0_), channel_id=1, source_target_pairs={{4,8},{5,9},{6,10},{7,11},{8,12},{9,13},{10,14},{11,15},{12,4},{13... | collective-permute-start | bytes 393224 | tf_op jit(solution)/shard_map/ppermute | solution.py:215
  83.7 2.4 %pick.7 = (f32[64,1024]{1,0:T(8,128)S(1)}, f32[64,1024]{1,0:T(8,128)S(1)}, f32[64,1024]{1,0:T(8,128)S(1)}, f32[64,1024]{1,0:T(8,128)S(1)}) custom-call(f32[512,1024]{1,0:T(8,128)S(1)} %copy-done.1, s32[64,256]{1,0:T(8,128)S(1)} %copy-done.3, s32[1,3]{1,0:T(1,128)S(1)} %add_bitcast_fusion.place), custom_call_target="tpu_custom_call" | custom-call | flops 805306368 | bytes 3211276 | tf_op jit(solution)/shard_map/pick/pallas_call | solution.py:23
  86.1 3.0 %tile.5.state = f32[512,1024]{1,0:T(8,128)S(1)} custom-call(f32[512,1024]{1,0:T(8,128)S(1)} %tile.4.state, bf16[256,1024]{1,0:T(8,128)(2,1)S(1)} %root.5.refs_6_.transformed, f32[1,1]{1,0:T(1,128)} %get-tuple-element.137.factor), custom_call_target="tpu_custom_call" | custom-call | flops 536870912 | bytes 4194304 | tf_op jit(solution)/shard_map/tile/pallas_call | solution.py:276
  89.2 0.1 collective-permute-start.26
  89.3 2.4 %collective-permute-start.27 = (bf16[64,1024]{1,0:T(8,128)(2,1)S(1)}, bf16[64,1024]{1,0:T(8,128)(2,1)S(1)}, u32[]{:S(2)}, u32[]{:S(2)}) collective-permute-start(bf16[64,1024]{1,0:T(8,128)(2,1)S(1)} %sum.8.refs_0_), channel_id=1, source_target_pairs={{0,2},{1,3},{2,0},{3,1},{4,6},{5,7},{6,4},{7,5},{8,10},{9,11},{10,... | collective-permute-start | bytes 393224 | tf_op jit(solution)/shard_map/ppermute | solution.py:215
  91.6 3.2 %collective-permute-start.23 = (f32[64,1024]{1,0:T(8,128)S(1)}, f32[64,1024]{1,0:T(8,128)S(1)}, u32[]{:S(2)}, u32[]{:S(2)}) collective-permute-start(f32[64,1024]{1,0:T(8,128)S(1)} %get-tuple-element.148), channel_id=1, source_target_pairs={{0,1},{1,2},{2,3},{3,0},{4,5},{5,6},{6,7},{7,4},{8,9},{9,10},{10,1... | collective-permute-start | bytes 786440 | tf_op jit(solution)/shard_map/ppermute | solution.py:215
  94.9 0.5 collective-permute-start.24
  95.4 0.3 collective-permute-done.26.refs_1_
  95.7 1.4 collective-permute-start.25
  97.0 6.0 %collective-permute-done.28.refs_3_ = bf16[64,1024]{1,0:T(8,128)(2,1)S(1)} collective-permute-done((bf16[64,1024]{1,0:T(8,128)(2,1)S(1)}, bf16[64,1024]{1,0:T(8,128)(2,1)S(1)}, u32[]{:S(2)}, u32[]{:S(2)}) %collective-permute-start.28) | collective-permute-done | bytes 131104 | tf_op jit(solution)/shard_map/ppermute | solution.py:215
  103.0 8.2 %root.6.refs_8_.transformed = bf16[256,1024]{1,0:T(8,128)(2,1)S(1)} custom-call(bf16[64,1024]{1,0:T(8,128)(2,1)S(1)} %sum.8.refs_0_, bf16[64,1024]{1,0:T(8,128)(2,1)S(1)} %collective-permute-done.26.refs_1_, bf16[64,1024]{1,0:T(8,128)(2,1)S(1)} %collective-permute-done.27.refs_2_, bf16[64,1024]{1,0:T(8,128)(2,1)S(1)} %collective-permute-done.28.refs_3_, ...), custom_call_target="tpu_custom_call" | custom-call | flops 8000000000 | bytes 1049600 | tf_op jit(solution)/shard_map/root/pallas_call | solution.py:23
  111.2 1.6 %rows.5.refs_0_ = bf16[64,1024]{1,0:T(8,128)(2,1)S(1)} custom-call(f32[64,1024]{1,0:T(8,128)S(1)} %get-tuple-element.147.refs_0_, f32[64,1024]{1,0:T(8,128)S(1)} %collective-permute-done.23.refs_1_, f32[64,1024]{1,0:T(8,128)S(1)} %collective-permute-done.24.refs_2_, f32[64,1024]{1,0:T(8,128)S(1)} %collective-permute-done.25.refs_3_, ...), custom_call_target="tpu_custom_call" | custom-call | flops 201326592 | bytes 2753280 | tf_op jit(solution)/shard_map/rows/pallas_call | solution.py:23
  112.9 0.5 collective-permute-start.29
  113.4 4.9 %collective-permute-start.30 = (bf16[64,1024]{1,0:T(8,128)(2,1)S(1)}, bf16[64,1024]{1,0:T(8,128)(2,1)S(1)}, u32[]{:S(2)}, u32[]{:S(2)}) collective-permute-start(bf16[64,1024]{1,0:T(8,128)(2,1)S(1)} %rows.5.refs_0_), channel_id=1, source_target_pairs={{8,12},{9,13},{10,14},{11,15},{12,16},{13,17},{14,18},{15,19},{16,... | collective-permute-start | bytes 393224 | tf_op jit(solution)/shard_map/ppermute | solution.py:215
  118.3 3.1 %tile.6.state = f32[512,1024]{1,0:T(8,128)S(1)} custom-call(f32[512,1024]{1,0:T(8,128)S(1)} %tile.5.state, bf16[256,1024]{1,0:T(8,128)(2,1)S(1)} %root.6.refs_8_.transformed, f32[1,1]{1,0:T(1,128)} %get-tuple-element.156.factor), custom_call_target="tpu_custom_call" | custom-call | flops 536870912 | bytes 4194304 | tf_op jit(solution)/shard_map/tile/pallas_call | solution.py:276
  121.4 1.1 collective-permute-done.29.refs_2_
  122.5 0.1 collective-permute-start.31
  122.6 1.2 collective-permute-start.32
  123.8 0.9 collective-permute-start.33
  124.7 2.9 %collective-permute-done.31.refs_1_ = bf16[64,1024]{1,0:T(8,128)(2,1)S(1)} collective-permute-done((bf16[64,1024]{1,0:T(8,128)(2,1)S(1)}, bf16[64,1024]{1,0:T(8,128)(2,1)S(1)}, u32[]{:S(2)}, u32[]{:S(2)}) %collective-permute-start.31) | collective-permute-done | bytes 131104 | tf_op jit(solution)/shard_map/ppermute | solution.py:215
  127.6 1.6 %collective-permute-done.32.refs_2_ = bf16[64,1024]{1,0:T(8,128)(2,1)S(1)} collective-permute-done((bf16[64,1024]{1,0:T(8,128)(2,1)S(1)}, bf16[64,1024]{1,0:T(8,128)(2,1)S(1)}, u32[]{:S(2)}, u32[]{:S(2)}) %collective-permute-start.32) | collective-permute-done | bytes 131104 | tf_op jit(solution)/shard_map/ppermute | solution.py:215
  129.2 1.4 collective-permute-done.33.refs_3_
  130.6 8.2 %root.7.transformed = bf16[256,1024]{1,0:T(8,128)(2,1)S(1)} custom-call(bf16[64,1024]{1,0:T(8,128)(2,1)S(1)} %sum.9.refs_0_, bf16[64,1024]{1,0:T(8,128)(2,1)S(1)} %collective-permute-done.31.refs_1_, bf16[64,1024]{1,0:T(8,128)(2,1)S(1)} %collective-permute-done.32.refs_2_, bf16[64,1024]{1,0:T(8,128)(2,1)S(1)} %collective-permute-done.33.refs_3_, ...), custom_call_target="tpu_custom_call" | custom-call | flops 8000000000 | bytes 1049600 | tf_op jit(solution)/shard_map/root/pallas_call | solution.py:23
  138.8 4.0 %tile.7 = f32[512,1024]{1,0:T(8,128)} custom-call(f32[512,1024]{1,0:T(8,128)S(1)} %tile.6.state, bf16[256,1024]{1,0:T(8,128)(2,1)S(1)} %root.7.transformed, f32[1,1]{1,0:T(1,128)} %get-tuple-element.160.factor), custom_call_target="tpu_custom_call" | custom-call | flops 536870912 | bytes 4194304 | tf_op jit(solution)/shard_map/tile/pallas_call | solution.py:276
  (40 shorter events, 0.2 us)
Async XLA Ops:
  0.0 8.0 %copy-start.4 = (f32[1,256]{1,0:T(1,128)S(1)}, f32[1,256]{1,0:T(1,128)}, u32[]{:S(2)}) copy-start(f32[1,256]{1,0:T(1,128)} %own.1) | copy-start | bytes 3076
  0.1 1.6 %copy-start = (f32[512,1024]{1,0:T(8,128)S(1)}, f32[512,1024]{1,0:T(8,128)}, u32[]{:S(2)}) copy-start(f32[512,1024]{1,0:T(8,128)} %state.9) | copy-start | bytes 6291460
  1.7 0.8 copy-start.2
  4.2 17.1 %copy-start.5 = (s32[64,3,4]{0,2,1:T(4,128)S(1)}, s32[64,3,4]{0,2,1:T(4,128)}, u32[]{:S(2)}) copy-start(s32[64,3,4]{0,2,1:T(4,128)} %param.7) | copy-start | bytes 9220
  4.2 17.2 %copy-start.3 = (s32[64,256]{1,0:T(8,128)S(1)}, s32[64,256]{1,0:T(8,128)}, u32[]{:S(2)}) copy-start(s32[64,256]{1,0:T(8,128)} %obs.9) | copy-start | bytes 196612
  4.2 13.0 %collective-permute-start = (bf16[64,1024]{1,0:T(8,128)(2,1)S(1)}, bf16[64,1024]{1,0:T(8,128)(2,1)S(1)}, u32[]{:S(2)}, u32[]{:S(2)}) collective-permute-start(bf16[64,1024]{1,0:T(8,128)(2,1)S(1)} %get-tuple-element.83), channel_id=1, source_target_pairs={{0,3},{1,0},{2,1},{3,2},{4,7},{5,4},{6,5},{7,6},{8,11},{9,8},{10,9... | collective-permute-start | bytes 393224 | tf_op jit(solution)/shard_map/ppermute | solution.py:215
  5.1 12.1 %collective-permute-start.3 = (bf16[64,1024]{1,0:T(8,128)(2,1)S(1)}, bf16[64,1024]{1,0:T(8,128)(2,1)S(1)}, u32[]{:S(2)}, u32[]{:S(2)}) collective-permute-start(bf16[64,1024]{1,0:T(8,128)(2,1)S(1)} %get-tuple-element.93), channel_id=1, source_target_pairs={{0,1},{1,2},{2,3},{3,0},{4,5},{5,6},{6,7},{7,4},{8,9},{9,10},{10,1... | collective-permute-start | bytes 393224 | tf_op jit(solution)/shard_map/ppermute | solution.py:215
  7.5 9.7 %collective-permute-start.4 = (bf16[64,1024]{1,0:T(8,128)(2,1)S(1)}, bf16[64,1024]{1,0:T(8,128)(2,1)S(1)}, u32[]{:S(2)}, u32[]{:S(2)}) collective-permute-start(bf16[64,1024]{1,0:T(8,128)(2,1)S(1)} %get-tuple-element.94), channel_id=1, source_target_pairs={{0,2},{1,3},{2,0},{3,1},{4,6},{5,7},{6,4},{7,5},{8,10},{9,11},{10,... | collective-permute-start | bytes 393224 | tf_op jit(solution)/shard_map/ppermute | solution.py:215
  8.0 9.2 %collective-permute-start.1 = (f32[1,256]{1,0:T(1,128)S(1)}, f32[1,256]{1,0:T(1,128)S(1)}, u32[]{:S(2)}, u32[]{:S(2)}) collective-permute-start(f32[1,256]{1,0:T(1,128)S(1)} %copy-done.4), channel_id=1, source_target_pairs={{0,4},{1,5},{2,6},{3,7},{4,8},{5,9},{6,10},{7,11},{8,12},{9,13},{1... | collective-permute-start | bytes 3080 | tf_op jit(solution)/shard_map/ppermute | solution.py:215
  8.0 9.2 %collective-permute-start.2 = (f32[1,256]{1,0:T(1,128)S(1)}, f32[1,256]{1,0:T(1,128)S(1)}, u32[]{:S(2)}, u32[]{:S(2)}) collective-permute-start(f32[1,256]{1,0:T(1,128)S(1)} %copy-done.4), channel_id=1, source_target_pairs={{0,252},{1,253},{2,254},{3,255},{4,0},{5,1},{6,2},{7,3},{8,4},{9,5... | collective-permute-start | bytes 3080 | tf_op jit(solution)/shard_map/ppermute | solution.py:215
  17.3 7.4 %collective-permute-start.6 = (bf16[64,1024]{1,0:T(8,128)(2,1)S(1)}, bf16[64,1024]{1,0:T(8,128)(2,1)S(1)}, u32[]{:S(2)}, u32[]{:S(2)}) collective-permute-start(bf16[64,1024]{1,0:T(8,128)(2,1)S(1)} %sum.5.refs_0_), channel_id=1, source_target_pairs={{252,4},{253,5},{254,6},{255,7},{0,252},{1,253},{2,254},{3,255},{4... | collective-permute-start | bytes 393224 | tf_op jit(solution)/shard_map/ppermute | solution.py:215
  21.3 7.7 %collective-permute-start.5 = (bf16[64,1024]{1,0:T(8,128)(2,1)S(1)}, bf16[64,1024]{1,0:T(8,128)(2,1)S(1)}, u32[]{:S(2)}, u32[]{:S(2)}) collective-permute-start(bf16[64,1024]{1,0:T(8,128)(2,1)S(1)} %sum.5.refs_0_), channel_id=1, source_target_pairs={{252,0},{253,1},{254,2},{255,3},{0,4},{1,5},{2,6},{3,7},{4,252},{5... | collective-permute-start | bytes 393224 | tf_op jit(solution)/shard_map/ppermute | solution.py:215
  29.0 21.8 %copy-start.1 = (f32[512,1024]{1,0:T(8,128)S(1)}, f32[512,1024]{1,0:T(8,128)}, u32[]{:S(2)}) copy-start(f32[512,1024]{1,0:T(8,128)} %state.9) | copy-start | bytes 6291460
  29.0 9.6 %collective-permute-start.10 = (bf16[64,1024]{1,0:T(8,128)(2,1)S(1)}, bf16[64,1024]{1,0:T(8,128)(2,1)S(1)}, u32[]{:S(2)}, u32[]{:S(2)}) collective-permute-start(bf16[64,1024]{1,0:T(8,128)(2,1)S(1)} %sum.6.refs_0_), channel_id=1, source_target_pairs={{0,1},{1,2},{2,3},{3,0},{4,5},{5,6},{6,7},{7,4},{8,9},{9,10},{10,1... | collective-permute-start | bytes 393224 | tf_op jit(solution)/shard_map/ppermute | solution.py:215
  31.0 8.0 %collective-permute-start.11 = (bf16[64,1024]{1,0:T(8,128)(2,1)S(1)}, bf16[64,1024]{1,0:T(8,128)(2,1)S(1)}, u32[]{:S(2)}, u32[]{:S(2)}) collective-permute-start(bf16[64,1024]{1,0:T(8,128)(2,1)S(1)} %sum.6.refs_0_), channel_id=1, source_target_pairs={{0,2},{1,3},{2,0},{3,1},{4,6},{5,7},{6,4},{7,5},{8,10},{9,11},{10,... | collective-permute-start | bytes 393224 | tf_op jit(solution)/shard_map/ppermute | solution.py:215
  32.4 9.0 %collective-permute-start.12 = (bf16[64,1024]{1,0:T(8,128)(2,1)S(1)}, bf16[64,1024]{1,0:T(8,128)(2,1)S(1)}, u32[]{:S(2)}, u32[]{:S(2)}) collective-permute-start(bf16[64,1024]{1,0:T(8,128)(2,1)S(1)} %sum.6.refs_0_), channel_id=1, source_target_pairs={{0,3},{1,0},{2,1},{3,2},{4,7},{5,4},{6,5},{7,6},{8,11},{9,8},{10,9... | collective-permute-start | bytes 393224 | tf_op jit(solution)/shard_map/ppermute | solution.py:215
  33.7 15.9 %collective-permute-start.7 = (f32[64,1024]{1,0:T(8,128)S(1)}, f32[64,1024]{1,0:T(8,128)S(1)}, u32[]{:S(2)}, u32[]{:S(2)}) collective-permute-start(f32[64,1024]{1,0:T(8,128)S(1)} %get-tuple-element.114), channel_id=1, source_target_pairs={{0,1},{1,2},{2,3},{3,0},{4,5},{5,6},{6,7},{7,4},{8,9},{9,10},{10,1... | collective-permute-start | bytes 786440 | tf_op jit(solution)/shard_map/ppermute | solution.py:215
  35.6 14.0 %collective-permute-start.8 = (f32[64,1024]{1,0:T(8,128)S(1)}, f32[64,1024]{1,0:T(8,128)S(1)}, u32[]{:S(2)}, u32[]{:S(2)}) collective-permute-start(f32[64,1024]{1,0:T(8,128)S(1)} %get-tuple-element.115), channel_id=1, source_target_pairs={{0,2},{1,3},{2,0},{3,1},{4,6},{5,7},{6,4},{7,5},{8,10},{9,11},{10,... | collective-permute-start | bytes 786440 | tf_op jit(solution)/shard_map/ppermute | solution.py:215
  38.6 11.0 %collective-permute-start.9 = (f32[64,1024]{1,0:T(8,128)S(1)}, f32[64,1024]{1,0:T(8,128)S(1)}, u32[]{:S(2)}, u32[]{:S(2)}) collective-permute-start(f32[64,1024]{1,0:T(8,128)S(1)} %get-tuple-element.116), channel_id=1, source_target_pairs={{0,3},{1,0},{2,1},{3,2},{4,7},{5,4},{6,5},{7,6},{8,11},{9,8},{10,9... | collective-permute-start | bytes 786440 | tf_op jit(solution)/shard_map/ppermute | solution.py:215
  50.2 6.1 %collective-permute-start.13 = (bf16[64,1024]{1,0:T(8,128)(2,1)S(1)}, bf16[64,1024]{1,0:T(8,128)(2,1)S(1)}, u32[]{:S(2)}, u32[]{:S(2)}) collective-permute-start(bf16[64,1024]{1,0:T(8,128)(2,1)S(1)} %rows.3.refs_0_), channel_id=1, source_target_pairs={{0,8},{1,9},{2,10},{3,11},{4,0},{5,1},{6,2},{7,3},{8,4},{9,5},{10,... | collective-permute-start | bytes 393224 | tf_op jit(solution)/shard_map/ppermute | solution.py:215
  50.3 6.0 %collective-permute-start.14 = (bf16[64,1024]{1,0:T(8,128)(2,1)S(1)}, bf16[64,1024]{1,0:T(8,128)(2,1)S(1)}, u32[]{:S(2)}, u32[]{:S(2)}) collective-permute-start(bf16[64,1024]{1,0:T(8,128)(2,1)S(1)} %rows.3.refs_0_), channel_id=1, source_target_pairs={{0,4},{1,5},{2,6},{3,7},{4,8},{5,9},{6,10},{7,11},{8,0},{9,1},{10,... | collective-permute-start | bytes 393224 | tf_op jit(solution)/shard_map/ppermute | solution.py:215
  56.3 6.7 %collective-permute-start.18 = (bf16[64,1024]{1,0:T(8,128)(2,1)S(1)}, bf16[64,1024]{1,0:T(8,128)(2,1)S(1)}, u32[]{:S(2)}, u32[]{:S(2)}) collective-permute-start(bf16[64,1024]{1,0:T(8,128)(2,1)S(1)} %sum.7.refs_0_), channel_id=1, source_target_pairs={{0,1},{1,2},{2,3},{3,0},{4,5},{5,6},{6,7},{7,4},{8,9},{9,10},{10,1... | collective-permute-start | bytes 393224 | tf_op jit(solution)/shard_map/ppermute | solution.py:215
  57.4 7.9 %collective-permute-start.19 = (bf16[64,1024]{1,0:T(8,128)(2,1)S(1)}, bf16[64,1024]{1,0:T(8,128)(2,1)S(1)}, u32[]{:S(2)}, u32[]{:S(2)}) collective-permute-start(bf16[64,1024]{1,0:T(8,128)(2,1)S(1)} %sum.7.refs_0_), channel_id=1, source_target_pairs={{0,2},{1,3},{2,0},{3,1},{4,6},{5,7},{6,4},{7,5},{8,10},{9,11},{10,... | collective-permute-start | bytes 393224 | tf_op jit(solution)/shard_map/ppermute | solution.py:215
  59.0 13.3 %collective-permute-start.20 = (bf16[64,1024]{1,0:T(8,128)(2,1)S(1)}, bf16[64,1024]{1,0:T(8,128)(2,1)S(1)}, u32[]{:S(2)}, u32[]{:S(2)}) collective-permute-start(bf16[64,1024]{1,0:T(8,128)(2,1)S(1)} %sum.7.refs_0_), channel_id=1, source_target_pairs={{0,3},{1,0},{2,1},{3,2},{4,7},{5,4},{6,5},{7,6},{8,11},{9,8},{10,9... | collective-permute-start | bytes 393224 | tf_op jit(solution)/shard_map/ppermute | solution.py:215
  60.3 20.1 %collective-permute-start.15 = (f32[64,1024]{1,0:T(8,128)S(1)}, f32[64,1024]{1,0:T(8,128)S(1)}, u32[]{:S(2)}, u32[]{:S(2)}) collective-permute-start(f32[64,1024]{1,0:T(8,128)S(1)} %get-tuple-element.130), channel_id=1, source_target_pairs={{0,1},{1,2},{2,3},{3,0},{4,5},{5,6},{6,7},{7,4},{8,9},{9,10},{10,1... | collective-permute-start | bytes 786440 | tf_op jit(solution)/shard_map/ppermute | solution.py:215
  62.2 18.2 %collective-permute-start.16 = (f32[64,1024]{1,0:T(8,128)S(1)}, f32[64,1024]{1,0:T(8,128)S(1)}, u32[]{:S(2)}, u32[]{:S(2)}) collective-permute-start(f32[64,1024]{1,0:T(8,128)S(1)} %get-tuple-element.131), channel_id=1, source_target_pairs={{0,2},{1,3},{2,0},{3,1},{4,6},{5,7},{6,4},{7,5},{8,10},{9,11},{10,... | collective-permute-start | bytes 786440 | tf_op jit(solution)/shard_map/ppermute | solution.py:215
  63.0 17.4 %collective-permute-start.17 = (f32[64,1024]{1,0:T(8,128)S(1)}, f32[64,1024]{1,0:T(8,128)S(1)}, u32[]{:S(2)}, u32[]{:S(2)}) collective-permute-start(f32[64,1024]{1,0:T(8,128)S(1)} %get-tuple-element.132), channel_id=1, source_target_pairs={{0,3},{1,0},{2,1},{3,2},{4,7},{5,4},{6,5},{7,6},{8,11},{9,8},{10,9... | collective-permute-start | bytes 786440 | tf_op jit(solution)/shard_map/ppermute | solution.py:215
  81.6 7.5 %collective-permute-start.21 = (bf16[64,1024]{1,0:T(8,128)(2,1)S(1)}, bf16[64,1024]{1,0:T(8,128)(2,1)S(1)}, u32[]{:S(2)}, u32[]{:S(2)}) collective-permute-start(bf16[64,1024]{1,0:T(8,128)(2,1)S(1)} %rows.4.refs_0_), channel_id=1, source_target_pairs={{4,12},{5,13},{6,14},{7,15},{8,4},{9,5},{10,6},{11,7},{12,8},{13,9... | collective-permute-start | bytes 393224 | tf_op jit(solution)/shard_map/ppermute | solution.py:215
  81.7 7.5 %collective-permute-start.22 = (bf16[64,1024]{1,0:T(8,128)(2,1)S(1)}, bf16[64,1024]{1,0:T(8,128)(2,1)S(1)}, u32[]{:S(2)}, u32[]{:S(2)}) collective-permute-start(bf16[64,1024]{1,0:T(8,128)(2,1)S(1)} %rows.4.refs_0_), channel_id=1, source_target_pairs={{4,8},{5,9},{6,10},{7,11},{8,12},{9,13},{10,14},{11,15},{12,4},{13... | collective-permute-start | bytes 393224 | tf_op jit(solution)/shard_map/ppermute | solution.py:215
  89.2 6.5 %collective-permute-start.26 = (bf16[64,1024]{1,0:T(8,128)(2,1)S(1)}, bf16[64,1024]{1,0:T(8,128)(2,1)S(1)}, u32[]{:S(2)}, u32[]{:S(2)}) collective-permute-start(bf16[64,1024]{1,0:T(8,128)(2,1)S(1)} %sum.8.refs_0_), channel_id=1, source_target_pairs={{0,1},{1,2},{2,3},{3,0},{4,5},{5,6},{6,7},{7,4},{8,9},{9,10},{10,1... | collective-permute-start | bytes 393224 | tf_op jit(solution)/shard_map/ppermute | solution.py:215
  89.3 7.8 %collective-permute-start.27 = (bf16[64,1024]{1,0:T(8,128)(2,1)S(1)}, bf16[64,1024]{1,0:T(8,128)(2,1)S(1)}, u32[]{:S(2)}, u32[]{:S(2)}) collective-permute-start(bf16[64,1024]{1,0:T(8,128)(2,1)S(1)} %sum.8.refs_0_), channel_id=1, source_target_pairs={{0,2},{1,3},{2,0},{3,1},{4,6},{5,7},{6,4},{7,5},{8,10},{9,11},{10,... | collective-permute-start | bytes 393224 | tf_op jit(solution)/shard_map/ppermute | solution.py:215
  91.6 11.4 %collective-permute-start.28 = (bf16[64,1024]{1,0:T(8,128)(2,1)S(1)}, bf16[64,1024]{1,0:T(8,128)(2,1)S(1)}, u32[]{:S(2)}, u32[]{:S(2)}) collective-permute-start(bf16[64,1024]{1,0:T(8,128)(2,1)S(1)} %sum.8.refs_0_), channel_id=1, source_target_pairs={{0,3},{1,0},{2,1},{3,2},{4,7},{5,4},{6,5},{7,6},{8,11},{9,8},{10,9... | collective-permute-start | bytes 393224 | tf_op jit(solution)/shard_map/ppermute | solution.py:215
  91.6 19.6 %collective-permute-start.23 = (f32[64,1024]{1,0:T(8,128)S(1)}, f32[64,1024]{1,0:T(8,128)S(1)}, u32[]{:S(2)}, u32[]{:S(2)}) collective-permute-start(f32[64,1024]{1,0:T(8,128)S(1)} %get-tuple-element.148), channel_id=1, source_target_pairs={{0,1},{1,2},{2,3},{3,0},{4,5},{5,6},{6,7},{7,4},{8,9},{9,10},{10,1... | collective-permute-start | bytes 786440 | tf_op jit(solution)/shard_map/ppermute | solution.py:215
  94.9 16.4 %collective-permute-start.24 = (f32[64,1024]{1,0:T(8,128)S(1)}, f32[64,1024]{1,0:T(8,128)S(1)}, u32[]{:S(2)}, u32[]{:S(2)}) collective-permute-start(f32[64,1024]{1,0:T(8,128)S(1)} %get-tuple-element.149), channel_id=1, source_target_pairs={{0,2},{1,3},{2,0},{3,1},{4,6},{5,7},{6,4},{7,5},{8,10},{9,11},{10,... | collective-permute-start | bytes 786440 | tf_op jit(solution)/shard_map/ppermute | solution.py:215
  95.7 15.6 %collective-permute-start.25 = (f32[64,1024]{1,0:T(8,128)S(1)}, f32[64,1024]{1,0:T(8,128)S(1)}, u32[]{:S(2)}, u32[]{:S(2)}) collective-permute-start(f32[64,1024]{1,0:T(8,128)S(1)} %get-tuple-element.150), channel_id=1, source_target_pairs={{0,3},{1,0},{2,1},{3,2},{4,7},{5,4},{6,5},{7,6},{8,11},{9,8},{10,9... | collective-permute-start | bytes 786440 | tf_op jit(solution)/shard_map/ppermute | solution.py:215
  112.9 9.7 %collective-permute-start.29 = (bf16[64,1024]{1,0:T(8,128)(2,1)S(1)}, bf16[64,1024]{1,0:T(8,128)(2,1)S(1)}, u32[]{:S(2)}, u32[]{:S(2)}) collective-permute-start(bf16[64,1024]{1,0:T(8,128)(2,1)S(1)} %rows.5.refs_0_), channel_id=1, source_target_pairs={{8,16},{9,17},{10,18},{11,19},{12,8},{13,9},{14,10},{15,11},{16,12... | collective-permute-start | bytes 393224 | tf_op jit(solution)/shard_map/ppermute | solution.py:215
  113.4 9.1 %collective-permute-start.30 = (bf16[64,1024]{1,0:T(8,128)(2,1)S(1)}, bf16[64,1024]{1,0:T(8,128)(2,1)S(1)}, u32[]{:S(2)}, u32[]{:S(2)}) collective-permute-start(bf16[64,1024]{1,0:T(8,128)(2,1)S(1)} %rows.5.refs_0_), channel_id=1, source_target_pairs={{8,12},{9,13},{10,14},{11,15},{12,16},{13,17},{14,18},{15,19},{16,... | collective-permute-start | bytes 393224 | tf_op jit(solution)/shard_map/ppermute | solution.py:215
  122.5 5.0 %collective-permute-start.31 = (bf16[64,1024]{1,0:T(8,128)(2,1)S(1)}, bf16[64,1024]{1,0:T(8,128)(2,1)S(1)}, u32[]{:S(2)}, u32[]{:S(2)}) collective-permute-start(bf16[64,1024]{1,0:T(8,128)(2,1)S(1)} %sum.9.refs_0_), channel_id=1, source_target_pairs={{0,1},{1,2},{2,3},{3,0},{4,5},{5,6},{6,7},{7,4},{8,9},{9,10},{10,1... | collective-permute-start | bytes 393224 | tf_op jit(solution)/shard_map/ppermute | solution.py:215
  122.6 6.6 %collective-permute-start.32 = (bf16[64,1024]{1,0:T(8,128)(2,1)S(1)}, bf16[64,1024]{1,0:T(8,128)(2,1)S(1)}, u32[]{:S(2)}, u32[]{:S(2)}) collective-permute-start(bf16[64,1024]{1,0:T(8,128)(2,1)S(1)} %sum.9.refs_0_), channel_id=1, source_target_pairs={{0,2},{1,3},{2,0},{3,1},{4,6},{5,7},{6,4},{7,5},{8,10},{9,11},{10,... | collective-permute-start | bytes 393224 | tf_op jit(solution)/shard_map/ppermute | solution.py:215
  123.8 6.8 %collective-permute-start.33 = (bf16[64,1024]{1,0:T(8,128)(2,1)S(1)}, bf16[64,1024]{1,0:T(8,128)(2,1)S(1)}, u32[]{:S(2)}, u32[]{:S(2)}) collective-permute-start(bf16[64,1024]{1,0:T(8,128)(2,1)S(1)} %sum.9.refs_0_), channel_id=1, source_target_pairs={{0,3},{1,0},{2,1},{3,2},{4,7},{5,4},{6,5},{7,6},{8,11},{9,8},{10,9... | collective-permute-start | bytes 393224 | tf_op jit(solution)/shard_map/ppermute | solution.py:215

commit v2 on v1

--- a/solution.py
+++ b/solution.py
@@ -11,6 +11,8 @@
 NS_STEPS = 12
 AXES = ("gx", "gy")
 VMEM_LIMIT = 20 << 20
+LAST_BLOCKS = 1
+EXTRA = 16
 INTERPRET = False
 F32 = jnp.float32
 BF16 = jnp.bfloat16
@@ -99,7 +101,7 @@
             out[n * share : (n + 1) * share, :] = scratch[pl.ds(start, share), :]
 
 
-def setup_kernel(pairs, tiles, tile_rows, obs, levels, place, own, left, right, *outs):
+def setup_kernel(pairs, tiles, tile_rows, obs, levels, place, own, *outs):
     columns, size = obs.shape
     share = size // tiles
     col, tile = place[0, 0], place[0, 1]
@@ -124,19 +126,27 @@
             out[n * share : (n + 1) * share, :] = column / members
     for colour in range(NCOL):
         outs[len(pairs) + colour][...] = jnp.full((1, 1), factor(colour, tile)) / members
-        slot, active, _ = standing(col, colour, columns)
-        value = jnp.where(
-            active & (slot == 2), left[...], jnp.where(active & (slot == 0), right[...], own[...])
-        )
-        pieces = [value[:, n * share : (n + 1) * share] for n in range(tiles)]
-        ordered = []
-        for step in range(tiles):
-            source = lax.rem(tile + tiles - step, tiles)
-            piece = pieces[0]
-            for n in range(1, tiles):
-                piece = jnp.where(source == n, pieces[n], piece)
-            ordered.append(piece)
-        outs[len(pairs) + NCOL + colour][...] = jnp.concatenate(ordered, axis=1)
+    pieces = [own[:, n * share : (n + 1) * share] for n in range(tiles)]
+    ordered = []
+    for step in range(tiles):
+        source = lax.rem(tile + tiles - step, tiles)
+        piece = pieces[0]
+        for n in range(1, tiles):
+            piece = jnp.where(source == n, pieces[n], piece)
+        ordered.append(piece)
+    rest = jnp.concatenate(ordered, axis=1)
+    row = lax.broadcasted_iota(jnp.int32, (EXTRA, size), 0)
+    block = jnp.zeros((EXTRA, size), F32)
+    for n in range(3):
+        part = rest.astype(BF16).astype(F32)
+        rest = rest - part
+        block = jnp.where(row == n, part, block)
+    for colour in range(NCOL):
+        offset = lax.rem(col + (NCOL - colour), NCOL)
+        sent = (offset == 0) | (offset == 2)
+        out = outs[len(pairs) + NCOL + colour]
+        out[...] = jnp.zeros(out.shape, BF16)
+        out[:, :size] = jnp.where(sent, block, 0.0).astype(BF16)
 
 
 def root_kernel(*refs):
@@ -174,13 +184,14 @@
 
 
 def rows_kernel(count, *refs):
-    *pairs, out = refs[count:]
+    *pairs, extra, out = refs[count:]
     rows = summed(refs[:count])
     for transformed, factor in zip(pairs[::2], pairs[1::2]):
         source = transformed[...]
         projected = dot_nt(rows.astype(BF16), source).astype(BF16)
         rows = rows - factor[...] * dot(projected, source)
-    out[...] = rows.astype(out.dtype)
+    out[: rows.shape[0], :] = rows.astype(out.dtype)
+    out[rows.shape[0] :, :] = extra[...]
 
 
 def tile_kernel(state, transformed, factor, out):
@@ -190,9 +201,24 @@
     out[...] = value - factor[...] * dot(projected, source)
 
 
-def sum_kernel(*refs):
-    *parts, out = refs
-    out[...] = summed(parts)
+def start_kernel(*refs):
+    *parts, extra, out = refs
+    rows = parts[0].shape[0]
+    out[:rows, :] = summed(parts)
+    out[rows:, :] = extra[...]
+
+
+def join_kernel(*refs):
+    *parts, whole, variance = refs
+    total = summed(parts)
+    rows, size = whole.shape[0], variance.shape[1]
+    whole[...] = total[:rows]
+    carried = total[rows:, :size].astype(F32)
+    row = lax.broadcasted_iota(jnp.int32, carried.shape, 0)
+    high, middle, low = (
+        jnp.sum(jnp.where(row == n, carried, 0.0), axis=0, keepdims=True) for n in range(3)
+    )
+    variance[...] = (high + middle) + low
 
 
 def on_device(anomalies, obs_rows, obs_var, taper_level):
@@ -232,9 +258,6 @@
         ]
         return hop(value, pairs)
 
-    def beside(value, step):
-        return hop(value, [((c, n), (c + step, n)) for c in everywhere for n in range(tiles)])
-
     def pick(colours, dtype, state):
         shape = jax.ShapeDtypeStruct((len(colours) * share, members), dtype)
         return kernel_call(
@@ -250,14 +273,15 @@
     def scattered(parts):
         return [parts[0], *[along_gy(parts[n], n) for n in range(1, tiles)]]
 
-    def added(parts):
-        shape = jax.ShapeDtypeStruct(parts[0].shape, parts[0].dtype)
-        return kernel_call(sum_kernel, shape, parts, "sum", 1_000_000)
-
     def joined(rows, colour, beside_it):
         first, second = (along_gx(rows, colour, step) for step in (1, 2))
         second, beside_it = lax.optimization_barrier((second, beside_it))
-        return added([rows, first, second]), beside_it
+        shapes = [
+            jax.ShapeDtypeStruct((share, members), BF16),
+            jax.ShapeDtypeStruct((1, size), F32),
+        ]
+        args = [rows, first, second]
+        return *kernel_call(join_kernel, shapes, args, "join", 1_000_000), beside_it
 
     def spread(whole):
         return [whole, *[along_gy(whole, step) for step in range(1, tiles)]]
@@ -293,55 +317,58 @@
             compiler_params=pltpu.CompilerParams(vmem_limit_bytes=VMEM_LIMIT),
         )(state, transformed, factor)
 
-    def move(parts, sources, dtype):
+    def move(parts, sources, extra):
         rows = share
         return kernel_call(
             functools.partial(rows_kernel, len(parts)),
-            jax.ShapeDtypeStruct((rows, members), dtype),
-            [*parts, *[ref for pair in sources for ref in pair]],
+            jax.ShapeDtypeStruct((rows + EXTRA, members), BF16),
+            [*parts, *[ref for pair in sources for ref in pair], extra],
             "rows",
             4 * rows * size * members * len(sources),
         )
 
-    together = lax.optimization_barrier
     parts = scattered(pick((0,), BF16, anomalies))
     picked = [None, *[pick((colour,), F32, anomalies) for colour in range(1, NCOL)]]
-    sides = [beside(obs_var, 1), beside(obs_var, -1)]
-    parts[-1], picked[1], sides = together((parts[-1], picked[1], sides))
-    total0 = added(parts)
-
     pairs = [((target,), source) for target in range(1, NCOL) for source in range(target)]
     prepared = kernel_call(
         functools.partial(setup_kernel, pairs, tiles, tile_rows),
         [jax.ShapeDtypeStruct((len(t) * share, 1), F32) for t, _ in pairs]
         + [jax.ShapeDtypeStruct((1, 1), F32)] * NCOL
-        + [jax.ShapeDtypeStruct((1, size), F32)] * NCOL,
-        [obs_rows, levels, place, obs_var, *sides],
+        + [jax.ShapeDtypeStruct((EXTRA, members), BF16)] * NCOL,
+        [obs_rows, levels, place, obs_var],
         "setup",
         1_000_000,
         smem=(1, 2),
     )
+    row_factor = {(t[0], source): out for (t, source), out in zip(pairs, prepared)}
+    tile_factor = prepared[len(pairs) : len(pairs) + NCOL]
+    extra = prepared[len(pairs) + NCOL :]
+    parts[-1], picked[1] = lax.optimization_barrier((parts[-1], picked[1]))
+    rows = kernel_call(
+        start_kernel,
+        jax.ShapeDtypeStruct((share + EXTRA, members), BF16),
+        [*parts, extra[0]],
+        "start",
+        1_000_000,
+    )
+
     state = anomalies
-    rows = total0
     done = []
     for colour in range(NCOL):
-        ahead = prepared if colour == 0 else [state, *picked[colour + 1 : colour + 2]]
-        whole, ahead = joined(rows, colour, ahead)
         if colour == 0:
-            row_factor = {(t[0], source): out for (t, source), out in zip(pairs, ahead)}
-            tile_factor = ahead[len(pairs) : len(pairs) + NCOL]
-            variance = ahead[len(pairs) + NCOL :]
+            whole, variance, picked[2:] = joined(rows, colour, picked[2:])
         else:
-            state, picked[colour + 1 : colour + 2] = ahead[0], ahead[1:]
+            whole, variance, state = joined(rows, colour, state)
         pieces = spread(whole)
         if colour < NCOL - 1:
-            coming, _ = together((picked[colour + 1], whole))
+            coming, _ = lax.optimization_barrier((picked[colour + 1], whole))
             parts = scattered(coming)
-        done.append(transform(pieces, variance[colour]))
+        done.append(transform(pieces, variance))
         if colour < NCOL - 1:
             sources = [(done[n], row_factor[colour + 1, n]) for n in range(colour + 1)]
-            rows = move(parts, sources, BF16)
-        state = move_tile(state, done[colour], tile_factor[colour], 4)
+            rows = move(parts, sources, extra[colour + 1])
+        blocks = 4 if colour < NCOL - 1 else LAST_BLOCKS
+        state = move_tile(state, done[colour], tile_factor[colour], blocks)
     return state
 
 

time: 144 us -> 142 us (0.986)
  starting transfers between devices: 47.6 us -> 43.6 us
  waiting for transfers between devices: 32.2 us -> 35.1 us
    ppermute x34 -> x32, starting transfers between devices: 47.6 us -> 43.6 us  [hop(): return lax.ppermute(value, AXES, flat)]
    ppermute x34 -> x32, waiting for transfers between devices: 32.2 us -> 35.1 us  [hop(): return lax.ppermute(value, AXES, flat)]
  transfers between devices with their start and end apart: 34 -> 32, of which waited for: 13 -> 20; matrix products, arithmetic and copies ran while one was open for 0% -> 0% of each run, Pallas kernels for 30% -> 30%
where the time goes in v2:
time: 142 us; the launch traced here: 141 us
  Pallas kernels  59.1 us (42%)
  starting transfers between devices  43.6 us (31%)
  waiting for transfers between devices  35.1 us (25%)
  local copies, waits for them, and re-layouts  2.55 us (2%)
    pallas_call x17, Pallas kernels, kernel_call(): pl.pallas_call(body, out_shape=out, in_specs=[scalar if n in smem else wh...  46.9 us
    ppermute x32, starting transfers between devices, hop(): return lax.ppermute(value, AXES, flat)  43.6 us
    ppermute x32, waiting for transfers between devices, hop(): return lax.ppermute(value, AXES, flat)  35.1 us
    pallas_call x4, Pallas kernels, move_tile(): pl.pallas_call(tile_kernel, out_shape=jax.ShapeDtypeStruct(state.shape, F...  12.2 us
  transfers between devices with their start and end apart: 32, of which 20 were waited for; matrix products, arithmetic and copies ran while one was open for 0% of the time, Pallas kernels for 30%

profile of v2, /device:TPU:6, one launch (start us, length us, event | category | flops | bytes accessed | tf_op | source)
XLA Modules:
  0.0 140.6 jit_solution(1666072674513416561)
XLA Ops:
  0.1 1.6 %copy-done = f32[512,1024]{1,0:T(8,128)S(1)} copy-done((f32[512,1024]{1,0:T(8,128)S(1)}, f32[512,1024]{1,0:T(8,128)}, u32[]{:S(2)}) %copy-start) | copy-done | bytes 2097176
  1.7 0.8 copy-done.2
  2.5 1.7 %pick.4 = (bf16[64,1024]{1,0:T(8,128)(2,1)S(1)}, bf16[64,1024]{1,0:T(8,128)(2,1)S(1)}, bf16[64,1024]{1,0:T(8,128)(2,1)S(1)}, bf16[64,1024]{1,0:T(8,128)(2,1)S(1)}) custom-call(f32[512,1024]{1,0:T(8,128)S(1)} %copy-done, s32[64,256]{1,0:T(8,128)S(1)} %copy-done.2, s32[1,3]{1,0:T(1,128)S(1)} %add_bitcast_fusion.place), custom_call_target="tpu_custom_call" | custom-call | flops 268435456 | bytes 2686988 | tf_op jit(solution)/shard_map/pick/pallas_call | solution.py:25
  4.2 0.9 collective-permute-start.2
  5.1 2.4 %collective-permute-start = (bf16[64,1024]{1,0:T(8,128)(2,1)S(1)}, bf16[64,1024]{1,0:T(8,128)(2,1)S(1)}, u32[]{:S(2)}, u32[]{:S(2)}) collective-permute-start(bf16[64,1024]{1,0:T(8,128)(2,1)S(1)} %get-tuple-element.76), channel_id=1, source_target_pairs={{0,1},{1,2},{2,3},{3,0},{4,5},{5,6},{6,7},{7,4},{8,9},{9,10},{10,1... | collective-permute-start | bytes 393224 | tf_op jit(solution)/shard_map/ppermute | solution.py:241
  7.5 0.4 collective-permute-start.1
  8.1 1.9 %setup.1 = (f32[64,1]{1,0:T(8,128)S(1)}, f32[64,1]{1,0:T(8,128)S(1)}, f32[64,1]{1,0:T(8,128)S(1)}, f32[64,1]{1,0:T(8,128)S(1)}, f32[64,1]{1,0:T(8,128)S(1)}, /*i...) custom-call(s32[64,256]{1,0:T(8,128)S(1)} %copy-done.3, ...), custom_call_target="tpu_custom_call" | custom-call | flops 1000000 | bytes 202268 | tf_op jit(solution)/shard_map/setup/pallas_call | solution.py:25
  10.0 2.4 %pick.5 = (f32[64,1024]{1,0:T(8,128)S(1)}, f32[64,1024]{1,0:T(8,128)S(1)}, f32[64,1024]{1,0:T(8,128)S(1)}, f32[64,1024]{1,0:T(8,128)S(1)}) custom-call(f32[512,1024]{1,0:T(8,128)S(1)} %copy-done.1, s32[64,256]{1,0:T(8,128)S(1)} %copy-done.3, s32[1,3]{1,0:T(1,128)S(1)} %add_bitcast_fusion.place), custom_call_target="tpu_custom_call" | custom-call | flops 805306368 | bytes 3211276 | tf_op jit(solution)/shard_map/pick/pallas_call | solution.py:25
  12.4 0.5 collective-permute-done.refs_1_
  12.8 1.2 collective-permute-done.1.refs_2_
  14.0 6.1 %collective-permute-start.3 = (bf16[80,1024]{1,0:T(8,128)(2,1)S(1)}, bf16[80,1024]{1,0:T(8,128)(2,1)S(1)}, u32[]{:S(2)}, u32[]{:S(2)}) collective-permute-start(bf16[80,1024]{1,0:T(8,128)(2,1)S(1)} %start.1.refs_0_), channel_id=1, source_target_pairs={{252,4},{253,5},{254,6},{255,7},{0,252},{1,253},{2,254},{3,255},{4... | collective-permute-start | bytes 491528 | tf_op jit(solution)/shard_map/ppermute | solution.py:241
  20.1 2.4 %pick.6 = (f32[64,1024]{1,0:T(8,128)S(1)}, f32[64,1024]{1,0:T(8,128)S(1)}, f32[64,1024]{1,0:T(8,128)S(1)}, f32[64,1024]{1,0:T(8,128)S(1)}) custom-call(f32[512,1024]{1,0:T(8,128)S(1)} %copy-done.1, s32[64,256]{1,0:T(8,128)S(1)} %copy-done.3, s32[1,3]{1,0:T(1,128)S(1)} %add_bitcast_fusion.place), custom_call_target="tpu_custom_call" | custom-call | flops 805306368 | bytes 3211276 | tf_op jit(solution)/shard_map/pick/pallas_call | solution.py:25
  22.5 2.4 %pick.7 = (f32[64,1024]{1,0:T(8,128)S(1)}, f32[64,1024]{1,0:T(8,128)S(1)}, f32[64,1024]{1,0:T(8,128)S(1)}, f32[64,1024]{1,0:T(8,128)S(1)}) custom-call(f32[512,1024]{1,0:T(8,128)S(1)} %copy-done.1, s32[64,256]{1,0:T(8,128)S(1)} %copy-done.3, s32[1,3]{1,0:T(1,128)S(1)} %add_bitcast_fusion.place), custom_call_target="tpu_custom_call" | custom-call | flops 805306368 | bytes 3211276 | tf_op jit(solution)/shard_map/pick/pallas_call | solution.py:25
  24.9 3.3 %collective-permute-done.4.refs_1_ = bf16[80,1024]{1,0:T(8,128)(2,1)S(1)} collective-permute-done((bf16[80,1024]{1,0:T(8,128)(2,1)S(1)}, bf16[80,1024]{1,0:T(8,128)(2,1)S(1)}, u32[]{:S(2)}, u32[]{:S(2)}) %collective-permute-start.4) | collective-permute-done | bytes 163872 | tf_op jit(solution)/shard_map/ppermute | solution.py:241
  28.2 2.2 %collective-permute-start.8 = (bf16[64,1024]{1,0:T(8,128)(2,1)S(1)}, bf16[64,1024]{1,0:T(8,128)(2,1)S(1)}, u32[]{:S(2)}, u32[]{:S(2)}) collective-permute-start(bf16[64,1024]{1,0:T(8,128)(2,1)S(1)} %get-tuple-element.106.refs_0_), channel_id=1, source_target_pairs={{0,1},{1,2},{2,3},{3,0},{4,5},{5,6},{6,7},{7,4},{8,9},{9,10},{10,1... | collective-permute-start | bytes 393224 | tf_op jit(solution)/shard_map/ppermute | solution.py:241
  30.5 1.3 collective-permute-start.9
  31.7 0.4 collective-permute-start.10
  32.1 2.9 %collective-permute-start.5 = (f32[64,1024]{1,0:T(8,128)S(1)}, f32[64,1024]{1,0:T(8,128)S(1)}, u32[]{:S(2)}, u32[]{:S(2)}) collective-permute-start(f32[64,1024]{1,0:T(8,128)S(1)} %get-tuple-element.108), channel_id=1, source_target_pairs={{0,1},{1,2},{2,3},{3,0},{4,5},{5,6},{6,7},{7,4},{8,9},{9,10},{10,1... | collective-permute-start | bytes 786440 | tf_op jit(solution)/shard_map/ppermute | solution.py:241
  35.0 1.0 collective-permute-start.6
  36.0 2.4 %collective-permute-done.9.refs_2_ = bf16[64,1024]{1,0:T(8,128)(2,1)S(1)} collective-permute-done((bf16[64,1024]{1,0:T(8,128)(2,1)S(1)}, bf16[64,1024]{1,0:T(8,128)(2,1)S(1)}, u32[]{:S(2)}, u32[]{:S(2)}) %collective-permute-start.9) | collective-permute-done | bytes 131104 | tf_op jit(solution)/shard_map/ppermute | solution.py:241
  38.4 4.4 %collective-permute-done.10.refs_3_ = bf16[64,1024]{1,0:T(8,128)(2,1)S(1)} collective-permute-done((bf16[64,1024]{1,0:T(8,128)(2,1)S(1)}, bf16[64,1024]{1,0:T(8,128)(2,1)S(1)}, u32[]{:S(2)}, u32[]{:S(2)}) %collective-permute-start.10) | collective-permute-done | bytes 131104 | tf_op jit(solution)/shard_map/ppermute | solution.py:241
  42.8 8.2 %root.4.refs_4_.transformed = bf16[256,1024]{1,0:T(8,128)(2,1)S(1)} custom-call(bf16[64,1024]{1,0:T(8,128)(2,1)S(1)} %get-tuple-element.106.refs_0_, bf16[64,1024]{1,0:T(8,128)(2,1)S(1)} %collective-permute-done.8.refs_1_, bf16[64,1024]{1,0:T(8,128)(2,1)S(1)} %collective-permute-done.9.refs_2_, bf16[64,1024]{1,0:T(8,128)(2,1)S(1)} %collective-permute-done.10.refs_3_, ...), custom_call_target="tpu_custom_call" | custom-call | flops 8000000000 | bytes 1049600 | tf_op jit(solution)/shard_map/root/pallas_call | solution.py:25
  51.0 0.6 rows.3.refs_0_
  51.6 0.3 collective-permute-start.12
  51.8 0.5 collective-permute-start.11
  52.3 3.1 %tile.4.state = f32[512,1024]{1,0:T(8,128)S(1)} custom-call(f32[512,1024]{1,0:T(8,128)S(1)} %copy-done.1, bf16[256,1024]{1,0:T(8,128)(2,1)S(1)} %root.4.refs_4_.transformed, f32[1,1]{1,0:T(1,128)} %get-tuple-element.114.factor), custom_call_target="tpu_custom_call" | custom-call | flops 536870912 | bytes 4194304 | tf_op jit(solution)/shard_map/tile/pallas_call | solution.py:300
  55.4 0.8 collective-permute-done.12.refs_2_
  56.2 1.0 collective-permute-done.11.refs_1_
  57.4 0.9 collective-permute-start.17
  58.3 1.3 collective-permute-start.18
  59.6 2.5 %collective-permute-start.13 = (f32[64,1024]{1,0:T(8,128)S(1)}, f32[64,1024]{1,0:T(8,128)S(1)}, u32[]{:S(2)}, u32[]{:S(2)}) collective-permute-start(f32[64,1024]{1,0:T(8,128)S(1)} %get-tuple-element.118), channel_id=1, source_target_pairs={{0,1},{1,2},{2,3},{3,0},{4,5},{5,6},{6,7},{7,4},{8,9},{9,10},{10,1... | collective-permute-start | bytes 786440 | tf_op jit(solution)/shard_map/ppermute | solution.py:241
  62.1 1.5 %collective-permute-start.14 = (f32[64,1024]{1,0:T(8,128)S(1)}, f32[64,1024]{1,0:T(8,128)S(1)}, u32[]{:S(2)}, u32[]{:S(2)}) collective-permute-start(f32[64,1024]{1,0:T(8,128)S(1)} %get-tuple-element.119), channel_id=1, source_target_pairs={{0,2},{1,3},{2,0},{3,1},{4,6},{5,7},{6,4},{7,5},{8,10},{9,11},{10,... | collective-permute-start | bytes 786440 | tf_op jit(solution)/shard_map/ppermute | solution.py:241
  63.5 0.3 collective-permute-done.16.refs_1_
  63.8 1.2 collective-permute-start.15
  64.9 0.4 collective-permute-done.17.refs_2_
  65.3 5.9 %collective-permute-done.18.refs_3_ = bf16[64,1024]{1,0:T(8,128)(2,1)S(1)} collective-permute-done((bf16[64,1024]{1,0:T(8,128)(2,1)S(1)}, bf16[64,1024]{1,0:T(8,128)(2,1)S(1)}, u32[]{:S(2)}, u32[]{:S(2)}) %collective-permute-start.18) | collective-permute-done | bytes 131104 | tf_op jit(solution)/shard_map/ppermute | solution.py:241
  71.3 8.2 %root.5.refs_6_.transformed = bf16[256,1024]{1,0:T(8,128)(2,1)S(1)} custom-call(bf16[64,1024]{1,0:T(8,128)(2,1)S(1)} %get-tuple-element.116.refs_0_, bf16[64,1024]{1,0:T(8,128)(2,1)S(1)} %collective-permute-done.16.refs_1_, bf16[64,1024]{1,0:T(8,128)(2,1)S(1)} %collective-permute-done.17.refs_2_, bf16[64,1024]{1,0:T(8,128)(2,1)S(1)} %collective-permute-done.18.refs_3_, ...), custom_call_target="tpu_custom_call" | custom-call | flops 8000000000 | bytes 1049600 | tf_op jit(solution)/shard_map/root/pallas_call | solution.py:25
  79.5 1.2 rows.4.refs_0_
  80.7 2.0 %collective-permute-start.19 = (bf16[80,1024]{1,0:T(8,128)(2,1)S(1)}, bf16[80,1024]{1,0:T(8,128)(2,1)S(1)}, u32[]{:S(2)}, u32[]{:S(2)}) collective-permute-start(bf16[80,1024]{1,0:T(8,128)(2,1)S(1)} %rows.4.refs_0_), channel_id=1, source_target_pairs={{4,8},{5,9},{6,10},{7,11},{8,12},{9,13},{10,14},{11,15},{12,4},{13... | collective-permute-start | bytes 491528 | tf_op jit(solution)/shard_map/ppermute | solution.py:241
  82.7 3.0 %tile.5.state = f32[512,1024]{1,0:T(8,128)S(1)} custom-call(f32[512,1024]{1,0:T(8,128)S(1)} %tile.4.state, bf16[256,1024]{1,0:T(8,128)(2,1)S(1)} %root.5.refs_6_.transformed, f32[1,1]{1,0:T(1,128)} %get-tuple-element.126.factor), custom_call_target="tpu_custom_call" | custom-call | flops 536870912 | bytes 4194304 | tf_op jit(solution)/shard_map/tile/pallas_call | solution.py:300
  85.7 0.3 collective-permute-done.20.refs_2_
  86.0 2.9 %collective-permute-done.19.refs_1_ = bf16[80,1024]{1,0:T(8,128)(2,1)S(1)} collective-permute-done((bf16[80,1024]{1,0:T(8,128)(2,1)S(1)}, bf16[80,1024]{1,0:T(8,128)(2,1)S(1)}, u32[]{:S(2)}, u32[]{:S(2)}) %collective-permute-start.19) | collective-permute-done | bytes 163872 | tf_op jit(solution)/shard_map/ppermute | solution.py:241
  89.0 2.0 %collective-permute-start.25 = (bf16[64,1024]{1,0:T(8,128)(2,1)S(1)}, bf16[64,1024]{1,0:T(8,128)(2,1)S(1)}, u32[]{:S(2)}, u32[]{:S(2)}) collective-permute-start(bf16[64,1024]{1,0:T(8,128)(2,1)S(1)} %get-tuple-element.128.refs_0_), channel_id=1, source_target_pairs={{0,2},{1,3},{2,0},{3,1},{4,6},{5,7},{6,4},{7,5},{8,10},{9,11},{10,... | collective-permute-start | bytes 393224 | tf_op jit(solution)/shard_map/ppermute | solution.py:241
  91.0 1.3 collective-permute-start.26
  92.4 1.9 %collective-permute-start.21 = (f32[64,1024]{1,0:T(8,128)S(1)}, f32[64,1024]{1,0:T(8,128)S(1)}, u32[]{:S(2)}, u32[]{:S(2)}) collective-permute-start(f32[64,1024]{1,0:T(8,128)S(1)} %get-tuple-element.130), channel_id=1, source_target_pairs={{0,1},{1,2},{2,3},{3,0},{4,5},{5,6},{6,7},{7,4},{8,9},{9,10},{10,1... | collective-permute-start | bytes 786440 | tf_op jit(solution)/shard_map/ppermute | solution.py:241
  94.3 0.9 collective-permute-start.22
  95.2 0.3 collective-permute-done.24.refs_1_
  95.4 1.2 collective-permute-start.23
  96.6 0.5 collective-permute-done.25.refs_2_
  97.1 2.2 %collective-permute-done.26.refs_3_ = bf16[64,1024]{1,0:T(8,128)(2,1)S(1)} collective-permute-done((bf16[64,1024]{1,0:T(8,128)(2,1)S(1)}, bf16[64,1024]{1,0:T(8,128)(2,1)S(1)}, u32[]{:S(2)}, u32[]{:S(2)}) %collective-permute-start.26) | collective-permute-done | bytes 131104 | tf_op jit(solution)/shard_map/ppermute | solution.py:241
  99.3 8.2 %root.6.refs_8_.transformed = bf16[256,1024]{1,0:T(8,128)(2,1)S(1)} custom-call(bf16[64,1024]{1,0:T(8,128)(2,1)S(1)} %get-tuple-element.128.refs_0_, bf16[64,1024]{1,0:T(8,128)(2,1)S(1)} %collective-permute-done.24.refs_1_, bf16[64,1024]{1,0:T(8,128)(2,1)S(1)} %collective-permute-done.25.refs_2_, bf16[64,1024]{1,0:T(8,128)(2,1)S(1)} %collective-permute-done.26.refs_3_, ...), custom_call_target="tpu_custom_call" | custom-call | flops 8000000000 | bytes 1049600 | tf_op jit(solution)/shard_map/root/pallas_call | solution.py:25
  107.5 1.6 %rows.5.refs_0_ = bf16[80,1024]{1,0:T(8,128)(2,1)S(1)} custom-call(f32[64,1024]{1,0:T(8,128)S(1)} %get-tuple-element.129.refs_0_, f32[64,1024]{1,0:T(8,128)S(1)} %collective-permute-done.21.refs_1_, f32[64,1024]{1,0:T(8,128)S(1)} %collective-permute-done.22.refs_2_, f32[64,1024]{1,0:T(8,128)S(1)} %collective-permute-done.23.refs_3_, ...), custom_call_target="tpu_custom_call" | custom-call | flops 201326592 | bytes 2818816 | tf_op jit(solution)/shard_map/rows/pallas_call | solution.py:25
  109.1 2.5 %collective-permute-start.27 = (bf16[80,1024]{1,0:T(8,128)(2,1)S(1)}, bf16[80,1024]{1,0:T(8,128)(2,1)S(1)}, u32[]{:S(2)}, u32[]{:S(2)}) collective-permute-start(bf16[80,1024]{1,0:T(8,128)(2,1)S(1)} %rows.5.refs_0_), channel_id=1, source_target_pairs={{8,16},{9,17},{10,18},{11,19},{12,8},{13,9},{14,10},{15,11},{16,12... | collective-permute-start | bytes 491528 | tf_op jit(solution)/shard_map/ppermute | solution.py:241
  111.5 3.0 %collective-permute-start.28 = (bf16[80,1024]{1,0:T(8,128)(2,1)S(1)}, bf16[80,1024]{1,0:T(8,128)(2,1)S(1)}, u32[]{:S(2)}, u32[]{:S(2)}) collective-permute-start(bf16[80,1024]{1,0:T(8,128)(2,1)S(1)} %rows.5.refs_0_), channel_id=1, source_target_pairs={{8,12},{9,13},{10,14},{11,15},{12,16},{13,17},{14,18},{15,19},{16,... | collective-permute-start | bytes 491528 | tf_op jit(solution)/shard_map/ppermute | solution.py:241
  114.6 3.1 %tile.6.state = f32[512,1024]{1,0:T(8,128)S(1)} custom-call(f32[512,1024]{1,0:T(8,128)S(1)} %tile.5.state, bf16[256,1024]{1,0:T(8,128)(2,1)S(1)} %root.6.refs_8_.transformed, f32[1,1]{1,0:T(1,128)} %get-tuple-element.139.factor), custom_call_target="tpu_custom_call" | custom-call | flops 536870912 | bytes 4194304 | tf_op jit(solution)/shard_map/tile/pallas_call | solution.py:300
  117.6 0.2 collective-permute-done.27.refs_2_
  117.8 1.8 %collective-permute-done.28.refs_1_ = bf16[80,1024]{1,0:T(8,128)(2,1)S(1)} collective-permute-done((bf16[80,1024]{1,0:T(8,128)(2,1)S(1)}, bf16[80,1024]{1,0:T(8,128)(2,1)S(1)}, u32[]{:S(2)}, u32[]{:S(2)}) %collective-permute-start.28) | collective-permute-done | bytes 163872 | tf_op jit(solution)/shard_map/ppermute | solution.py:241
  119.6 1.8 %collective-permute-start.29 = (bf16[64,1024]{1,0:T(8,128)(2,1)S(1)}, bf16[64,1024]{1,0:T(8,128)(2,1)S(1)}, u32[]{:S(2)}, u32[]{:S(2)}) collective-permute-start(bf16[64,1024]{1,0:T(8,128)(2,1)S(1)} %get-tuple-element.142.refs_0_), channel_id=1, source_target_pairs={{0,1},{1,2},{2,3},{3,0},{4,5},{5,6},{6,7},{7,4},{8,9},{9,10},{10,1... | collective-permute-start | bytes 393224 | tf_op jit(solution)/shard_map/ppermute | solution.py:241
  121.4 0.9 collective-permute-start.30
  122.4 2.3 %collective-permute-done.29.refs_1_ = bf16[64,1024]{1,0:T(8,128)(2,1)S(1)} collective-permute-done((bf16[64,1024]{1,0:T(8,128)(2,1)S(1)}, bf16[64,1024]{1,0:T(8,128)(2,1)S(1)}, u32[]{:S(2)}, u32[]{:S(2)}) %collective-permute-start.29) | collective-permute-done | bytes 131104 | tf_op jit(solution)/shard_map/ppermute | solution.py:241
  124.7 3.3 %collective-permute-done.30.refs_2_ = bf16[64,1024]{1,0:T(8,128)(2,1)S(1)} collective-permute-done((bf16[64,1024]{1,0:T(8,128)(2,1)S(1)}, bf16[64,1024]{1,0:T(8,128)(2,1)S(1)}, u32[]{:S(2)}, u32[]{:S(2)}) %collective-permute-start.30) | collective-permute-done | bytes 131104 | tf_op jit(solution)/shard_map/ppermute | solution.py:241
  128.0 1.3 collective-permute-done.31.refs_3_
  129.3 8.2 %root.7.transformed = bf16[256,1024]{1,0:T(8,128)(2,1)S(1)} custom-call(bf16[64,1024]{1,0:T(8,128)(2,1)S(1)} %get-tuple-element.142.refs_0_, bf16[64,1024]{1,0:T(8,128)(2,1)S(1)} %collective-permute-done.29.refs_1_, bf16[64,1024]{1,0:T(8,128)(2,1)S(1)} %collective-permute-done.30.refs_2_, bf16[64,1024]{1,0:T(8,128)(2,1)S(1)} %collective-permute-done.31.refs_3_, ...), custom_call_target="tpu_custom_call" | custom-call | flops 8000000000 | bytes 1049600 | tf_op jit(solution)/shard_map/root/pallas_call | solution.py:25
  137.5 3.1 %tile.7 = f32[512,1024]{1,0:T(8,128)} custom-call(f32[512,1024]{1,0:T(8,128)S(1)} %tile.6.state, bf16[256,1024]{1,0:T(8,128)(2,1)S(1)} %root.7.transformed, f32[1,1]{1,0:T(1,128)} %get-tuple-element.144.factor), custom_call_target="tpu_custom_call" | custom-call | flops 536870912 | bytes 4194304 | tf_op jit(solution)/shard_map/tile/pallas_call | solution.py:300
  (36 shorter events, 0.8 us)
Async XLA Ops:
  0.0 8.0 %copy-start.5 = (s32[64,3,4]{0,2,1:T(4,128)S(1)}, s32[64,3,4]{0,2,1:T(4,128)}, u32[]{:S(2)}) copy-start(s32[64,3,4]{0,2,1:T(4,128)} %param.7) | copy-start | bytes 9220
  0.0 8.1 %copy-start.4 = (f32[1,256]{1,0:T(1,128)S(1)}, f32[1,256]{1,0:T(1,128)}, u32[]{:S(2)}) copy-start(f32[1,256]{1,0:T(1,128)} %own.1) | copy-start | bytes 3076
  0.1 1.6 %copy-start = (f32[512,1024]{1,0:T(8,128)S(1)}, f32[512,1024]{1,0:T(8,128)}, u32[]{:S(2)}) copy-start(f32[512,1024]{1,0:T(8,128)} %state.9) | copy-start | bytes 6291460
  1.7 0.8 copy-start.2
  2.5 5.6 %copy-start.3 = (s32[64,256]{1,0:T(8,128)S(1)}, s32[64,256]{1,0:T(8,128)}, u32[]{:S(2)}) copy-start(s32[64,256]{1,0:T(8,128)} %obs.9) | copy-start | bytes 196612
  2.5 7.5 %copy-start.1 = (f32[512,1024]{1,0:T(8,128)S(1)}, f32[512,1024]{1,0:T(8,128)}, u32[]{:S(2)}) copy-start(f32[512,1024]{1,0:T(8,128)} %state.9) | copy-start | bytes 6291460
  4.2 8.2 %collective-permute-start.2 = (bf16[64,1024]{1,0:T(8,128)(2,1)S(1)}, bf16[64,1024]{1,0:T(8,128)(2,1)S(1)}, u32[]{:S(2)}, u32[]{:S(2)}) collective-permute-start(bf16[64,1024]{1,0:T(8,128)(2,1)S(1)} %get-tuple-element.78), channel_id=1, source_target_pairs={{0,3},{1,0},{2,1},{3,2},{4,7},{5,4},{6,5},{7,6},{8,11},{9,8},{10,9... | collective-permute-start | bytes 393224 | tf_op jit(solution)/shard_map/ppermute | solution.py:241
  5.1 7.7 %collective-permute-start = (bf16[64,1024]{1,0:T(8,128)(2,1)S(1)}, bf16[64,1024]{1,0:T(8,128)(2,1)S(1)}, u32[]{:S(2)}, u32[]{:S(2)}) collective-permute-start(bf16[64,1024]{1,0:T(8,128)(2,1)S(1)} %get-tuple-element.76), channel_id=1, source_target_pairs={{0,1},{1,2},{2,3},{3,0},{4,5},{5,6},{6,7},{7,4},{8,9},{9,10},{10,1... | collective-permute-start | bytes 393224 | tf_op jit(solution)/shard_map/ppermute | solution.py:241
  7.5 6.5 %collective-permute-start.1 = (bf16[64,1024]{1,0:T(8,128)(2,1)S(1)}, bf16[64,1024]{1,0:T(8,128)(2,1)S(1)}, u32[]{:S(2)}, u32[]{:S(2)}) collective-permute-start(bf16[64,1024]{1,0:T(8,128)(2,1)S(1)} %get-tuple-element.77), channel_id=1, source_target_pairs={{0,2},{1,3},{2,0},{3,1},{4,6},{5,7},{6,4},{7,5},{8,10},{9,11},{10,... | collective-permute-start | bytes 393224 | tf_op jit(solution)/shard_map/ppermute | solution.py:241
  14.0 10.9 %collective-permute-start.3 = (bf16[80,1024]{1,0:T(8,128)(2,1)S(1)}, bf16[80,1024]{1,0:T(8,128)(2,1)S(1)}, u32[]{:S(2)}, u32[]{:S(2)}) collective-permute-start(bf16[80,1024]{1,0:T(8,128)(2,1)S(1)} %start.1.refs_0_), channel_id=1, source_target_pairs={{252,4},{253,5},{254,6},{255,7},{0,252},{1,253},{2,254},{3,255},{4... | collective-permute-start | bytes 491528 | tf_op jit(solution)/shard_map/ppermute | solution.py:241
  20.1 8.1 %collective-permute-start.4 = (bf16[80,1024]{1,0:T(8,128)(2,1)S(1)}, bf16[80,1024]{1,0:T(8,128)(2,1)S(1)}, u32[]{:S(2)}, u32[]{:S(2)}) collective-permute-start(bf16[80,1024]{1,0:T(8,128)(2,1)S(1)} %start.1.refs_0_), channel_id=1, source_target_pairs={{252,0},{253,1},{254,2},{255,3},{0,4},{1,5},{2,6},{3,7},{4,252},{5... | collective-permute-start | bytes 491528 | tf_op jit(solution)/shard_map/ppermute | solution.py:241
  28.2 7.8 %collective-permute-start.8 = (bf16[64,1024]{1,0:T(8,128)(2,1)S(1)}, bf16[64,1024]{1,0:T(8,128)(2,1)S(1)}, u32[]{:S(2)}, u32[]{:S(2)}) collective-permute-start(bf16[64,1024]{1,0:T(8,128)(2,1)S(1)} %get-tuple-element.106.refs_0_), channel_id=1, source_target_pairs={{0,1},{1,2},{2,3},{3,0},{4,5},{5,6},{6,7},{7,4},{8,9},{9,10},{10,1... | collective-permute-start | bytes 393224 | tf_op jit(solution)/shard_map/ppermute | solution.py:241
  30.5 7.9 %collective-permute-start.9 = (bf16[64,1024]{1,0:T(8,128)(2,1)S(1)}, bf16[64,1024]{1,0:T(8,128)(2,1)S(1)}, u32[]{:S(2)}, u32[]{:S(2)}) collective-permute-start(bf16[64,1024]{1,0:T(8,128)(2,1)S(1)} %get-tuple-element.106.refs_0_), channel_id=1, source_target_pairs={{0,2},{1,3},{2,0},{3,1},{4,6},{5,7},{6,4},{7,5},{8,10},{9,11},{10,... | collective-permute-start | bytes 393224 | tf_op jit(solution)/shard_map/ppermute | solution.py:241
  31.7 11.0 %collective-permute-start.10 = (bf16[64,1024]{1,0:T(8,128)(2,1)S(1)}, bf16[64,1024]{1,0:T(8,128)(2,1)S(1)}, u32[]{:S(2)}, u32[]{:S(2)}) collective-permute-start(bf16[64,1024]{1,0:T(8,128)(2,1)S(1)} %get-tuple-element.106.refs_0_), channel_id=1, source_target_pairs={{0,3},{1,0},{2,1},{3,2},{4,7},{5,4},{6,5},{7,6},{8,11},{9,8},{10,9... | collective-permute-start | bytes 393224 | tf_op jit(solution)/shard_map/ppermute | solution.py:241
  32.1 18.8 %collective-permute-start.5 = (f32[64,1024]{1,0:T(8,128)S(1)}, f32[64,1024]{1,0:T(8,128)S(1)}, u32[]{:S(2)}, u32[]{:S(2)}) collective-permute-start(f32[64,1024]{1,0:T(8,128)S(1)} %get-tuple-element.108), channel_id=1, source_target_pairs={{0,1},{1,2},{2,3},{3,0},{4,5},{5,6},{6,7},{7,4},{8,9},{9,10},{10,1... | collective-permute-start | bytes 786440 | tf_op jit(solution)/shard_map/ppermute | solution.py:241
  35.0 16.0 %collective-permute-start.6 = (f32[64,1024]{1,0:T(8,128)S(1)}, f32[64,1024]{1,0:T(8,128)S(1)}, u32[]{:S(2)}, u32[]{:S(2)}) collective-permute-start(f32[64,1024]{1,0:T(8,128)S(1)} %get-tuple-element.109), channel_id=1, source_target_pairs={{0,2},{1,3},{2,0},{3,1},{4,6},{5,7},{6,4},{7,5},{8,10},{9,11},{10,... | collective-permute-start | bytes 786440 | tf_op jit(solution)/shard_map/ppermute | solution.py:241
  36.0 15.0 %collective-permute-start.7 = (f32[64,1024]{1,0:T(8,128)S(1)}, f32[64,1024]{1,0:T(8,128)S(1)}, u32[]{:S(2)}, u32[]{:S(2)}) collective-permute-start(f32[64,1024]{1,0:T(8,128)S(1)} %get-tuple-element.110), channel_id=1, source_target_pairs={{0,3},{1,0},{2,1},{3,2},{4,7},{5,4},{6,5},{7,6},{8,11},{9,8},{10,9... | collective-permute-start | bytes 786440 | tf_op jit(solution)/shard_map/ppermute | solution.py:241
  51.6 4.7 %collective-permute-start.12 = (bf16[80,1024]{1,0:T(8,128)(2,1)S(1)}, bf16[80,1024]{1,0:T(8,128)(2,1)S(1)}, u32[]{:S(2)}, u32[]{:S(2)}) collective-permute-start(bf16[80,1024]{1,0:T(8,128)(2,1)S(1)} %rows.3.refs_0_), channel_id=1, source_target_pairs={{0,8},{1,9},{2,10},{3,11},{4,0},{5,1},{6,2},{7,3},{8,4},{9,5},{10,... | collective-permute-start | bytes 491528 | tf_op jit(solution)/shard_map/ppermute | solution.py:241
  51.8 5.4 %collective-permute-start.11 = (bf16[80,1024]{1,0:T(8,128)(2,1)S(1)}, bf16[80,1024]{1,0:T(8,128)(2,1)S(1)}, u32[]{:S(2)}, u32[]{:S(2)}) collective-permute-start(bf16[80,1024]{1,0:T(8,128)(2,1)S(1)} %rows.3.refs_0_), channel_id=1, source_target_pairs={{0,4},{1,5},{2,6},{3,7},{4,8},{5,9},{6,10},{7,11},{8,0},{9,1},{10,... | collective-permute-start | bytes 491528 | tf_op jit(solution)/shard_map/ppermute | solution.py:241
  57.3 6.5 %collective-permute-start.16 = (bf16[64,1024]{1,0:T(8,128)(2,1)S(1)}, bf16[64,1024]{1,0:T(8,128)(2,1)S(1)}, u32[]{:S(2)}, u32[]{:S(2)}) collective-permute-start(bf16[64,1024]{1,0:T(8,128)(2,1)S(1)} %get-tuple-element.116.refs_0_), channel_id=1, source_target_pairs={{0,1},{1,2},{2,3},{3,0},{4,5},{5,6},{6,7},{7,4},{8,9},{9,10},{10,1... | collective-permute-start | bytes 393224 | tf_op jit(solution)/shard_map/ppermute | solution.py:241
  57.4 8.0 %collective-permute-start.17 = (bf16[64,1024]{1,0:T(8,128)(2,1)S(1)}, bf16[64,1024]{1,0:T(8,128)(2,1)S(1)}, u32[]{:S(2)}, u32[]{:S(2)}) collective-permute-start(bf16[64,1024]{1,0:T(8,128)(2,1)S(1)} %get-tuple-element.116.refs_0_), channel_id=1, source_target_pairs={{0,2},{1,3},{2,0},{3,1},{4,6},{5,7},{6,4},{7,5},{8,10},{9,11},{10,... | collective-permute-start | bytes 393224 | tf_op jit(solution)/shard_map/ppermute | solution.py:241
  58.3 13.0 %collective-permute-start.18 = (bf16[64,1024]{1,0:T(8,128)(2,1)S(1)}, bf16[64,1024]{1,0:T(8,128)(2,1)S(1)}, u32[]{:S(2)}, u32[]{:S(2)}) collective-permute-start(bf16[64,1024]{1,0:T(8,128)(2,1)S(1)} %get-tuple-element.116.refs_0_), channel_id=1, source_target_pairs={{0,3},{1,0},{2,1},{3,2},{4,7},{5,4},{6,5},{7,6},{8,11},{9,8},{10,9... | collective-permute-start | bytes 393224 | tf_op jit(solution)/shard_map/ppermute | solution.py:241
  59.6 19.8 %collective-permute-start.13 = (f32[64,1024]{1,0:T(8,128)S(1)}, f32[64,1024]{1,0:T(8,128)S(1)}, u32[]{:S(2)}, u32[]{:S(2)}) collective-permute-start(f32[64,1024]{1,0:T(8,128)S(1)} %get-tuple-element.118), channel_id=1, source_target_pairs={{0,1},{1,2},{2,3},{3,0},{4,5},{5,6},{6,7},{7,4},{8,9},{9,10},{10,1... | collective-permute-start | bytes 786440 | tf_op jit(solution)/shard_map/ppermute | solution.py:241
  62.1 17.4 %collective-permute-start.14 = (f32[64,1024]{1,0:T(8,128)S(1)}, f32[64,1024]{1,0:T(8,128)S(1)}, u32[]{:S(2)}, u32[]{:S(2)}) collective-permute-start(f32[64,1024]{1,0:T(8,128)S(1)} %get-tuple-element.119), channel_id=1, source_target_pairs={{0,2},{1,3},{2,0},{3,1},{4,6},{5,7},{6,4},{7,5},{8,10},{9,11},{10,... | collective-permute-start | bytes 786440 | tf_op jit(solution)/shard_map/ppermute | solution.py:241
  63.8 15.7 %collective-permute-start.15 = (f32[64,1024]{1,0:T(8,128)S(1)}, f32[64,1024]{1,0:T(8,128)S(1)}, u32[]{:S(2)}, u32[]{:S(2)}) collective-permute-start(f32[64,1024]{1,0:T(8,128)S(1)} %get-tuple-element.120), channel_id=1, source_target_pairs={{0,3},{1,0},{2,1},{3,2},{4,7},{5,4},{6,5},{7,6},{8,11},{9,8},{10,9... | collective-permute-start | bytes 786440 | tf_op jit(solution)/shard_map/ppermute | solution.py:241
  80.6 5.4 %collective-permute-start.20 = (bf16[80,1024]{1,0:T(8,128)(2,1)S(1)}, bf16[80,1024]{1,0:T(8,128)(2,1)S(1)}, u32[]{:S(2)}, u32[]{:S(2)}) collective-permute-start(bf16[80,1024]{1,0:T(8,128)(2,1)S(1)} %rows.4.refs_0_), channel_id=1, source_target_pairs={{4,12},{5,13},{6,14},{7,15},{8,4},{9,5},{10,6},{11,7},{12,8},{13,9... | collective-permute-start | bytes 491528 | tf_op jit(solution)/shard_map/ppermute | solution.py:241
  80.7 8.2 %collective-permute-start.19 = (bf16[80,1024]{1,0:T(8,128)(2,1)S(1)}, bf16[80,1024]{1,0:T(8,128)(2,1)S(1)}, u32[]{:S(2)}, u32[]{:S(2)}) collective-permute-start(bf16[80,1024]{1,0:T(8,128)(2,1)S(1)} %rows.4.refs_0_), channel_id=1, source_target_pairs={{4,8},{5,9},{6,10},{7,11},{8,12},{9,13},{10,14},{11,15},{12,4},{13... | collective-permute-start | bytes 491528 | tf_op jit(solution)/shard_map/ppermute | solution.py:241
  88.9 6.5 %collective-permute-start.24 = (bf16[64,1024]{1,0:T(8,128)(2,1)S(1)}, bf16[64,1024]{1,0:T(8,128)(2,1)S(1)}, u32[]{:S(2)}, u32[]{:S(2)}) collective-permute-start(bf16[64,1024]{1,0:T(8,128)(2,1)S(1)} %get-tuple-element.128.refs_0_), channel_id=1, source_target_pairs={{0,1},{1,2},{2,3},{3,0},{4,5},{5,6},{6,7},{7,4},{8,9},{9,10},{10,1... | collective-permute-start | bytes 393224 | tf_op jit(solution)/shard_map/ppermute | solution.py:241
  89.0 8.1 %collective-permute-start.25 = (bf16[64,1024]{1,0:T(8,128)(2,1)S(1)}, bf16[64,1024]{1,0:T(8,128)(2,1)S(1)}, u32[]{:S(2)}, u32[]{:S(2)}) collective-permute-start(bf16[64,1024]{1,0:T(8,128)(2,1)S(1)} %get-tuple-element.128.refs_0_), channel_id=1, source_target_pairs={{0,2},{1,3},{2,0},{3,1},{4,6},{5,7},{6,4},{7,5},{8,10},{9,11},{10,... | collective-permute-start | bytes 393224 | tf_op jit(solution)/shard_map/ppermute | solution.py:241
  91.0 8.2 %collective-permute-start.26 = (bf16[64,1024]{1,0:T(8,128)(2,1)S(1)}, bf16[64,1024]{1,0:T(8,128)(2,1)S(1)}, u32[]{:S(2)}, u32[]{:S(2)}) collective-permute-start(bf16[64,1024]{1,0:T(8,128)(2,1)S(1)} %get-tuple-element.128.refs_0_), channel_id=1, source_target_pairs={{0,3},{1,0},{2,1},{3,2},{4,7},{5,4},{6,5},{7,6},{8,11},{9,8},{10,9... | collective-permute-start | bytes 393224 | tf_op jit(solution)/shard_map/ppermute | solution.py:241
  92.4 15.1 %collective-permute-start.21 = (f32[64,1024]{1,0:T(8,128)S(1)}, f32[64,1024]{1,0:T(8,128)S(1)}, u32[]{:S(2)}, u32[]{:S(2)}) collective-permute-start(f32[64,1024]{1,0:T(8,128)S(1)} %get-tuple-element.130), channel_id=1, source_target_pairs={{0,1},{1,2},{2,3},{3,0},{4,5},{5,6},{6,7},{7,4},{8,9},{9,10},{10,1... | collective-permute-start | bytes 786440 | tf_op jit(solution)/shard_map/ppermute | solution.py:241
  94.3 13.2 %collective-permute-start.22 = (f32[64,1024]{1,0:T(8,128)S(1)}, f32[64,1024]{1,0:T(8,128)S(1)}, u32[]{:S(2)}, u32[]{:S(2)}) collective-permute-start(f32[64,1024]{1,0:T(8,128)S(1)} %get-tuple-element.131), channel_id=1, source_target_pairs={{0,2},{1,3},{2,0},{3,1},{4,6},{5,7},{6,4},{7,5},{8,10},{9,11},{10,... | collective-permute-start | bytes 786440 | tf_op jit(solution)/shard_map/ppermute | solution.py:241
  95.4 12.0 %collective-permute-start.23 = (f32[64,1024]{1,0:T(8,128)S(1)}, f32[64,1024]{1,0:T(8,128)S(1)}, u32[]{:S(2)}, u32[]{:S(2)}) collective-permute-start(f32[64,1024]{1,0:T(8,128)S(1)} %get-tuple-element.132), channel_id=1, source_target_pairs={{0,3},{1,0},{2,1},{3,2},{4,7},{5,4},{6,5},{7,6},{8,11},{9,8},{10,9... | collective-permute-start | bytes 786440 | tf_op jit(solution)/shard_map/ppermute | solution.py:241
  109.1 8.7 %collective-permute-start.27 = (bf16[80,1024]{1,0:T(8,128)(2,1)S(1)}, bf16[80,1024]{1,0:T(8,128)(2,1)S(1)}, u32[]{:S(2)}, u32[]{:S(2)}) collective-permute-start(bf16[80,1024]{1,0:T(8,128)(2,1)S(1)} %rows.5.refs_0_), channel_id=1, source_target_pairs={{8,16},{9,17},{10,18},{11,19},{12,8},{13,9},{14,10},{15,11},{16,12... | collective-permute-start | bytes 491528 | tf_op jit(solution)/shard_map/ppermute | solution.py:241
  111.5 8.1 %collective-permute-start.28 = (bf16[80,1024]{1,0:T(8,128)(2,1)S(1)}, bf16[80,1024]{1,0:T(8,128)(2,1)S(1)}, u32[]{:S(2)}, u32[]{:S(2)}) collective-permute-start(bf16[80,1024]{1,0:T(8,128)(2,1)S(1)} %rows.5.refs_0_), channel_id=1, source_target_pairs={{8,12},{9,13},{10,14},{11,15},{12,16},{13,17},{14,18},{15,19},{16,... | collective-permute-start | bytes 491528 | tf_op jit(solution)/shard_map/ppermute | solution.py:241
  119.6 5.0 %collective-permute-start.29 = (bf16[64,1024]{1,0:T(8,128)(2,1)S(1)}, bf16[64,1024]{1,0:T(8,128)(2,1)S(1)}, u32[]{:S(2)}, u32[]{:S(2)}) collective-permute-start(bf16[64,1024]{1,0:T(8,128)(2,1)S(1)} %get-tuple-element.142.refs_0_), channel_id=1, source_target_pairs={{0,1},{1,2},{2,3},{3,0},{4,5},{5,6},{6,7},{7,4},{8,9},{9,10},{10,1... | collective-permute-start | bytes 393224 | tf_op jit(solution)/shard_map/ppermute | solution.py:241
  121.4 6.6 %collective-permute-start.30 = (bf16[64,1024]{1,0:T(8,128)(2,1)S(1)}, bf16[64,1024]{1,0:T(8,128)(2,1)S(1)}, u32[]{:S(2)}, u32[]{:S(2)}) collective-permute-start(bf16[64,1024]{1,0:T(8,128)(2,1)S(1)} %get-tuple-element.142.refs_0_), channel_id=1, source_target_pairs={{0,2},{1,3},{2,0},{3,1},{4,6},{5,7},{6,4},{7,5},{8,10},{9,11},{10,... | collective-permute-start | bytes 393224 | tf_op jit(solution)/shard_map/ppermute | solution.py:241
  122.3 7.0 %collective-permute-start.31 = (bf16[64,1024]{1,0:T(8,128)(2,1)S(1)}, bf16[64,1024]{1,0:T(8,128)(2,1)S(1)}, u32[]{:S(2)}, u32[]{:S(2)}) collective-permute-start(bf16[64,1024]{1,0:T(8,128)(2,1)S(1)} %get-tuple-element.142.refs_0_), channel_id=1, source_target_pairs={{0,3},{1,0},{2,1},{3,2},{4,7},{5,4},{6,5},{7,6},{8,11},{9,8},{10,9... | collective-permute-start | bytes 393224 | tf_op jit(solution)/shard_map/ppermute | solution.py:241

commit v3 on v2

--- a/solution.py
+++ b/solution.py
@@ -355,14 +355,15 @@
     state = anomalies
     done = []
     for colour in range(NCOL):
-        if colour == 0:
-            whole, variance, picked[2:] = joined(rows, colour, picked[2:])
-        else:
-            whole, variance, state = joined(rows, colour, state)
+        if colour < NCOL - 1:
+            coming, rows = lax.optimization_barrier((picked[colour + 1], rows))
+            parts = scattered(coming)
+        whole, variance, picked[colour + 2 :] = joined(rows, colour, picked[colour + 2 :])
         pieces = spread(whole)
+        if colour > 0:
+            pieces[-1], state = lax.optimization_barrier((pieces[-1], state))
         if colour < NCOL - 1:
-            coming, _ = lax.optimization_barrier((picked[colour + 1], whole))
-            parts = scattered(coming)
+            pieces[-1], parts = lax.optimization_barrier((pieces[-1], parts))
         done.append(transform(pieces, variance))
         if colour < NCOL - 1:
             sources = [(done[n], row_factor[colour + 1, n]) for n in range(colour + 1)]

time: 142 us -> 157 us (1.11)
  waiting for transfers between devices: 35.1 us -> 51.2 us
    ppermute x32, waiting for transfers between devices: 35.1 us -> 51.2 us  [hop(): return lax.ppermute(value, AXES, flat)]
  transfers between devices with their start and end apart: 32 -> 32, of which waited for: 20 -> 17; matrix products, arithmetic and copies ran while one was open for 0% -> 0% of each run, Pallas kernels for 30% -> 12%
where the time goes in v3:
time: 157 us; the launch traced here: 156 us
  Pallas kernels  59.1 us (38%)
  waiting for transfers between devices  51.2 us (33%)
  starting transfers between devices  43.1 us (27%)
  local copies, waits for them, and re-layouts  2.55 us (2%)
    ppermute x32, waiting for transfers between devices, hop(): return lax.ppermute(value, AXES, flat)  51.2 us
    pallas_call x17, Pallas kernels, kernel_call(): pl.pallas_call(body, out_shape=out, in_specs=[scalar if n in smem else wh...  46.8 us
    ppermute x32, starting transfers between devices, hop(): return lax.ppermute(value, AXES, flat)  43.1 us
    pallas_call x4, Pallas kernels, move_tile(): pl.pallas_call(tile_kernel, out_shape=jax.ShapeDtypeStruct(state.shape, F...  12.2 us
  transfers between devices with their start and end apart: 32, of which 17 were waited for; matrix products, arithmetic and copies ran while one was open for 0% of the time, Pallas kernels for 12%

profile of v3, /device:TPU:6, one launch (start us, length us, event | category | flops | bytes accessed | tf_op | source)
XLA Modules:
  0.0 156.3 jit_solution(5789802376718928206)
XLA Ops:
  0.1 1.6 %copy-done = f32[512,1024]{1,0:T(8,128)S(1)} copy-done((f32[512,1024]{1,0:T(8,128)S(1)}, f32[512,1024]{1,0:T(8,128)}, u32[]{:S(2)}) %copy-start) | copy-done | bytes 2097176
  1.7 0.8 copy-done.2
  2.5 1.7 %pick.4 = (bf16[64,1024]{1,0:T(8,128)(2,1)S(1)}, bf16[64,1024]{1,0:T(8,128)(2,1)S(1)}, bf16[64,1024]{1,0:T(8,128)(2,1)S(1)}, bf16[64,1024]{1,0:T(8,128)(2,1)S(1)}) custom-call(f32[512,1024]{1,0:T(8,128)S(1)} %copy-done, s32[64,256]{1,0:T(8,128)S(1)} %copy-done.2, s32[1,3]{1,0:T(1,128)S(1)} %add_bitcast_fusion.place), custom_call_target="tpu_custom_call" | custom-call | flops 268435456 | bytes 2686988 | tf_op jit(solution)/shard_map/pick/pallas_call | solution.py:25
  4.2 0.9 collective-permute-start
  5.1 2.4 %collective-permute-start.1 = (bf16[64,1024]{1,0:T(8,128)(2,1)S(1)}, bf16[64,1024]{1,0:T(8,128)(2,1)S(1)}, u32[]{:S(2)}, u32[]{:S(2)}) collective-permute-start(bf16[64,1024]{1,0:T(8,128)(2,1)S(1)} %get-tuple-element.108), channel_id=1, source_target_pairs={{0,1},{1,2},{2,3},{3,0},{4,5},{5,6},{6,7},{7,4},{8,9},{9,10},{10,1... | collective-permute-start | bytes 393224 | tf_op jit(solution)/shard_map/ppermute | solution.py:241
  7.5 0.4 collective-permute-start.2
  8.0 0.1 copy.6.levels
  8.1 1.9 %setup.1 = (f32[64,1]{1,0:T(8,128)S(1)}, f32[64,1]{1,0:T(8,128)S(1)}, f32[64,1]{1,0:T(8,128)S(1)}, f32[64,1]{1,0:T(8,128)S(1)}, f32[64,1]{1,0:T(8,128)S(1)}, /*i...) custom-call(s32[64,256]{1,0:T(8,128)S(1)} %copy-done.3, ...), custom_call_target="tpu_custom_call" | custom-call | flops 1000000 | bytes 202268 | tf_op jit(solution)/shard_map/setup/pallas_call | solution.py:25
  10.0 2.4 %pick.5 = (f32[64,1024]{1,0:T(8,128)S(1)}, f32[64,1024]{1,0:T(8,128)S(1)}, f32[64,1024]{1,0:T(8,128)S(1)}, f32[64,1024]{1,0:T(8,128)S(1)}) custom-call(f32[512,1024]{1,0:T(8,128)S(1)} %copy-done.1, s32[64,256]{1,0:T(8,128)S(1)} %copy-done.3, s32[1,3]{1,0:T(1,128)S(1)} %add_bitcast_fusion.place), custom_call_target="tpu_custom_call" | custom-call | flops 805306368 | bytes 3211276 | tf_op jit(solution)/shard_map/pick/pallas_call | solution.py:25
  12.4 0.5 collective-permute-done.1.refs_1_
  12.8 1.2 collective-permute-done.2.refs_2_
  14.0 2.6 %collective-permute-start.6 = (f32[64,1024]{1,0:T(8,128)S(1)}, f32[64,1024]{1,0:T(8,128)S(1)}, u32[]{:S(2)}, u32[]{:S(2)}) collective-permute-start(f32[64,1024]{1,0:T(8,128)S(1)} %get-tuple-element.128), channel_id=1, source_target_pairs={{0,1},{1,2},{2,3},{3,0},{4,5},{5,6},{6,7},{7,4},{8,9},{9,10},{10,1... | collective-permute-start | bytes 786440 | tf_op jit(solution)/shard_map/ppermute | solution.py:241
  16.6 5.4 %collective-permute-start.3 = (bf16[80,1024]{1,0:T(8,128)(2,1)S(1)}, bf16[80,1024]{1,0:T(8,128)(2,1)S(1)}, u32[]{:S(2)}, u32[]{:S(2)}) collective-permute-start(bf16[80,1024]{1,0:T(8,128)(2,1)S(1)} %start.1.refs_0_), channel_id=1, source_target_pairs={{252,4},{253,5},{254,6},{255,7},{0,252},{1,253},{2,254},{3,255},{4... | collective-permute-start | bytes 491528 | tf_op jit(solution)/shard_map/ppermute | solution.py:241
  22.0 1.2 collective-permute-start.7
  23.2 0.4 collective-permute-start.8
  23.6 2.4 %pick.6 = (f32[64,1024]{1,0:T(8,128)S(1)}, f32[64,1024]{1,0:T(8,128)S(1)}, f32[64,1024]{1,0:T(8,128)S(1)}, f32[64,1024]{1,0:T(8,128)S(1)}) custom-call(f32[512,1024]{1,0:T(8,128)S(1)} %copy-done.1, s32[64,256]{1,0:T(8,128)S(1)} %copy-done.3, s32[1,3]{1,0:T(1,128)S(1)} %add_bitcast_fusion.place), custom_call_target="tpu_custom_call" | custom-call | flops 805306368 | bytes 3211276 | tf_op jit(solution)/shard_map/pick/pallas_call | solution.py:25
  26.0 2.4 %pick.7 = (f32[64,1024]{1,0:T(8,128)S(1)}, f32[64,1024]{1,0:T(8,128)S(1)}, f32[64,1024]{1,0:T(8,128)S(1)}, f32[64,1024]{1,0:T(8,128)S(1)}) custom-call(f32[512,1024]{1,0:T(8,128)S(1)} %copy-done.1, s32[64,256]{1,0:T(8,128)S(1)} %copy-done.3, s32[1,3]{1,0:T(1,128)S(1)} %add_bitcast_fusion.place), custom_call_target="tpu_custom_call" | custom-call | flops 805306368 | bytes 3211276 | tf_op jit(solution)/shard_map/pick/pallas_call | solution.py:25
  28.4 1.6 %collective-permute-done.4.refs_1_ = bf16[80,1024]{1,0:T(8,128)(2,1)S(1)} collective-permute-done((bf16[80,1024]{1,0:T(8,128)(2,1)S(1)}, bf16[80,1024]{1,0:T(8,128)(2,1)S(1)}, u32[]{:S(2)}, u32[]{:S(2)}) %collective-permute-start.4) | collective-permute-done | bytes 163872 | tf_op jit(solution)/shard_map/ppermute | solution.py:241
  30.1 0.3 collective-permute-start.5
  30.4 2.5 %collective-permute-start.10 = (bf16[64,1024]{1,0:T(8,128)(2,1)S(1)}, bf16[64,1024]{1,0:T(8,128)(2,1)S(1)}, u32[]{:S(2)}, u32[]{:S(2)}) collective-permute-start(bf16[64,1024]{1,0:T(8,128)(2,1)S(1)} %get-tuple-element.126.refs_0_), channel_id=1, source_target_pairs={{0,2},{1,3},{2,0},{3,1},{4,6},{5,7},{6,4},{7,5},{8,10},{9,11},{10,... | collective-permute-start | bytes 393224 | tf_op jit(solution)/shard_map/ppermute | solution.py:241
  32.8 1.2 collective-permute-start.9
  34.0 3.5 %collective-permute-done.8.refs_3_ = f32[64,1024]{1,0:T(8,128)S(1)} collective-permute-done((f32[64,1024]{1,0:T(8,128)S(1)}, f32[64,1024]{1,0:T(8,128)S(1)}, u32[]{:S(2)}, u32[]{:S(2)}) %collective-permute-start.8) | collective-permute-done | bytes 262176 | tf_op jit(solution)/shard_map/ppermute | solution.py:241
  37.6 3.5 %collective-permute-done.5.refs_3_ = bf16[64,1024]{1,0:T(8,128)(2,1)S(1)} collective-permute-done((bf16[64,1024]{1,0:T(8,128)(2,1)S(1)}, bf16[64,1024]{1,0:T(8,128)(2,1)S(1)}, u32[]{:S(2)}, u32[]{:S(2)}) %collective-permute-start.5) | collective-permute-done | bytes 131104 | tf_op jit(solution)/shard_map/ppermute | solution.py:241
  41.0 2.1 %collective-permute-done.10.refs_2_ = bf16[64,1024]{1,0:T(8,128)(2,1)S(1)} collective-permute-done((bf16[64,1024]{1,0:T(8,128)(2,1)S(1)}, bf16[64,1024]{1,0:T(8,128)(2,1)S(1)}, u32[]{:S(2)}, u32[]{:S(2)}) %collective-permute-start.10) | collective-permute-done | bytes 131104 | tf_op jit(solution)/shard_map/ppermute | solution.py:241
  43.1 8.2 %root.4.refs_4_.transformed = bf16[256,1024]{1,0:T(8,128)(2,1)S(1)} custom-call(bf16[64,1024]{1,0:T(8,128)(2,1)S(1)} %get-tuple-element.126.refs_0_, bf16[64,1024]{1,0:T(8,128)(2,1)S(1)} %collective-permute-done.9.refs_1_, bf16[64,1024]{1,0:T(8,128)(2,1)S(1)} %collective-permute-done.10.refs_2_, bf16[64,1024]{1,0:T(8,128)(2,1)S(1)} %collective-permute-done.5.refs_3_, ...), custom_call_target="tpu_custom_call" | custom-call | flops 8000000000 | bytes 1049600 | tf_op jit(solution)/shard_map/root/pallas_call | solution.py:25
  51.3 0.6 rows.3.refs_0_
  51.9 0.3 collective-permute-start.11
  52.2 0.5 collective-permute-start.12
  52.7 1.2 collective-permute-start.15
  53.9 1.4 collective-permute-start.16
  55.3 1.1 collective-permute-done.11.refs_2_
  56.5 1.7 %collective-permute-done.12.refs_1_ = bf16[80,1024]{1,0:T(8,128)(2,1)S(1)} collective-permute-done((bf16[80,1024]{1,0:T(8,128)(2,1)S(1)}, bf16[80,1024]{1,0:T(8,128)(2,1)S(1)}, u32[]{:S(2)}, u32[]{:S(2)}) %collective-permute-start.12) | collective-permute-done | bytes 163872 | tf_op jit(solution)/shard_map/ppermute | solution.py:241
  58.3 1.3 collective-permute-start.18
  59.6 12.0 %collective-permute-done.13.refs_3_ = bf16[64,1024]{1,0:T(8,128)(2,1)S(1)} collective-permute-done((bf16[64,1024]{1,0:T(8,128)(2,1)S(1)}, bf16[64,1024]{1,0:T(8,128)(2,1)S(1)}, u32[]{:S(2)}, u32[]{:S(2)}) %collective-permute-start.13) | collective-permute-done | bytes 131104 | tf_op jit(solution)/shard_map/ppermute | solution.py:241
  71.7 0.7 collective-permute-start.17
  72.3 3.1 %tile.4.state = f32[512,1024]{1,0:T(8,128)S(1)} custom-call(f32[512,1024]{1,0:T(8,128)S(1)} %copy-done.1, bf16[256,1024]{1,0:T(8,128)(2,1)S(1)} %root.4.refs_4_.transformed, f32[1,1]{1,0:T(1,128)} %get-tuple-element.150.factor), custom_call_target="tpu_custom_call" | custom-call | flops 536870912 | bytes 4194304 | tf_op jit(solution)/shard_map/tile/pallas_call | solution.py:300
  75.4 1.6 %collective-permute-done.17.refs_1_ = bf16[64,1024]{1,0:T(8,128)(2,1)S(1)} collective-permute-done((bf16[64,1024]{1,0:T(8,128)(2,1)S(1)}, bf16[64,1024]{1,0:T(8,128)(2,1)S(1)}, u32[]{:S(2)}, u32[]{:S(2)}) %collective-permute-start.17) | collective-permute-done | bytes 131104 | tf_op jit(solution)/shard_map/ppermute | solution.py:241
  77.0 8.2 %root.5.refs_6_.transformed = bf16[256,1024]{1,0:T(8,128)(2,1)S(1)} custom-call(bf16[64,1024]{1,0:T(8,128)(2,1)S(1)} %get-tuple-element.149.refs_0_, bf16[64,1024]{1,0:T(8,128)(2,1)S(1)} %collective-permute-done.17.refs_1_, bf16[64,1024]{1,0:T(8,128)(2,1)S(1)} %collective-permute-done.18.refs_2_, bf16[64,1024]{1,0:T(8,128)(2,1)S(1)} %collective-permute-done.13.refs_3_, ...), custom_call_target="tpu_custom_call" | custom-call | flops 8000000000 | bytes 1049600 | tf_op jit(solution)/shard_map/root/pallas_call | solution.py:25
  85.2 1.2 rows.4.refs_0_
  86.5 2.0 %collective-permute-start.19 = (bf16[80,1024]{1,0:T(8,128)(2,1)S(1)}, bf16[80,1024]{1,0:T(8,128)(2,1)S(1)}, u32[]{:S(2)}, u32[]{:S(2)}) collective-permute-start(bf16[80,1024]{1,0:T(8,128)(2,1)S(1)} %rows.4.refs_0_), channel_id=1, source_target_pairs={{4,8},{5,9},{6,10},{7,11},{8,12},{9,13},{10,14},{11,15},{12,4},{13... | collective-permute-start | bytes 491528 | tf_op jit(solution)/shard_map/ppermute | solution.py:241
  88.5 1.5 collective-permute-start.22
  90.0 0.7 collective-permute-start.23
  90.6 0.5 collective-permute-start.24
  91.1 2.4 %collective-permute-done.20.refs_2_ = bf16[80,1024]{1,0:T(8,128)(2,1)S(1)} collective-permute-done((bf16[80,1024]{1,0:T(8,128)(2,1)S(1)}, bf16[80,1024]{1,0:T(8,128)(2,1)S(1)}, u32[]{:S(2)}, u32[]{:S(2)}) %collective-permute-start.20) | collective-permute-done | bytes 163872 | tf_op jit(solution)/shard_map/ppermute | solution.py:241
  93.5 3.5 %collective-permute-done.19.refs_1_ = bf16[80,1024]{1,0:T(8,128)(2,1)S(1)} collective-permute-done((bf16[80,1024]{1,0:T(8,128)(2,1)S(1)}, bf16[80,1024]{1,0:T(8,128)(2,1)S(1)}, u32[]{:S(2)}, u32[]{:S(2)}) %collective-permute-start.19) | collective-permute-done | bytes 163872 | tf_op jit(solution)/shard_map/ppermute | solution.py:241
  97.1 0.3 collective-permute-start.21
  97.4 2.0 %collective-permute-start.26 = (bf16[64,1024]{1,0:T(8,128)(2,1)S(1)}, bf16[64,1024]{1,0:T(8,128)(2,1)S(1)}, u32[]{:S(2)}, u32[]{:S(2)}) collective-permute-start(bf16[64,1024]{1,0:T(8,128)(2,1)S(1)} %get-tuple-element.166.refs_0_), channel_id=1, source_target_pairs={{0,2},{1,3},{2,0},{3,1},{4,6},{5,7},{6,4},{7,5},{8,10},{9,11},{10,... | collective-permute-start | bytes 393224 | tf_op jit(solution)/shard_map/ppermute | solution.py:241
  99.3 7.7 %collective-permute-done.21.refs_3_ = bf16[64,1024]{1,0:T(8,128)(2,1)S(1)} collective-permute-done((bf16[64,1024]{1,0:T(8,128)(2,1)S(1)}, bf16[64,1024]{1,0:T(8,128)(2,1)S(1)}, u32[]{:S(2)}, u32[]{:S(2)}) %collective-permute-start.21) | collective-permute-done | bytes 131104 | tf_op jit(solution)/shard_map/ppermute | solution.py:241
  107.0 3.4 %collective-permute-start.25 = (bf16[64,1024]{1,0:T(8,128)(2,1)S(1)}, bf16[64,1024]{1,0:T(8,128)(2,1)S(1)}, u32[]{:S(2)}, u32[]{:S(2)}) collective-permute-start(bf16[64,1024]{1,0:T(8,128)(2,1)S(1)} %get-tuple-element.166.refs_0_), channel_id=1, source_target_pairs={{0,1},{1,2},{2,3},{3,0},{4,5},{5,6},{6,7},{7,4},{8,9},{9,10},{10,1... | collective-permute-start | bytes 393224 | tf_op jit(solution)/shard_map/ppermute | solution.py:241
  110.5 3.0 %tile.5.state = f32[512,1024]{1,0:T(8,128)S(1)} custom-call(f32[512,1024]{1,0:T(8,128)S(1)} %tile.4.state, bf16[256,1024]{1,0:T(8,128)(2,1)S(1)} %root.5.refs_6_.transformed, f32[1,1]{1,0:T(1,128)} %get-tuple-element.168.factor), custom_call_target="tpu_custom_call" | custom-call | flops 536870912 | bytes 4194304 | tf_op jit(solution)/shard_map/tile/pallas_call | solution.py:300
  113.5 8.2 %root.6.refs_8_.transformed = bf16[256,1024]{1,0:T(8,128)(2,1)S(1)} custom-call(bf16[64,1024]{1,0:T(8,128)(2,1)S(1)} %get-tuple-element.166.refs_0_, bf16[64,1024]{1,0:T(8,128)(2,1)S(1)} %collective-permute-done.25.refs_1_, bf16[64,1024]{1,0:T(8,128)(2,1)S(1)} %collective-permute-done.26.refs_2_, bf16[64,1024]{1,0:T(8,128)(2,1)S(1)} %collective-permute-done.21.refs_3_, ...), custom_call_target="tpu_custom_call" | custom-call | flops 8000000000 | bytes 1049600 | tf_op jit(solution)/shard_map/root/pallas_call | solution.py:25
  121.7 1.6 %rows.5.refs_0_ = bf16[80,1024]{1,0:T(8,128)(2,1)S(1)} custom-call(f32[64,1024]{1,0:T(8,128)S(1)} %get-tuple-element.174.refs_0_, f32[64,1024]{1,0:T(8,128)S(1)} %collective-permute-done.22.refs_1_, f32[64,1024]{1,0:T(8,128)S(1)} %collective-permute-done.23.refs_2_, f32[64,1024]{1,0:T(8,128)S(1)} %collective-permute-done.24.refs_3_, ...), custom_call_target="tpu_custom_call" | custom-call | flops 201326592 | bytes 2818816 | tf_op jit(solution)/shard_map/rows/pallas_call | solution.py:25
  123.3 5.0 %collective-permute-start.28 = (bf16[80,1024]{1,0:T(8,128)(2,1)S(1)}, bf16[80,1024]{1,0:T(8,128)(2,1)S(1)}, u32[]{:S(2)}, u32[]{:S(2)}) collective-permute-start(bf16[80,1024]{1,0:T(8,128)(2,1)S(1)} %rows.5.refs_0_), channel_id=1, source_target_pairs={{8,16},{9,17},{10,18},{11,19},{12,8},{13,9},{14,10},{15,11},{16,12... | collective-permute-start | bytes 491528 | tf_op jit(solution)/shard_map/ppermute | solution.py:241
  128.3 1.4 collective-permute-start.27
  129.7 3.2 %collective-permute-done.28.refs_2_ = bf16[80,1024]{1,0:T(8,128)(2,1)S(1)} collective-permute-done((bf16[80,1024]{1,0:T(8,128)(2,1)S(1)}, bf16[80,1024]{1,0:T(8,128)(2,1)S(1)}, u32[]{:S(2)}, u32[]{:S(2)}) %collective-permute-start.28) | collective-permute-done | bytes 163872 | tf_op jit(solution)/shard_map/ppermute | solution.py:241
  132.9 3.4 %collective-permute-done.27.refs_1_ = bf16[80,1024]{1,0:T(8,128)(2,1)S(1)} collective-permute-done((bf16[80,1024]{1,0:T(8,128)(2,1)S(1)}, bf16[80,1024]{1,0:T(8,128)(2,1)S(1)}, u32[]{:S(2)}, u32[]{:S(2)}) %collective-permute-start.27) | collective-permute-done | bytes 163872 | tf_op jit(solution)/shard_map/ppermute | solution.py:241
  136.4 0.4 collective-permute-start.29
  136.8 2.0 %collective-permute-start.31 = (bf16[64,1024]{1,0:T(8,128)(2,1)S(1)}, bf16[64,1024]{1,0:T(8,128)(2,1)S(1)}, u32[]{:S(2)}, u32[]{:S(2)}) collective-permute-start(bf16[64,1024]{1,0:T(8,128)(2,1)S(1)} %get-tuple-element.184.refs_0_), channel_id=1, source_target_pairs={{0,2},{1,3},{2,0},{3,1},{4,6},{5,7},{6,4},{7,5},{8,10},{9,11},{10,... | collective-permute-start | bytes 393224 | tf_op jit(solution)/shard_map/ppermute | solution.py:241
  138.8 0.9 collective-permute-start.30
  139.8 3.1 %tile.6.state = f32[512,1024]{1,0:T(8,128)S(1)} custom-call(f32[512,1024]{1,0:T(8,128)S(1)} %tile.5.state, bf16[256,1024]{1,0:T(8,128)(2,1)S(1)} %root.6.refs_8_.transformed, f32[1,1]{1,0:T(1,128)} %get-tuple-element.186.factor), custom_call_target="tpu_custom_call" | custom-call | flops 536870912 | bytes 4194304 | tf_op jit(solution)/shard_map/tile/pallas_call | solution.py:300
  142.8 1.3 collective-permute-done.29.refs_3_
  144.1 0.9 collective-permute-done.30.refs_1_
  145.0 8.2 %root.7.transformed = bf16[256,1024]{1,0:T(8,128)(2,1)S(1)} custom-call(bf16[64,1024]{1,0:T(8,128)(2,1)S(1)} %get-tuple-element.184.refs_0_, bf16[64,1024]{1,0:T(8,128)(2,1)S(1)} %collective-permute-done.30.refs_1_, bf16[64,1024]{1,0:T(8,128)(2,1)S(1)} %collective-permute-done.31.refs_2_, bf16[64,1024]{1,0:T(8,128)(2,1)S(1)} %collective-permute-done.29.refs_3_, ...), custom_call_target="tpu_custom_call" | custom-call | flops 8000000000 | bytes 1049600 | tf_op jit(solution)/shard_map/root/pallas_call | solution.py:25
  153.1 3.1 %tile.7 = f32[512,1024]{1,0:T(8,128)} custom-call(f32[512,1024]{1,0:T(8,128)S(1)} %tile.6.state, bf16[256,1024]{1,0:T(8,128)(2,1)S(1)} %root.7.transformed, f32[1,1]{1,0:T(1,128)} %get-tuple-element.190.factor), custom_call_target="tpu_custom_call" | custom-call | flops 536870912 | bytes 4194304 | tf_op jit(solution)/shard_map/tile/pallas_call | solution.py:300
  (36 shorter events, 0.5 us)
Async XLA Ops:
  0.0 8.0 %copy-start.5 = (s32[64,3,4]{0,2,1:T(4,128)S(1)}, s32[64,3,4]{0,2,1:T(4,128)}, u32[]{:S(2)}) copy-start(s32[64,3,4]{0,2,1:T(4,128)} %param.7) | copy-start | bytes 9220
  0.0 8.1 %copy-start.4 = (f32[1,256]{1,0:T(1,128)S(1)}, f32[1,256]{1,0:T(1,128)}, u32[]{:S(2)}) copy-start(f32[1,256]{1,0:T(1,128)} %own.1) | copy-start | bytes 3076
  0.1 1.6 %copy-start = (f32[512,1024]{1,0:T(8,128)S(1)}, f32[512,1024]{1,0:T(8,128)}, u32[]{:S(2)}) copy-start(f32[512,1024]{1,0:T(8,128)} %state.9) | copy-start | bytes 6291460
  1.7 0.8 copy-start.2
  2.5 5.6 %copy-start.3 = (s32[64,256]{1,0:T(8,128)S(1)}, s32[64,256]{1,0:T(8,128)}, u32[]{:S(2)}) copy-start(s32[64,256]{1,0:T(8,128)} %obs.9) | copy-start | bytes 196612
  2.5 7.5 %copy-start.1 = (f32[512,1024]{1,0:T(8,128)S(1)}, f32[512,1024]{1,0:T(8,128)}, u32[]{:S(2)}) copy-start(f32[512,1024]{1,0:T(8,128)} %state.9) | copy-start | bytes 6291460
  4.2 8.2 %collective-permute-start = (bf16[64,1024]{1,0:T(8,128)(2,1)S(1)}, bf16[64,1024]{1,0:T(8,128)(2,1)S(1)}, u32[]{:S(2)}, u32[]{:S(2)}) collective-permute-start(bf16[64,1024]{1,0:T(8,128)(2,1)S(1)} %get-tuple-element.98), channel_id=1, source_target_pairs={{0,3},{1,0},{2,1},{3,2},{4,7},{5,4},{6,5},{7,6},{8,11},{9,8},{10,9... | collective-permute-start | bytes 393224 | tf_op jit(solution)/shard_map/ppermute | solution.py:241
  5.1 7.7 %collective-permute-start.1 = (bf16[64,1024]{1,0:T(8,128)(2,1)S(1)}, bf16[64,1024]{1,0:T(8,128)(2,1)S(1)}, u32[]{:S(2)}, u32[]{:S(2)}) collective-permute-start(bf16[64,1024]{1,0:T(8,128)(2,1)S(1)} %get-tuple-element.108), channel_id=1, source_target_pairs={{0,1},{1,2},{2,3},{3,0},{4,5},{5,6},{6,7},{7,4},{8,9},{9,10},{10,1... | collective-permute-start | bytes 393224 | tf_op jit(solution)/shard_map/ppermute | solution.py:241
  7.5 6.5 %collective-permute-start.2 = (bf16[64,1024]{1,0:T(8,128)(2,1)S(1)}, bf16[64,1024]{1,0:T(8,128)(2,1)S(1)}, u32[]{:S(2)}, u32[]{:S(2)}) collective-permute-start(bf16[64,1024]{1,0:T(8,128)(2,1)S(1)} %get-tuple-element.109), channel_id=1, source_target_pairs={{0,2},{1,3},{2,0},{3,1},{4,6},{5,7},{6,4},{7,5},{8,10},{9,11},{10,... | collective-permute-start | bytes 393224 | tf_op jit(solution)/shard_map/ppermute | solution.py:241
  14.0 18.8 %collective-permute-start.6 = (f32[64,1024]{1,0:T(8,128)S(1)}, f32[64,1024]{1,0:T(8,128)S(1)}, u32[]{:S(2)}, u32[]{:S(2)}) collective-permute-start(f32[64,1024]{1,0:T(8,128)S(1)} %get-tuple-element.128), channel_id=1, source_target_pairs={{0,1},{1,2},{2,3},{3,0},{4,5},{5,6},{6,7},{7,4},{8,9},{9,10},{10,1... | collective-permute-start | bytes 786440 | tf_op jit(solution)/shard_map/ppermute | solution.py:241
  16.6 11.8 %collective-permute-start.3 = (bf16[80,1024]{1,0:T(8,128)(2,1)S(1)}, bf16[80,1024]{1,0:T(8,128)(2,1)S(1)}, u32[]{:S(2)}, u32[]{:S(2)}) collective-permute-start(bf16[80,1024]{1,0:T(8,128)(2,1)S(1)} %start.1.refs_0_), channel_id=1, source_target_pairs={{252,4},{253,5},{254,6},{255,7},{0,252},{1,253},{2,254},{3,255},{4... | collective-permute-start | bytes 491528 | tf_op jit(solution)/shard_map/ppermute | solution.py:241
  22.0 8.1 %collective-permute-start.4 = (bf16[80,1024]{1,0:T(8,128)(2,1)S(1)}, bf16[80,1024]{1,0:T(8,128)(2,1)S(1)}, u32[]{:S(2)}, u32[]{:S(2)}) collective-permute-start(bf16[80,1024]{1,0:T(8,128)(2,1)S(1)} %start.1.refs_0_), channel_id=1, source_target_pairs={{252,0},{253,1},{254,2},{255,3},{0,4},{1,5},{2,6},{3,7},{4,252},{5... | collective-permute-start | bytes 491528 | tf_op jit(solution)/shard_map/ppermute | solution.py:241
  22.0 12.1 %collective-permute-start.7 = (f32[64,1024]{1,0:T(8,128)S(1)}, f32[64,1024]{1,0:T(8,128)S(1)}, u32[]{:S(2)}, u32[]{:S(2)}) collective-permute-start(f32[64,1024]{1,0:T(8,128)S(1)} %get-tuple-element.129), channel_id=1, source_target_pairs={{0,2},{1,3},{2,0},{3,1},{4,6},{5,7},{6,4},{7,5},{8,10},{9,11},{10,... | collective-permute-start | bytes 786440 | tf_op jit(solution)/shard_map/ppermute | solution.py:241
  23.2 14.3 %collective-permute-start.8 = (f32[64,1024]{1,0:T(8,128)S(1)}, f32[64,1024]{1,0:T(8,128)S(1)}, u32[]{:S(2)}, u32[]{:S(2)}) collective-permute-start(f32[64,1024]{1,0:T(8,128)S(1)} %get-tuple-element.130), channel_id=1, source_target_pairs={{0,3},{1,0},{2,1},{3,2},{4,7},{5,4},{6,5},{7,6},{8,11},{9,8},{10,9... | collective-permute-start | bytes 786440 | tf_op jit(solution)/shard_map/ppermute | solution.py:241
  30.1 10.9 %collective-permute-start.5 = (bf16[64,1024]{1,0:T(8,128)(2,1)S(1)}, bf16[64,1024]{1,0:T(8,128)(2,1)S(1)}, u32[]{:S(2)}, u32[]{:S(2)}) collective-permute-start(bf16[64,1024]{1,0:T(8,128)(2,1)S(1)} %get-tuple-element.126.refs_0_), channel_id=1, source_target_pairs={{0,3},{1,0},{2,1},{3,2},{4,7},{5,4},{6,5},{7,6},{8,11},{9,8},{10,9... | collective-permute-start | bytes 393224 | tf_op jit(solution)/shard_map/ppermute | solution.py:241
  30.4 12.8 %collective-permute-start.10 = (bf16[64,1024]{1,0:T(8,128)(2,1)S(1)}, bf16[64,1024]{1,0:T(8,128)(2,1)S(1)}, u32[]{:S(2)}, u32[]{:S(2)}) collective-permute-start(bf16[64,1024]{1,0:T(8,128)(2,1)S(1)} %get-tuple-element.126.refs_0_), channel_id=1, source_target_pairs={{0,2},{1,3},{2,0},{3,1},{4,6},{5,7},{6,4},{7,5},{8,10},{9,11},{10,... | collective-permute-start | bytes 393224 | tf_op jit(solution)/shard_map/ppermute | solution.py:241
  32.8 10.3 %collective-permute-start.9 = (bf16[64,1024]{1,0:T(8,128)(2,1)S(1)}, bf16[64,1024]{1,0:T(8,128)(2,1)S(1)}, u32[]{:S(2)}, u32[]{:S(2)}) collective-permute-start(bf16[64,1024]{1,0:T(8,128)(2,1)S(1)} %get-tuple-element.126.refs_0_), channel_id=1, source_target_pairs={{0,1},{1,2},{2,3},{3,0},{4,5},{5,6},{6,7},{7,4},{8,9},{9,10},{10,1... | collective-permute-start | bytes 393224 | tf_op jit(solution)/shard_map/ppermute | solution.py:241
  51.9 4.6 %collective-permute-start.11 = (bf16[80,1024]{1,0:T(8,128)(2,1)S(1)}, bf16[80,1024]{1,0:T(8,128)(2,1)S(1)}, u32[]{:S(2)}, u32[]{:S(2)}) collective-permute-start(bf16[80,1024]{1,0:T(8,128)(2,1)S(1)} %rows.3.refs_0_), channel_id=1, source_target_pairs={{0,8},{1,9},{2,10},{3,11},{4,0},{5,1},{6,2},{7,3},{8,4},{9,5},{10,... | collective-permute-start | bytes 491528 | tf_op jit(solution)/shard_map/ppermute | solution.py:241
  52.2 6.0 %collective-permute-start.12 = (bf16[80,1024]{1,0:T(8,128)(2,1)S(1)}, bf16[80,1024]{1,0:T(8,128)(2,1)S(1)}, u32[]{:S(2)}, u32[]{:S(2)}) collective-permute-start(bf16[80,1024]{1,0:T(8,128)(2,1)S(1)} %rows.3.refs_0_), channel_id=1, source_target_pairs={{0,4},{1,5},{2,6},{3,7},{4,8},{5,9},{6,10},{7,11},{8,0},{9,1},{10,... | collective-permute-start | bytes 491528 | tf_op jit(solution)/shard_map/ppermute | solution.py:241
  52.7 22.7 %collective-permute-start.14 = (f32[64,1024]{1,0:T(8,128)S(1)}, f32[64,1024]{1,0:T(8,128)S(1)}, u32[]{:S(2)}, u32[]{:S(2)}) collective-permute-start(f32[64,1024]{1,0:T(8,128)S(1)} %get-tuple-element.153), channel_id=1, source_target_pairs={{0,1},{1,2},{2,3},{3,0},{4,5},{5,6},{6,7},{7,4},{8,9},{9,10},{10,1... | collective-permute-start | bytes 786440 | tf_op jit(solution)/shard_map/ppermute | solution.py:241
  52.7 22.7 %collective-permute-start.15 = (f32[64,1024]{1,0:T(8,128)S(1)}, f32[64,1024]{1,0:T(8,128)S(1)}, u32[]{:S(2)}, u32[]{:S(2)}) collective-permute-start(f32[64,1024]{1,0:T(8,128)S(1)} %get-tuple-element.154), channel_id=1, source_target_pairs={{0,2},{1,3},{2,0},{3,1},{4,6},{5,7},{6,4},{7,5},{8,10},{9,11},{10,... | collective-permute-start | bytes 786440 | tf_op jit(solution)/shard_map/ppermute | solution.py:241
  53.9 21.5 %collective-permute-start.16 = (f32[64,1024]{1,0:T(8,128)S(1)}, f32[64,1024]{1,0:T(8,128)S(1)}, u32[]{:S(2)}, u32[]{:S(2)}) collective-permute-start(f32[64,1024]{1,0:T(8,128)S(1)} %get-tuple-element.155), channel_id=1, source_target_pairs={{0,3},{1,0},{2,1},{3,2},{4,7},{5,4},{6,5},{7,6},{8,11},{9,8},{10,9... | collective-permute-start | bytes 786440 | tf_op jit(solution)/shard_map/ppermute | solution.py:241
  58.2 13.5 %collective-permute-start.13 = (bf16[64,1024]{1,0:T(8,128)(2,1)S(1)}, bf16[64,1024]{1,0:T(8,128)(2,1)S(1)}, u32[]{:S(2)}, u32[]{:S(2)}) collective-permute-start(bf16[64,1024]{1,0:T(8,128)(2,1)S(1)} %get-tuple-element.149.refs_0_), channel_id=1, source_target_pairs={{0,3},{1,0},{2,1},{3,2},{4,7},{5,4},{6,5},{7,6},{8,11},{9,8},{10,9... | collective-permute-start | bytes 393224 | tf_op jit(solution)/shard_map/ppermute | solution.py:241
  58.3 17.1 %collective-permute-start.18 = (bf16[64,1024]{1,0:T(8,128)(2,1)S(1)}, bf16[64,1024]{1,0:T(8,128)(2,1)S(1)}, u32[]{:S(2)}, u32[]{:S(2)}) collective-permute-start(bf16[64,1024]{1,0:T(8,128)(2,1)S(1)} %get-tuple-element.149.refs_0_), channel_id=1, source_target_pairs={{0,2},{1,3},{2,0},{3,1},{4,6},{5,7},{6,4},{7,5},{8,10},{9,11},{10,... | collective-permute-start | bytes 393224 | tf_op jit(solution)/shard_map/ppermute | solution.py:241
  71.7 5.4 %collective-permute-start.17 = (bf16[64,1024]{1,0:T(8,128)(2,1)S(1)}, bf16[64,1024]{1,0:T(8,128)(2,1)S(1)}, u32[]{:S(2)}, u32[]{:S(2)}) collective-permute-start(bf16[64,1024]{1,0:T(8,128)(2,1)S(1)} %get-tuple-element.149.refs_0_), channel_id=1, source_target_pairs={{0,1},{1,2},{2,3},{3,0},{4,5},{5,6},{6,7},{7,4},{8,9},{9,10},{10,1... | collective-permute-start | bytes 393224 | tf_op jit(solution)/shard_map/ppermute | solution.py:241
  86.4 7.2 %collective-permute-start.20 = (bf16[80,1024]{1,0:T(8,128)(2,1)S(1)}, bf16[80,1024]{1,0:T(8,128)(2,1)S(1)}, u32[]{:S(2)}, u32[]{:S(2)}) collective-permute-start(bf16[80,1024]{1,0:T(8,128)(2,1)S(1)} %rows.4.refs_0_), channel_id=1, source_target_pairs={{4,12},{5,13},{6,14},{7,15},{8,4},{9,5},{10,6},{11,7},{12,8},{13,9... | collective-permute-start | bytes 491528 | tf_op jit(solution)/shard_map/ppermute | solution.py:241
  86.5 10.6 %collective-permute-start.19 = (bf16[80,1024]{1,0:T(8,128)(2,1)S(1)}, bf16[80,1024]{1,0:T(8,128)(2,1)S(1)}, u32[]{:S(2)}, u32[]{:S(2)}) collective-permute-start(bf16[80,1024]{1,0:T(8,128)(2,1)S(1)} %rows.4.refs_0_), channel_id=1, source_target_pairs={{4,8},{5,9},{6,10},{7,11},{8,12},{9,13},{10,14},{11,15},{12,4},{13... | collective-permute-start | bytes 491528 | tf_op jit(solution)/shard_map/ppermute | solution.py:241
  88.5 25.0 %collective-permute-start.22 = (f32[64,1024]{1,0:T(8,128)S(1)}, f32[64,1024]{1,0:T(8,128)S(1)}, u32[]{:S(2)}, u32[]{:S(2)}) collective-permute-start(f32[64,1024]{1,0:T(8,128)S(1)} %get-tuple-element.171), channel_id=1, source_target_pairs={{0,1},{1,2},{2,3},{3,0},{4,5},{5,6},{6,7},{7,4},{8,9},{9,10},{10,1... | collective-permute-start | bytes 786440 | tf_op jit(solution)/shard_map/ppermute | solution.py:241
  90.0 23.5 %collective-permute-start.23 = (f32[64,1024]{1,0:T(8,128)S(1)}, f32[64,1024]{1,0:T(8,128)S(1)}, u32[]{:S(2)}, u32[]{:S(2)}) collective-permute-start(f32[64,1024]{1,0:T(8,128)S(1)} %get-tuple-element.172), channel_id=1, source_target_pairs={{0,2},{1,3},{2,0},{3,1},{4,6},{5,7},{6,4},{7,5},{8,10},{9,11},{10,... | collective-permute-start | bytes 786440 | tf_op jit(solution)/shard_map/ppermute | solution.py:241
  90.6 22.8 %collective-permute-start.24 = (f32[64,1024]{1,0:T(8,128)S(1)}, f32[64,1024]{1,0:T(8,128)S(1)}, u32[]{:S(2)}, u32[]{:S(2)}) collective-permute-start(f32[64,1024]{1,0:T(8,128)S(1)} %get-tuple-element.173), channel_id=1, source_target_pairs={{0,3},{1,0},{2,1},{3,2},{4,7},{5,4},{6,5},{7,6},{8,11},{9,8},{10,9... | collective-permute-start | bytes 786440 | tf_op jit(solution)/shard_map/ppermute | solution.py:241
  97.1 10.0 %collective-permute-start.21 = (bf16[64,1024]{1,0:T(8,128)(2,1)S(1)}, bf16[64,1024]{1,0:T(8,128)(2,1)S(1)}, u32[]{:S(2)}, u32[]{:S(2)}) collective-permute-start(bf16[64,1024]{1,0:T(8,128)(2,1)S(1)} %get-tuple-element.166.refs_0_), channel_id=1, source_target_pairs={{0,3},{1,0},{2,1},{3,2},{4,7},{5,4},{6,5},{7,6},{8,11},{9,8},{10,9... | collective-permute-start | bytes 393224 | tf_op jit(solution)/shard_map/ppermute | solution.py:241
  97.4 16.1 %collective-permute-start.26 = (bf16[64,1024]{1,0:T(8,128)(2,1)S(1)}, bf16[64,1024]{1,0:T(8,128)(2,1)S(1)}, u32[]{:S(2)}, u32[]{:S(2)}) collective-permute-start(bf16[64,1024]{1,0:T(8,128)(2,1)S(1)} %get-tuple-element.166.refs_0_), channel_id=1, source_target_pairs={{0,2},{1,3},{2,0},{3,1},{4,6},{5,7},{6,4},{7,5},{8,10},{9,11},{10,... | collective-permute-start | bytes 393224 | tf_op jit(solution)/shard_map/ppermute | solution.py:241
  107.0 6.5 %collective-permute-start.25 = (bf16[64,1024]{1,0:T(8,128)(2,1)S(1)}, bf16[64,1024]{1,0:T(8,128)(2,1)S(1)}, u32[]{:S(2)}, u32[]{:S(2)}) collective-permute-start(bf16[64,1024]{1,0:T(8,128)(2,1)S(1)} %get-tuple-element.166.refs_0_), channel_id=1, source_target_pairs={{0,1},{1,2},{2,3},{3,0},{4,5},{5,6},{6,7},{7,4},{8,9},{9,10},{10,1... | collective-permute-start | bytes 393224 | tf_op jit(solution)/shard_map/ppermute | solution.py:241
  123.3 9.7 %collective-permute-start.28 = (bf16[80,1024]{1,0:T(8,128)(2,1)S(1)}, bf16[80,1024]{1,0:T(8,128)(2,1)S(1)}, u32[]{:S(2)}, u32[]{:S(2)}) collective-permute-start(bf16[80,1024]{1,0:T(8,128)(2,1)S(1)} %rows.5.refs_0_), channel_id=1, source_target_pairs={{8,16},{9,17},{10,18},{11,19},{12,8},{13,9},{14,10},{15,11},{16,12... | collective-permute-start | bytes 491528 | tf_op jit(solution)/shard_map/ppermute | solution.py:241
  128.3 8.1 %collective-permute-start.27 = (bf16[80,1024]{1,0:T(8,128)(2,1)S(1)}, bf16[80,1024]{1,0:T(8,128)(2,1)S(1)}, u32[]{:S(2)}, u32[]{:S(2)}) collective-permute-start(bf16[80,1024]{1,0:T(8,128)(2,1)S(1)} %rows.5.refs_0_), channel_id=1, source_target_pairs={{8,12},{9,13},{10,14},{11,15},{12,16},{13,17},{14,18},{15,19},{16,... | collective-permute-start | bytes 491528 | tf_op jit(solution)/shard_map/ppermute | solution.py:241
  136.4 7.7 %collective-permute-start.29 = (bf16[64,1024]{1,0:T(8,128)(2,1)S(1)}, bf16[64,1024]{1,0:T(8,128)(2,1)S(1)}, u32[]{:S(2)}, u32[]{:S(2)}) collective-permute-start(bf16[64,1024]{1,0:T(8,128)(2,1)S(1)} %get-tuple-element.184.refs_0_), channel_id=1, source_target_pairs={{0,3},{1,0},{2,1},{3,2},{4,7},{5,4},{6,5},{7,6},{8,11},{9,8},{10,9... | collective-permute-start | bytes 393224 | tf_op jit(solution)/shard_map/ppermute | solution.py:241
  136.8 7.3 %collective-permute-start.31 = (bf16[64,1024]{1,0:T(8,128)(2,1)S(1)}, bf16[64,1024]{1,0:T(8,128)(2,1)S(1)}, u32[]{:S(2)}, u32[]{:S(2)}) collective-permute-start(bf16[64,1024]{1,0:T(8,128)(2,1)S(1)} %get-tuple-element.184.refs_0_), channel_id=1, source_target_pairs={{0,2},{1,3},{2,0},{3,1},{4,6},{5,7},{6,4},{7,5},{8,10},{9,11},{10,... | collective-permute-start | bytes 393224 | tf_op jit(solution)/shard_map/ppermute | solution.py:241
  138.8 6.2 %collective-permute-start.30 = (bf16[64,1024]{1,0:T(8,128)(2,1)S(1)}, bf16[64,1024]{1,0:T(8,128)(2,1)S(1)}, u32[]{:S(2)}, u32[]{:S(2)}) collective-permute-start(bf16[64,1024]{1,0:T(8,128)(2,1)S(1)} %get-tuple-element.184.refs_0_), channel_id=1, source_target_pairs={{0,1},{1,2},{2,3},{3,0},{4,5},{5,6},{6,7},{7,4},{8,9},{9,10},{10,1... | collective-permute-start | bytes 393224 | tf_op jit(solution)/shard_map/ppermute | solution.py:241

commit v4 on v2

--- a/solution.py
+++ b/solution.py
@@ -71,7 +71,8 @@
     columns, size = obs.shape
     share = size // tiles
     col, tile = place[0, 0], place[0, 1]
-    band = state.shape[1] // tiles
+    bands = tiles if scratch.dtype == F32 else 1
+    band = state.shape[1] // bands
     for n, colour in enumerate(colours):
         slot, active, batch = standing(col, colour, columns)
         first = jnp.where(active, (slot * tiles + tile) * tile_rows, -(1 << 20))
@@ -95,7 +96,7 @@
             scratch[:, lanes] = picked.astype(scratch.dtype)
             return 0
 
-        lax.fori_loop(0, tiles, pick_band, 0)
+        lax.fori_loop(0, bands, pick_band, 0)
         for step, out in enumerate(outs):
             start = pl.multiple_of(lax.rem(tile + step, tiles) * share, share)
             out[n * share : (n + 1) * share, :] = scratch[pl.ds(start, share), :]
@@ -355,14 +356,19 @@
     state = anomalies
     done = []
     for colour in range(NCOL):
+        ahead = picked[2:] if colour == 0 else [state]
+        if colour < NCOL - 1:
+            coming, rows = lax.optimization_barrier((picked[colour + 1], rows))
+            ahead = [*ahead, along_gy(coming[1], 1)]
+        whole, variance, ahead = joined(rows, colour, ahead)
         if colour == 0:
-            whole, variance, picked[2:] = joined(rows, colour, picked[2:])
+            picked[2:] = ahead[:2]
         else:
-            whole, variance, state = joined(rows, colour, state)
+            state = ahead[0]
         pieces = spread(whole)
         if colour < NCOL - 1:
-            coming, _ = lax.optimization_barrier((picked[colour + 1], whole))
-            parts = scattered(coming)
+            late, _ = lax.optimization_barrier((coming, whole))
+            parts = [coming[0], ahead[-1], *[along_gy(late[n], n) for n in (2, 3)]]
         done.append(transform(pieces, variance))
         if colour < NCOL - 1:
             sources = [(done[n], row_factor[colour + 1, n]) for n in range(colour + 1)]

time: 142 us -> 146 us (1.028)
  waiting for transfers between devices: 35.1 us -> 39.2 us
  starting transfers between devices: 43.6 us -> 45.2 us
    ppermute x32, waiting for transfers between devices: 35.1 us -> 39.2 us  [hop(): return lax.ppermute(value, AXES, flat)]
    ppermute x32, starting transfers between devices: 43.6 us -> 45.2 us  [hop(): return lax.ppermute(value, AXES, flat)]
  transfers between devices with their start and end apart: 32 -> 32, of which waited for: 20 -> 19; matrix products, arithmetic and copies ran while one was open for 0% -> 0% of each run, Pallas kernels for 30% -> 29%
where the time goes in v4:
time: 146 us
  Pallas kernels  58.5 us (40%)
  starting transfers between devices  45.2 us (31%)
  waiting for transfers between devices  39.2 us (27%)
  local copies, waits for them, and re-layouts  2.55 us (2%)
    pallas_call x17, Pallas kernels, kernel_call(): pl.pallas_call(body, out_shape=out, in_specs=[scalar if n in smem else wh...  46.3 us
    ppermute x32, starting transfers between devices, hop(): return lax.ppermute(value, AXES, flat)  45.2 us
    ppermute x32, waiting for transfers between devices, hop(): return lax.ppermute(value, AXES, flat)  39.2 us
    pallas_call x4, Pallas kernels, move_tile(): pl.pallas_call(tile_kernel, out_shape=jax.ShapeDtypeStruct(state.shape, F...  12.2 us
  transfers between devices with their start and end apart: 32, of which 19 were waited for; matrix products, arithmetic and copies ran while one was open for 0% of the time, Pallas kernels for 29%

profile of v4, /device:TPU:6, one launch (start us, length us, event | category | flops | bytes accessed | tf_op | source)
XLA Modules:
  0.0 145.8 jit_solution(6255130848115346712)
XLA Ops:
  0.1 1.6 %copy-done = f32[512,1024]{1,0:T(8,128)S(1)} copy-done((f32[512,1024]{1,0:T(8,128)S(1)}, f32[512,1024]{1,0:T(8,128)}, u32[]{:S(2)}) %copy-start) | copy-done | bytes 2097176
  1.7 0.8 copy-done.2
  2.5 1.1 pick.4
  3.6 0.9 collective-permute-start
  4.5 2.4 %collective-permute-start.1 = (bf16[64,1024]{1,0:T(8,128)(2,1)S(1)}, bf16[64,1024]{1,0:T(8,128)(2,1)S(1)}, u32[]{:S(2)}, u32[]{:S(2)}) collective-permute-start(bf16[64,1024]{1,0:T(8,128)(2,1)S(1)} %get-tuple-element.97), channel_id=1, source_target_pairs={{0,1},{1,2},{2,3},{3,0},{4,5},{5,6},{6,7},{7,4},{8,9},{9,10},{10,1... | collective-permute-start | bytes 393224 | tf_op jit(solution)/shard_map/ppermute | solution.py:242
  6.9 0.5 collective-permute-start.2
  7.4 0.1 copy.6.levels
  7.5 1.9 %setup.1 = (f32[64,1]{1,0:T(8,128)S(1)}, f32[64,1]{1,0:T(8,128)S(1)}, f32[64,1]{1,0:T(8,128)S(1)}, f32[64,1]{1,0:T(8,128)S(1)}, f32[64,1]{1,0:T(8,128)S(1)}, /*i...) custom-call(s32[64,256]{1,0:T(8,128)S(1)} %copy-done.3, ...), custom_call_target="tpu_custom_call" | custom-call | flops 1000000 | bytes 202268 | tf_op jit(solution)/shard_map/setup/pallas_call | solution.py:25
  9.4 2.4 %pick.5 = (f32[64,1024]{1,0:T(8,128)S(1)}, f32[64,1024]{1,0:T(8,128)S(1)}, f32[64,1024]{1,0:T(8,128)S(1)}, f32[64,1024]{1,0:T(8,128)S(1)}) custom-call(f32[512,1024]{1,0:T(8,128)S(1)} %copy-done.1, s32[64,256]{1,0:T(8,128)S(1)} %copy-done.3, s32[1,3]{1,0:T(1,128)S(1)} %add_bitcast_fusion.place), custom_call_target="tpu_custom_call" | custom-call | flops 805306368 | bytes 3211276 | tf_op jit(solution)/shard_map/pick/pallas_call | solution.py:25
  11.8 0.5 collective-permute-done.1.refs_1_
  12.2 1.2 collective-permute-done.2.refs_2_
  13.4 2.6 %collective-permute-start.4 = (f32[64,1024]{1,0:T(8,128)S(1)}, f32[64,1024]{1,0:T(8,128)S(1)}, u32[]{:S(2)}, u32[]{:S(2)}) collective-permute-start(f32[64,1024]{1,0:T(8,128)S(1)} %get-tuple-element.110), channel_id=1, source_target_pairs={{0,1},{1,2},{2,3},{3,0},{4,5},{5,6},{6,7},{7,4},{8,9},{9,10},{10,1... | collective-permute-start | bytes 786440 | tf_op jit(solution)/shard_map/ppermute | solution.py:242
  16.0 5.4 %collective-permute-start.3 = (bf16[80,1024]{1,0:T(8,128)(2,1)S(1)}, bf16[80,1024]{1,0:T(8,128)(2,1)S(1)}, u32[]{:S(2)}, u32[]{:S(2)}) collective-permute-start(bf16[80,1024]{1,0:T(8,128)(2,1)S(1)} %start.1.refs_0_), channel_id=1, source_target_pairs={{252,4},{253,5},{254,6},{255,7},{0,252},{1,253},{2,254},{3,255},{4... | collective-permute-start | bytes 491528 | tf_op jit(solution)/shard_map/ppermute | solution.py:242
  21.4 2.4 %pick.6 = (f32[64,1024]{1,0:T(8,128)S(1)}, f32[64,1024]{1,0:T(8,128)S(1)}, f32[64,1024]{1,0:T(8,128)S(1)}, f32[64,1024]{1,0:T(8,128)S(1)}) custom-call(f32[512,1024]{1,0:T(8,128)S(1)} %copy-done.1, s32[64,256]{1,0:T(8,128)S(1)} %copy-done.3, s32[1,3]{1,0:T(1,128)S(1)} %add_bitcast_fusion.place), custom_call_target="tpu_custom_call" | custom-call | flops 805306368 | bytes 3211276 | tf_op jit(solution)/shard_map/pick/pallas_call | solution.py:25
  23.8 2.4 %pick.7 = (f32[64,1024]{1,0:T(8,128)S(1)}, f32[64,1024]{1,0:T(8,128)S(1)}, f32[64,1024]{1,0:T(8,128)S(1)}, f32[64,1024]{1,0:T(8,128)S(1)}) custom-call(f32[512,1024]{1,0:T(8,128)S(1)} %copy-done.1, s32[64,256]{1,0:T(8,128)S(1)} %copy-done.3, s32[1,3]{1,0:T(1,128)S(1)} %add_bitcast_fusion.place), custom_call_target="tpu_custom_call" | custom-call | flops 805306368 | bytes 3211276 | tf_op jit(solution)/shard_map/pick/pallas_call | solution.py:25
  26.2 3.3 %collective-permute-done.5.refs_1_ = bf16[80,1024]{1,0:T(8,128)(2,1)S(1)} collective-permute-done((bf16[80,1024]{1,0:T(8,128)(2,1)S(1)}, bf16[80,1024]{1,0:T(8,128)(2,1)S(1)}, u32[]{:S(2)}, u32[]{:S(2)}) %collective-permute-start.5) | collective-permute-done | bytes 163872 | tf_op jit(solution)/shard_map/ppermute | solution.py:242
  29.5 0.9 collective-permute-start.8
  30.4 1.2 collective-permute-start.9
  31.5 0.7 collective-permute-start.10
  32.3 3.5 %collective-permute-start.6 = (f32[64,1024]{1,0:T(8,128)S(1)}, f32[64,1024]{1,0:T(8,128)S(1)}, u32[]{:S(2)}, u32[]{:S(2)}) collective-permute-start(f32[64,1024]{1,0:T(8,128)S(1)} %get-tuple-element.125), channel_id=1, source_target_pairs={{0,2},{1,3},{2,0},{3,1},{4,6},{5,7},{6,4},{7,5},{8,10},{9,11},{10,... | collective-permute-start | bytes 786440 | tf_op jit(solution)/shard_map/ppermute | solution.py:242
  35.7 0.2 collective-permute-done.8.refs_1_
  35.9 2.4 %collective-permute-done.9.refs_2_ = bf16[64,1024]{1,0:T(8,128)(2,1)S(1)} collective-permute-done((bf16[64,1024]{1,0:T(8,128)(2,1)S(1)}, bf16[64,1024]{1,0:T(8,128)(2,1)S(1)}, u32[]{:S(2)}, u32[]{:S(2)}) %collective-permute-start.9) | collective-permute-done | bytes 131104 | tf_op jit(solution)/shard_map/ppermute | solution.py:242
  38.4 2.8 %collective-permute-done.10.refs_3_ = bf16[64,1024]{1,0:T(8,128)(2,1)S(1)} collective-permute-done((bf16[64,1024]{1,0:T(8,128)(2,1)S(1)}, bf16[64,1024]{1,0:T(8,128)(2,1)S(1)}, u32[]{:S(2)}, u32[]{:S(2)}) %collective-permute-start.10) | collective-permute-done | bytes 131104 | tf_op jit(solution)/shard_map/ppermute | solution.py:242
  41.1 8.2 %root.4.refs_4_.transformed = bf16[256,1024]{1,0:T(8,128)(2,1)S(1)} custom-call(bf16[64,1024]{1,0:T(8,128)(2,1)S(1)} %get-tuple-element.124.refs_0_, bf16[64,1024]{1,0:T(8,128)(2,1)S(1)} %collective-permute-done.8.refs_1_, bf16[64,1024]{1,0:T(8,128)(2,1)S(1)} %collective-permute-done.9.refs_2_, bf16[64,1024]{1,0:T(8,128)(2,1)S(1)} %collective-permute-done.10.refs_3_, ...), custom_call_target="tpu_custom_call" | custom-call | flops 8000000000 | bytes 1049600 | tf_op jit(solution)/shard_map/root/pallas_call | solution.py:25
  49.3 0.6 rows.3.refs_0_
  49.9 0.9 collective-permute-start.12
  50.8 0.5 collective-permute-start.13
  51.3 3.1 %tile.4.state = f32[512,1024]{1,0:T(8,128)S(1)} custom-call(f32[512,1024]{1,0:T(8,128)S(1)} %copy-done.1, bf16[256,1024]{1,0:T(8,128)(2,1)S(1)} %root.4.refs_4_.transformed, f32[1,1]{1,0:T(1,128)} %get-tuple-element.132.factor), custom_call_target="tpu_custom_call" | custom-call | flops 536870912 | bytes 4194304 | tf_op jit(solution)/shard_map/tile/pallas_call | solution.py:301
  54.4 0.8 collective-permute-done.11.refs_2_
  55.2 1.4 collective-permute-done.12.refs_1_
  56.6 2.3 %collective-permute-start.16 = (bf16[64,1024]{1,0:T(8,128)(2,1)S(1)}, bf16[64,1024]{1,0:T(8,128)(2,1)S(1)}, u32[]{:S(2)}, u32[]{:S(2)}) collective-permute-start(bf16[64,1024]{1,0:T(8,128)(2,1)S(1)} %get-tuple-element.138.refs_0_), channel_id=1, source_target_pairs={{0,1},{1,2},{2,3},{3,0},{4,5},{5,6},{6,7},{7,4},{8,9},{9,10},{10,1... | collective-permute-start | bytes 393224 | tf_op jit(solution)/shard_map/ppermute | solution.py:242
  58.9 0.8 collective-permute-start.17
  59.7 1.1 collective-permute-start.18
  60.8 2.0 %collective-permute-start.14 = (f32[64,1024]{1,0:T(8,128)S(1)}, f32[64,1024]{1,0:T(8,128)S(1)}, u32[]{:S(2)}, u32[]{:S(2)}) collective-permute-start(f32[64,1024]{1,0:T(8,128)S(1)} %get-tuple-element.139), channel_id=1, source_target_pairs={{0,2},{1,3},{2,0},{3,1},{4,6},{5,7},{6,4},{7,5},{8,10},{9,11},{10,... | collective-permute-start | bytes 786440 | tf_op jit(solution)/shard_map/ppermute | solution.py:242
  62.8 1.0 collective-permute-start.15
  63.8 5.5 %collective-permute-done.16.refs_1_ = bf16[64,1024]{1,0:T(8,128)(2,1)S(1)} collective-permute-done((bf16[64,1024]{1,0:T(8,128)(2,1)S(1)}, bf16[64,1024]{1,0:T(8,128)(2,1)S(1)}, u32[]{:S(2)}, u32[]{:S(2)}) %collective-permute-start.16) | collective-permute-done | bytes 131104 | tf_op jit(solution)/shard_map/ppermute | solution.py:242
  69.3 3.7 %collective-permute-done.18.refs_3_ = bf16[64,1024]{1,0:T(8,128)(2,1)S(1)} collective-permute-done((bf16[64,1024]{1,0:T(8,128)(2,1)S(1)}, bf16[64,1024]{1,0:T(8,128)(2,1)S(1)}, u32[]{:S(2)}, u32[]{:S(2)}) %collective-permute-start.18) | collective-permute-done | bytes 131104 | tf_op jit(solution)/shard_map/ppermute | solution.py:242
  73.0 8.2 %root.5.refs_6_.transformed = bf16[256,1024]{1,0:T(8,128)(2,1)S(1)} custom-call(bf16[64,1024]{1,0:T(8,128)(2,1)S(1)} %get-tuple-element.138.refs_0_, bf16[64,1024]{1,0:T(8,128)(2,1)S(1)} %collective-permute-done.16.refs_1_, bf16[64,1024]{1,0:T(8,128)(2,1)S(1)} %collective-permute-done.17.refs_2_, bf16[64,1024]{1,0:T(8,128)(2,1)S(1)} %collective-permute-done.18.refs_3_, ...), custom_call_target="tpu_custom_call" | custom-call | flops 8000000000 | bytes 1049600 | tf_op jit(solution)/shard_map/root/pallas_call | solution.py:25
  81.2 1.2 rows.4.refs_0_
  82.4 0.1 collective-permute-start.20
  82.5 2.0 %collective-permute-start.19 = (bf16[80,1024]{1,0:T(8,128)(2,1)S(1)}, bf16[80,1024]{1,0:T(8,128)(2,1)S(1)}, u32[]{:S(2)}, u32[]{:S(2)}) collective-permute-start(bf16[80,1024]{1,0:T(8,128)(2,1)S(1)} %rows.4.refs_0_), channel_id=1, source_target_pairs={{4,12},{5,13},{6,14},{7,15},{8,4},{9,5},{10,6},{11,7},{12,8},{13,9... | collective-permute-start | bytes 491528 | tf_op jit(solution)/shard_map/ppermute | solution.py:242
  84.5 0.1 collective-permute-start.21
  84.6 3.0 %tile.5.state = f32[512,1024]{1,0:T(8,128)S(1)} custom-call(f32[512,1024]{1,0:T(8,128)S(1)} %tile.4.state, bf16[256,1024]{1,0:T(8,128)(2,1)S(1)} %root.5.refs_6_.transformed, f32[1,1]{1,0:T(1,128)} %get-tuple-element.148.factor), custom_call_target="tpu_custom_call" | custom-call | flops 536870912 | bytes 4194304 | tf_op jit(solution)/shard_map/tile/pallas_call | solution.py:301
  87.6 3.2 %collective-permute-done.19.refs_2_ = bf16[80,1024]{1,0:T(8,128)(2,1)S(1)} collective-permute-done((bf16[80,1024]{1,0:T(8,128)(2,1)S(1)}, bf16[80,1024]{1,0:T(8,128)(2,1)S(1)}, u32[]{:S(2)}, u32[]{:S(2)}) %collective-permute-start.19) | collective-permute-done | bytes 163872 | tf_op jit(solution)/shard_map/ppermute | solution.py:242
  90.8 3.5 %collective-permute-done.21.refs_1_ = bf16[80,1024]{1,0:T(8,128)(2,1)S(1)} collective-permute-done((bf16[80,1024]{1,0:T(8,128)(2,1)S(1)}, bf16[80,1024]{1,0:T(8,128)(2,1)S(1)}, u32[]{:S(2)}, u32[]{:S(2)}) %collective-permute-start.21) | collective-permute-done | bytes 163872 | tf_op jit(solution)/shard_map/ppermute | solution.py:242
  94.4 1.8 %collective-permute-start.25 = (bf16[64,1024]{1,0:T(8,128)(2,1)S(1)}, bf16[64,1024]{1,0:T(8,128)(2,1)S(1)}, u32[]{:S(2)}, u32[]{:S(2)}) collective-permute-start(bf16[64,1024]{1,0:T(8,128)(2,1)S(1)} %get-tuple-element.154.refs_0_), channel_id=1, source_target_pairs={{0,2},{1,3},{2,0},{3,1},{4,6},{5,7},{6,4},{7,5},{8,10},{9,11},{10,... | collective-permute-start | bytes 393224 | tf_op jit(solution)/shard_map/ppermute | solution.py:242
  96.2 1.3 collective-permute-start.26
  97.5 3.0 %collective-permute-start.22 = (f32[64,1024]{1,0:T(8,128)S(1)}, f32[64,1024]{1,0:T(8,128)S(1)}, u32[]{:S(2)}, u32[]{:S(2)}) collective-permute-start(f32[64,1024]{1,0:T(8,128)S(1)} %get-tuple-element.155), channel_id=1, source_target_pairs={{0,2},{1,3},{2,0},{3,1},{4,6},{5,7},{6,4},{7,5},{8,10},{9,11},{10,... | collective-permute-start | bytes 786440 | tf_op jit(solution)/shard_map/ppermute | solution.py:242
  100.5 1.9 %collective-permute-done.25.refs_2_ = bf16[64,1024]{1,0:T(8,128)(2,1)S(1)} collective-permute-done((bf16[64,1024]{1,0:T(8,128)(2,1)S(1)}, bf16[64,1024]{1,0:T(8,128)(2,1)S(1)}, u32[]{:S(2)}, u32[]{:S(2)}) %collective-permute-start.25) | collective-permute-done | bytes 131104 | tf_op jit(solution)/shard_map/ppermute | solution.py:242
  102.4 2.1 %collective-permute-done.26.refs_3_ = bf16[64,1024]{1,0:T(8,128)(2,1)S(1)} collective-permute-done((bf16[64,1024]{1,0:T(8,128)(2,1)S(1)}, bf16[64,1024]{1,0:T(8,128)(2,1)S(1)}, u32[]{:S(2)}, u32[]{:S(2)}) %collective-permute-start.26) | collective-permute-done | bytes 131104 | tf_op jit(solution)/shard_map/ppermute | solution.py:242
  104.6 8.2 %root.6.refs_8_.transformed = bf16[256,1024]{1,0:T(8,128)(2,1)S(1)} custom-call(bf16[64,1024]{1,0:T(8,128)(2,1)S(1)} %get-tuple-element.154.refs_0_, bf16[64,1024]{1,0:T(8,128)(2,1)S(1)} %collective-permute-done.24.refs_1_, bf16[64,1024]{1,0:T(8,128)(2,1)S(1)} %collective-permute-done.25.refs_2_, bf16[64,1024]{1,0:T(8,128)(2,1)S(1)} %collective-permute-done.26.refs_3_, ...), custom_call_target="tpu_custom_call" | custom-call | flops 8000000000 | bytes 1049600 | tf_op jit(solution)/shard_map/root/pallas_call | solution.py:25
  112.8 1.6 %rows.5.refs_0_ = bf16[80,1024]{1,0:T(8,128)(2,1)S(1)} custom-call(f32[64,1024]{1,0:T(8,128)S(1)} %get-tuple-element.145.refs_0_, f32[64,1024]{1,0:T(8,128)S(1)} %collective-permute-done.20.refs_1_, f32[64,1024]{1,0:T(8,128)S(1)} %collective-permute-done.22.refs_2_, f32[64,1024]{1,0:T(8,128)S(1)} %collective-permute-done.23.refs_3_, ...), custom_call_target="tpu_custom_call" | custom-call | flops 201326592 | bytes 2818816 | tf_op jit(solution)/shard_map/rows/pallas_call | solution.py:25
  114.4 3.1 %collective-permute-start.27 = (bf16[80,1024]{1,0:T(8,128)(2,1)S(1)}, bf16[80,1024]{1,0:T(8,128)(2,1)S(1)}, u32[]{:S(2)}, u32[]{:S(2)}) collective-permute-start(bf16[80,1024]{1,0:T(8,128)(2,1)S(1)} %rows.5.refs_0_), channel_id=1, source_target_pairs={{8,16},{9,17},{10,18},{11,19},{12,8},{13,9},{14,10},{15,11},{16,12... | collective-permute-start | bytes 491528 | tf_op jit(solution)/shard_map/ppermute | solution.py:242
  117.4 3.6 %collective-permute-start.28 = (bf16[80,1024]{1,0:T(8,128)(2,1)S(1)}, bf16[80,1024]{1,0:T(8,128)(2,1)S(1)}, u32[]{:S(2)}, u32[]{:S(2)}) collective-permute-start(bf16[80,1024]{1,0:T(8,128)(2,1)S(1)} %rows.5.refs_0_), channel_id=1, source_target_pairs={{8,12},{9,13},{10,14},{11,15},{12,16},{13,17},{14,18},{15,19},{16,... | collective-permute-start | bytes 491528 | tf_op jit(solution)/shard_map/ppermute | solution.py:242
  121.1 3.1 %tile.6.state = f32[512,1024]{1,0:T(8,128)S(1)} custom-call(f32[512,1024]{1,0:T(8,128)S(1)} %tile.5.state, bf16[256,1024]{1,0:T(8,128)(2,1)S(1)} %root.6.refs_8_.transformed, f32[1,1]{1,0:T(1,128)} %get-tuple-element.163.factor), custom_call_target="tpu_custom_call" | custom-call | flops 536870912 | bytes 4194304 | tf_op jit(solution)/shard_map/tile/pallas_call | solution.py:301
  124.1 0.6 collective-permute-done.27.refs_2_
  124.8 1.3 collective-permute-done.28.refs_1_
  126.2 2.1 %collective-permute-start.30 = (bf16[64,1024]{1,0:T(8,128)(2,1)S(1)}, bf16[64,1024]{1,0:T(8,128)(2,1)S(1)}, u32[]{:S(2)}, u32[]{:S(2)}) collective-permute-start(bf16[64,1024]{1,0:T(8,128)(2,1)S(1)} %get-tuple-element.166.refs_0_), channel_id=1, source_target_pairs={{0,2},{1,3},{2,0},{3,1},{4,6},{5,7},{6,4},{7,5},{8,10},{9,11},{10,... | collective-permute-start | bytes 393224 | tf_op jit(solution)/shard_map/ppermute | solution.py:242
  128.3 1.3 collective-permute-start.31
  129.6 1.5 %collective-permute-done.29.refs_1_ = bf16[64,1024]{1,0:T(8,128)(2,1)S(1)} collective-permute-done((bf16[64,1024]{1,0:T(8,128)(2,1)S(1)}, bf16[64,1024]{1,0:T(8,128)(2,1)S(1)}, u32[]{:S(2)}, u32[]{:S(2)}) %collective-permute-start.29) | collective-permute-done | bytes 131104 | tf_op jit(solution)/shard_map/ppermute | solution.py:242
  131.1 1.6 %collective-permute-done.30.refs_2_ = bf16[64,1024]{1,0:T(8,128)(2,1)S(1)} collective-permute-done((bf16[64,1024]{1,0:T(8,128)(2,1)S(1)}, bf16[64,1024]{1,0:T(8,128)(2,1)S(1)}, u32[]{:S(2)}, u32[]{:S(2)}) %collective-permute-start.30) | collective-permute-done | bytes 131104 | tf_op jit(solution)/shard_map/ppermute | solution.py:242
  132.7 1.8 %collective-permute-done.31.refs_3_ = bf16[64,1024]{1,0:T(8,128)(2,1)S(1)} collective-permute-done((bf16[64,1024]{1,0:T(8,128)(2,1)S(1)}, bf16[64,1024]{1,0:T(8,128)(2,1)S(1)}, u32[]{:S(2)}, u32[]{:S(2)}) %collective-permute-start.31) | collective-permute-done | bytes 131104 | tf_op jit(solution)/shard_map/ppermute | solution.py:242
  134.5 8.2 %root.7.transformed = bf16[256,1024]{1,0:T(8,128)(2,1)S(1)} custom-call(bf16[64,1024]{1,0:T(8,128)(2,1)S(1)} %get-tuple-element.166.refs_0_, bf16[64,1024]{1,0:T(8,128)(2,1)S(1)} %collective-permute-done.29.refs_1_, bf16[64,1024]{1,0:T(8,128)(2,1)S(1)} %collective-permute-done.30.refs_2_, bf16[64,1024]{1,0:T(8,128)(2,1)S(1)} %collective-permute-done.31.refs_3_, ...), custom_call_target="tpu_custom_call" | custom-call | flops 8000000000 | bytes 1049600 | tf_op jit(solution)/shard_map/root/pallas_call | solution.py:25
  142.7 3.1 %tile.7 = f32[512,1024]{1,0:T(8,128)} custom-call(f32[512,1024]{1,0:T(8,128)S(1)} %tile.6.state, bf16[256,1024]{1,0:T(8,128)(2,1)S(1)} %root.7.transformed, f32[1,1]{1,0:T(1,128)} %get-tuple-element.168.factor), custom_call_target="tpu_custom_call" | custom-call | flops 536870912 | bytes 4194304 | tf_op jit(solution)/shard_map/tile/pallas_call | solution.py:301
  (36 shorter events, 0.5 us)
Async XLA Ops:
  0.0 7.4 %copy-start.5 = (s32[64,3,4]{0,2,1:T(4,128)S(1)}, s32[64,3,4]{0,2,1:T(4,128)}, u32[]{:S(2)}) copy-start(s32[64,3,4]{0,2,1:T(4,128)} %param.7) | copy-start | bytes 9220
  0.0 7.5 %copy-start.4 = (f32[1,256]{1,0:T(1,128)S(1)}, f32[1,256]{1,0:T(1,128)}, u32[]{:S(2)}) copy-start(f32[1,256]{1,0:T(1,128)} %own.1) | copy-start | bytes 3076
  0.1 1.6 %copy-start = (f32[512,1024]{1,0:T(8,128)S(1)}, f32[512,1024]{1,0:T(8,128)}, u32[]{:S(2)}) copy-start(f32[512,1024]{1,0:T(8,128)} %state.9) | copy-start | bytes 6291460
  1.7 0.8 copy-start.2
  2.5 5.0 %copy-start.3 = (s32[64,256]{1,0:T(8,128)S(1)}, s32[64,256]{1,0:T(8,128)}, u32[]{:S(2)}) copy-start(s32[64,256]{1,0:T(8,128)} %obs.9) | copy-start | bytes 196612
  2.5 6.9 %copy-start.1 = (f32[512,1024]{1,0:T(8,128)S(1)}, f32[512,1024]{1,0:T(8,128)}, u32[]{:S(2)}) copy-start(f32[512,1024]{1,0:T(8,128)} %state.9) | copy-start | bytes 6291460
  3.6 8.2 %collective-permute-start = (bf16[64,1024]{1,0:T(8,128)(2,1)S(1)}, bf16[64,1024]{1,0:T(8,128)(2,1)S(1)}, u32[]{:S(2)}, u32[]{:S(2)}) collective-permute-start(bf16[64,1024]{1,0:T(8,128)(2,1)S(1)} %get-tuple-element.87), channel_id=1, source_target_pairs={{0,3},{1,0},{2,1},{3,2},{4,7},{5,4},{6,5},{7,6},{8,11},{9,8},{10,9... | collective-permute-start | bytes 393224 | tf_op jit(solution)/shard_map/ppermute | solution.py:242
  4.5 7.7 %collective-permute-start.1 = (bf16[64,1024]{1,0:T(8,128)(2,1)S(1)}, bf16[64,1024]{1,0:T(8,128)(2,1)S(1)}, u32[]{:S(2)}, u32[]{:S(2)}) collective-permute-start(bf16[64,1024]{1,0:T(8,128)(2,1)S(1)} %get-tuple-element.97), channel_id=1, source_target_pairs={{0,1},{1,2},{2,3},{3,0},{4,5},{5,6},{6,7},{7,4},{8,9},{9,10},{10,1... | collective-permute-start | bytes 393224 | tf_op jit(solution)/shard_map/ppermute | solution.py:242
  6.9 6.5 %collective-permute-start.2 = (bf16[64,1024]{1,0:T(8,128)(2,1)S(1)}, bf16[64,1024]{1,0:T(8,128)(2,1)S(1)}, u32[]{:S(2)}, u32[]{:S(2)}) collective-permute-start(bf16[64,1024]{1,0:T(8,128)(2,1)S(1)} %get-tuple-element.98), channel_id=1, source_target_pairs={{0,2},{1,3},{2,0},{3,1},{4,6},{5,7},{6,4},{7,5},{8,10},{9,11},{10,... | collective-permute-start | bytes 393224 | tf_op jit(solution)/shard_map/ppermute | solution.py:242
  13.4 12.7 %collective-permute-start.4 = (f32[64,1024]{1,0:T(8,128)S(1)}, f32[64,1024]{1,0:T(8,128)S(1)}, u32[]{:S(2)}, u32[]{:S(2)}) collective-permute-start(f32[64,1024]{1,0:T(8,128)S(1)} %get-tuple-element.110), channel_id=1, source_target_pairs={{0,1},{1,2},{2,3},{3,0},{4,5},{5,6},{6,7},{7,4},{8,9},{9,10},{10,1... | collective-permute-start | bytes 786440 | tf_op jit(solution)/shard_map/ppermute | solution.py:242
  16.0 10.1 %collective-permute-start.3 = (bf16[80,1024]{1,0:T(8,128)(2,1)S(1)}, bf16[80,1024]{1,0:T(8,128)(2,1)S(1)}, u32[]{:S(2)}, u32[]{:S(2)}) collective-permute-start(bf16[80,1024]{1,0:T(8,128)(2,1)S(1)} %start.1.refs_0_), channel_id=1, source_target_pairs={{252,4},{253,5},{254,6},{255,7},{0,252},{1,253},{2,254},{3,255},{4... | collective-permute-start | bytes 491528 | tf_op jit(solution)/shard_map/ppermute | solution.py:242
  21.4 8.1 %collective-permute-start.5 = (bf16[80,1024]{1,0:T(8,128)(2,1)S(1)}, bf16[80,1024]{1,0:T(8,128)(2,1)S(1)}, u32[]{:S(2)}, u32[]{:S(2)}) collective-permute-start(bf16[80,1024]{1,0:T(8,128)(2,1)S(1)} %start.1.refs_0_), channel_id=1, source_target_pairs={{252,0},{253,1},{254,2},{255,3},{0,4},{1,5},{2,6},{3,7},{4,252},{5... | collective-permute-start | bytes 491528 | tf_op jit(solution)/shard_map/ppermute | solution.py:242
  29.5 6.4 %collective-permute-start.8 = (bf16[64,1024]{1,0:T(8,128)(2,1)S(1)}, bf16[64,1024]{1,0:T(8,128)(2,1)S(1)}, u32[]{:S(2)}, u32[]{:S(2)}) collective-permute-start(bf16[64,1024]{1,0:T(8,128)(2,1)S(1)} %get-tuple-element.124.refs_0_), channel_id=1, source_target_pairs={{0,1},{1,2},{2,3},{3,0},{4,5},{5,6},{6,7},{7,4},{8,9},{9,10},{10,1... | collective-permute-start | bytes 393224 | tf_op jit(solution)/shard_map/ppermute | solution.py:242
  30.4 8.0 %collective-permute-start.9 = (bf16[64,1024]{1,0:T(8,128)(2,1)S(1)}, bf16[64,1024]{1,0:T(8,128)(2,1)S(1)}, u32[]{:S(2)}, u32[]{:S(2)}) collective-permute-start(bf16[64,1024]{1,0:T(8,128)(2,1)S(1)} %get-tuple-element.124.refs_0_), channel_id=1, source_target_pairs={{0,2},{1,3},{2,0},{3,1},{4,6},{5,7},{6,4},{7,5},{8,10},{9,11},{10,... | collective-permute-start | bytes 393224 | tf_op jit(solution)/shard_map/ppermute | solution.py:242
  31.5 9.6 %collective-permute-start.10 = (bf16[64,1024]{1,0:T(8,128)(2,1)S(1)}, bf16[64,1024]{1,0:T(8,128)(2,1)S(1)}, u32[]{:S(2)}, u32[]{:S(2)}) collective-permute-start(bf16[64,1024]{1,0:T(8,128)(2,1)S(1)} %get-tuple-element.124.refs_0_), channel_id=1, source_target_pairs={{0,3},{1,0},{2,1},{3,2},{4,7},{5,4},{6,5},{7,6},{8,11},{9,8},{10,9... | collective-permute-start | bytes 393224 | tf_op jit(solution)/shard_map/ppermute | solution.py:242
  32.3 17.0 %collective-permute-start.6 = (f32[64,1024]{1,0:T(8,128)S(1)}, f32[64,1024]{1,0:T(8,128)S(1)}, u32[]{:S(2)}, u32[]{:S(2)}) collective-permute-start(f32[64,1024]{1,0:T(8,128)S(1)} %get-tuple-element.125), channel_id=1, source_target_pairs={{0,2},{1,3},{2,0},{3,1},{4,6},{5,7},{6,4},{7,5},{8,10},{9,11},{10,... | collective-permute-start | bytes 786440 | tf_op jit(solution)/shard_map/ppermute | solution.py:242
  35.7 13.6 %collective-permute-start.7 = (f32[64,1024]{1,0:T(8,128)S(1)}, f32[64,1024]{1,0:T(8,128)S(1)}, u32[]{:S(2)}, u32[]{:S(2)}) collective-permute-start(f32[64,1024]{1,0:T(8,128)S(1)} %get-tuple-element.126), channel_id=1, source_target_pairs={{0,3},{1,0},{2,1},{3,2},{4,7},{5,4},{6,5},{7,6},{8,11},{9,8},{10,9... | collective-permute-start | bytes 786440 | tf_op jit(solution)/shard_map/ppermute | solution.py:242
  49.9 6.6 %collective-permute-start.12 = (f32[64,1024]{1,0:T(8,128)S(1)}, f32[64,1024]{1,0:T(8,128)S(1)}, u32[]{:S(2)}, u32[]{:S(2)}) collective-permute-start(f32[64,1024]{1,0:T(8,128)S(1)} %get-tuple-element.133), channel_id=1, source_target_pairs={{0,1},{1,2},{2,3},{3,0},{4,5},{5,6},{6,7},{7,4},{8,9},{9,10},{10,1... | collective-permute-start | bytes 786440 | tf_op jit(solution)/shard_map/ppermute | solution.py:242
  50.8 4.4 %collective-permute-start.11 = (bf16[80,1024]{1,0:T(8,128)(2,1)S(1)}, bf16[80,1024]{1,0:T(8,128)(2,1)S(1)}, u32[]{:S(2)}, u32[]{:S(2)}) collective-permute-start(bf16[80,1024]{1,0:T(8,128)(2,1)S(1)} %rows.3.refs_0_), channel_id=1, source_target_pairs={{0,8},{1,9},{2,10},{3,11},{4,0},{5,1},{6,2},{7,3},{8,4},{9,5},{10,... | collective-permute-start | bytes 491528 | tf_op jit(solution)/shard_map/ppermute | solution.py:242
  50.8 5.8 %collective-permute-start.13 = (bf16[80,1024]{1,0:T(8,128)(2,1)S(1)}, bf16[80,1024]{1,0:T(8,128)(2,1)S(1)}, u32[]{:S(2)}, u32[]{:S(2)}) collective-permute-start(bf16[80,1024]{1,0:T(8,128)(2,1)S(1)} %rows.3.refs_0_), channel_id=1, source_target_pairs={{0,4},{1,5},{2,6},{3,7},{4,8},{5,9},{6,10},{7,11},{8,0},{9,1},{10,... | collective-permute-start | bytes 491528 | tf_op jit(solution)/shard_map/ppermute | solution.py:242
  56.6 12.7 %collective-permute-start.16 = (bf16[64,1024]{1,0:T(8,128)(2,1)S(1)}, bf16[64,1024]{1,0:T(8,128)(2,1)S(1)}, u32[]{:S(2)}, u32[]{:S(2)}) collective-permute-start(bf16[64,1024]{1,0:T(8,128)(2,1)S(1)} %get-tuple-element.138.refs_0_), channel_id=1, source_target_pairs={{0,1},{1,2},{2,3},{3,0},{4,5},{5,6},{6,7},{7,4},{8,9},{9,10},{10,1... | collective-permute-start | bytes 393224 | tf_op jit(solution)/shard_map/ppermute | solution.py:242
  58.9 10.4 %collective-permute-start.17 = (bf16[64,1024]{1,0:T(8,128)(2,1)S(1)}, bf16[64,1024]{1,0:T(8,128)(2,1)S(1)}, u32[]{:S(2)}, u32[]{:S(2)}) collective-permute-start(bf16[64,1024]{1,0:T(8,128)(2,1)S(1)} %get-tuple-element.138.refs_0_), channel_id=1, source_target_pairs={{0,2},{1,3},{2,0},{3,1},{4,6},{5,7},{6,4},{7,5},{8,10},{9,11},{10,... | collective-permute-start | bytes 393224 | tf_op jit(solution)/shard_map/ppermute | solution.py:242
  59.7 13.3 %collective-permute-start.18 = (bf16[64,1024]{1,0:T(8,128)(2,1)S(1)}, bf16[64,1024]{1,0:T(8,128)(2,1)S(1)}, u32[]{:S(2)}, u32[]{:S(2)}) collective-permute-start(bf16[64,1024]{1,0:T(8,128)(2,1)S(1)} %get-tuple-element.138.refs_0_), channel_id=1, source_target_pairs={{0,3},{1,0},{2,1},{3,2},{4,7},{5,4},{6,5},{7,6},{8,11},{9,8},{10,9... | collective-permute-start | bytes 393224 | tf_op jit(solution)/shard_map/ppermute | solution.py:242
  60.8 20.4 %collective-permute-start.14 = (f32[64,1024]{1,0:T(8,128)S(1)}, f32[64,1024]{1,0:T(8,128)S(1)}, u32[]{:S(2)}, u32[]{:S(2)}) collective-permute-start(f32[64,1024]{1,0:T(8,128)S(1)} %get-tuple-element.139), channel_id=1, source_target_pairs={{0,2},{1,3},{2,0},{3,1},{4,6},{5,7},{6,4},{7,5},{8,10},{9,11},{10,... | collective-permute-start | bytes 786440 | tf_op jit(solution)/shard_map/ppermute | solution.py:242
  62.8 18.4 %collective-permute-start.15 = (f32[64,1024]{1,0:T(8,128)S(1)}, f32[64,1024]{1,0:T(8,128)S(1)}, u32[]{:S(2)}, u32[]{:S(2)}) collective-permute-start(f32[64,1024]{1,0:T(8,128)S(1)} %get-tuple-element.140), channel_id=1, source_target_pairs={{0,3},{1,0},{2,1},{3,2},{4,7},{5,4},{6,5},{7,6},{8,11},{9,8},{10,9... | collective-permute-start | bytes 786440 | tf_op jit(solution)/shard_map/ppermute | solution.py:242
  82.4 8.4 %collective-permute-start.20 = (f32[64,1024]{1,0:T(8,128)S(1)}, f32[64,1024]{1,0:T(8,128)S(1)}, u32[]{:S(2)}, u32[]{:S(2)}) collective-permute-start(f32[64,1024]{1,0:T(8,128)S(1)} %get-tuple-element.149), channel_id=1, source_target_pairs={{0,1},{1,2},{2,3},{3,0},{4,5},{5,6},{6,7},{7,4},{8,9},{9,10},{10,1... | collective-permute-start | bytes 786440 | tf_op jit(solution)/shard_map/ppermute | solution.py:242
  82.5 8.3 %collective-permute-start.19 = (bf16[80,1024]{1,0:T(8,128)(2,1)S(1)}, bf16[80,1024]{1,0:T(8,128)(2,1)S(1)}, u32[]{:S(2)}, u32[]{:S(2)}) collective-permute-start(bf16[80,1024]{1,0:T(8,128)(2,1)S(1)} %rows.4.refs_0_), channel_id=1, source_target_pairs={{4,12},{5,13},{6,14},{7,15},{8,4},{9,5},{10,6},{11,7},{12,8},{13,9... | collective-permute-start | bytes 491528 | tf_op jit(solution)/shard_map/ppermute | solution.py:242
  84.5 9.8 %collective-permute-start.21 = (bf16[80,1024]{1,0:T(8,128)(2,1)S(1)}, bf16[80,1024]{1,0:T(8,128)(2,1)S(1)}, u32[]{:S(2)}, u32[]{:S(2)}) collective-permute-start(bf16[80,1024]{1,0:T(8,128)(2,1)S(1)} %rows.4.refs_0_), channel_id=1, source_target_pairs={{4,8},{5,9},{6,10},{7,11},{8,12},{9,13},{10,14},{11,15},{12,4},{13... | collective-permute-start | bytes 491528 | tf_op jit(solution)/shard_map/ppermute | solution.py:242
  94.3 6.2 %collective-permute-start.24 = (bf16[64,1024]{1,0:T(8,128)(2,1)S(1)}, bf16[64,1024]{1,0:T(8,128)(2,1)S(1)}, u32[]{:S(2)}, u32[]{:S(2)}) collective-permute-start(bf16[64,1024]{1,0:T(8,128)(2,1)S(1)} %get-tuple-element.154.refs_0_), channel_id=1, source_target_pairs={{0,1},{1,2},{2,3},{3,0},{4,5},{5,6},{6,7},{7,4},{8,9},{9,10},{10,1... | collective-permute-start | bytes 393224 | tf_op jit(solution)/shard_map/ppermute | solution.py:242
  94.4 8.0 %collective-permute-start.25 = (bf16[64,1024]{1,0:T(8,128)(2,1)S(1)}, bf16[64,1024]{1,0:T(8,128)(2,1)S(1)}, u32[]{:S(2)}, u32[]{:S(2)}) collective-permute-start(bf16[64,1024]{1,0:T(8,128)(2,1)S(1)} %get-tuple-element.154.refs_0_), channel_id=1, source_target_pairs={{0,2},{1,3},{2,0},{3,1},{4,6},{5,7},{6,4},{7,5},{8,10},{9,11},{10,... | collective-permute-start | bytes 393224 | tf_op jit(solution)/shard_map/ppermute | solution.py:242
  96.2 8.4 %collective-permute-start.26 = (bf16[64,1024]{1,0:T(8,128)(2,1)S(1)}, bf16[64,1024]{1,0:T(8,128)(2,1)S(1)}, u32[]{:S(2)}, u32[]{:S(2)}) collective-permute-start(bf16[64,1024]{1,0:T(8,128)(2,1)S(1)} %get-tuple-element.154.refs_0_), channel_id=1, source_target_pairs={{0,3},{1,0},{2,1},{3,2},{4,7},{5,4},{6,5},{7,6},{8,11},{9,8},{10,9... | collective-permute-start | bytes 393224 | tf_op jit(solution)/shard_map/ppermute | solution.py:242
  97.5 15.2 %collective-permute-start.22 = (f32[64,1024]{1,0:T(8,128)S(1)}, f32[64,1024]{1,0:T(8,128)S(1)}, u32[]{:S(2)}, u32[]{:S(2)}) collective-permute-start(f32[64,1024]{1,0:T(8,128)S(1)} %get-tuple-element.155), channel_id=1, source_target_pairs={{0,2},{1,3},{2,0},{3,1},{4,6},{5,7},{6,4},{7,5},{8,10},{9,11},{10,... | collective-permute-start | bytes 786440 | tf_op jit(solution)/shard_map/ppermute | solution.py:242
  100.5 12.2 %collective-permute-start.23 = (f32[64,1024]{1,0:T(8,128)S(1)}, f32[64,1024]{1,0:T(8,128)S(1)}, u32[]{:S(2)}, u32[]{:S(2)}) collective-permute-start(f32[64,1024]{1,0:T(8,128)S(1)} %get-tuple-element.156), channel_id=1, source_target_pairs={{0,3},{1,0},{2,1},{3,2},{4,7},{5,4},{6,5},{7,6},{8,11},{9,8},{10,9... | collective-permute-start | bytes 786440 | tf_op jit(solution)/shard_map/ppermute | solution.py:242
  114.4 10.4 %collective-permute-start.27 = (bf16[80,1024]{1,0:T(8,128)(2,1)S(1)}, bf16[80,1024]{1,0:T(8,128)(2,1)S(1)}, u32[]{:S(2)}, u32[]{:S(2)}) collective-permute-start(bf16[80,1024]{1,0:T(8,128)(2,1)S(1)} %rows.5.refs_0_), channel_id=1, source_target_pairs={{8,16},{9,17},{10,18},{11,19},{12,8},{13,9},{14,10},{15,11},{16,12... | collective-permute-start | bytes 491528 | tf_op jit(solution)/shard_map/ppermute | solution.py:242
  117.4 8.6 %collective-permute-start.28 = (bf16[80,1024]{1,0:T(8,128)(2,1)S(1)}, bf16[80,1024]{1,0:T(8,128)(2,1)S(1)}, u32[]{:S(2)}, u32[]{:S(2)}) collective-permute-start(bf16[80,1024]{1,0:T(8,128)(2,1)S(1)} %rows.5.refs_0_), channel_id=1, source_target_pairs={{8,12},{9,13},{10,14},{11,15},{12,16},{13,17},{14,18},{15,19},{16,... | collective-permute-start | bytes 491528 | tf_op jit(solution)/shard_map/ppermute | solution.py:242
  126.1 5.0 %collective-permute-start.29 = (bf16[64,1024]{1,0:T(8,128)(2,1)S(1)}, bf16[64,1024]{1,0:T(8,128)(2,1)S(1)}, u32[]{:S(2)}, u32[]{:S(2)}) collective-permute-start(bf16[64,1024]{1,0:T(8,128)(2,1)S(1)} %get-tuple-element.166.refs_0_), channel_id=1, source_target_pairs={{0,1},{1,2},{2,3},{3,0},{4,5},{5,6},{6,7},{7,4},{8,9},{9,10},{10,1... | collective-permute-start | bytes 393224 | tf_op jit(solution)/shard_map/ppermute | solution.py:242
  126.2 6.6 %collective-permute-start.30 = (bf16[64,1024]{1,0:T(8,128)(2,1)S(1)}, bf16[64,1024]{1,0:T(8,128)(2,1)S(1)}, u32[]{:S(2)}, u32[]{:S(2)}) collective-permute-start(bf16[64,1024]{1,0:T(8,128)(2,1)S(1)} %get-tuple-element.166.refs_0_), channel_id=1, source_target_pairs={{0,2},{1,3},{2,0},{3,1},{4,6},{5,7},{6,4},{7,5},{8,10},{9,11},{10,... | collective-permute-start | bytes 393224 | tf_op jit(solution)/shard_map/ppermute | solution.py:242
  128.3 6.2 %collective-permute-start.31 = (bf16[64,1024]{1,0:T(8,128)(2,1)S(1)}, bf16[64,1024]{1,0:T(8,128)(2,1)S(1)}, u32[]{:S(2)}, u32[]{:S(2)}) collective-permute-start(bf16[64,1024]{1,0:T(8,128)(2,1)S(1)} %get-tuple-element.166.refs_0_), channel_id=1, source_target_pairs={{0,3},{1,0},{2,1},{3,2},{4,7},{5,4},{6,5},{7,6},{8,11},{9,8},{10,9... | collective-permute-start | bytes 393224 | tf_op jit(solution)/shard_map/ppermute | solution.py:242

commit v5 on v2

--- a/solution.py
+++ b/solution.py
@@ -71,7 +71,8 @@
     columns, size = obs.shape
     share = size // tiles
     col, tile = place[0, 0], place[0, 1]
-    band = state.shape[1] // tiles
+    bands = tiles if scratch.dtype == F32 else 1
+    band = state.shape[1] // bands
     for n, colour in enumerate(colours):
         slot, active, batch = standing(col, colour, columns)
         first = jnp.where(active, (slot * tiles + tile) * tile_rows, -(1 << 20))
@@ -95,7 +96,7 @@
             scratch[:, lanes] = picked.astype(scratch.dtype)
             return 0
 
-        lax.fori_loop(0, tiles, pick_band, 0)
+        lax.fori_loop(0, bands, pick_band, 0)
         for step, out in enumerate(outs):
             start = pl.multiple_of(lax.rem(tile + step, tiles) * share, share)
             out[n * share : (n + 1) * share, :] = scratch[pl.ds(start, share), :]
@@ -367,7 +368,7 @@
         if colour < NCOL - 1:
             sources = [(done[n], row_factor[colour + 1, n]) for n in range(colour + 1)]
             rows = move(parts, sources, extra[colour + 1])
-        blocks = 4 if colour < NCOL - 1 else LAST_BLOCKS
+        blocks = 2 if colour < NCOL - 1 else LAST_BLOCKS
         state = move_tile(state, done[colour], tile_factor[colour], blocks)
     return state
 

time: 142 us -> 142 us (level)
  Pallas kernels: 59.1 us -> 56 us
  waiting for transfers between devices: 35.1 us -> 37.5 us
    pallas_call x4, Pallas kernels: 12.2 us -> 9.74 us  [move_tile(): pl.pallas_call(tile_kernel, out_shape=jax.ShapeDtypeStruct(state.shape, F...]
    ppermute x32, waiting for transfers between devices: 35.1 us -> 37.5 us  [hop(): return lax.ppermute(value, AXES, flat)]
  transfers between devices with their start and end apart: 32 -> 32, of which waited for: 20 -> 20; matrix products, arithmetic and copies ran while one was open for 0% -> 0% of each run, Pallas kernels for 30% -> 29%
where the time goes in v5:
time: 142 us; the launch traced here: 140 us
  Pallas kernels  56 us (39%)
  starting transfers between devices  43.6 us (31%)
  waiting for transfers between devices  37.5 us (26%)
  local copies, waits for them, and re-layouts  2.55 us (2%)
    pallas_call x17, Pallas kernels, kernel_call(): pl.pallas_call(body, out_shape=out, in_specs=[scalar if n in smem else wh...  46.3 us
    ppermute x32, starting transfers between devices, hop(): return lax.ppermute(value, AXES, flat)  43.6 us
    ppermute x32, waiting for transfers between devices, hop(): return lax.ppermute(value, AXES, flat)  37.5 us
    pallas_call x4, Pallas kernels, move_tile(): pl.pallas_call(tile_kernel, out_shape=jax.ShapeDtypeStruct(state.shape, F...  9.74 us
  transfers between devices with their start and end apart: 32, of which 20 were waited for; matrix products, arithmetic and copies ran while one was open for 0% of the time, Pallas kernels for 29%

profile of v5, /device:TPU:6, one launch (start us, length us, event | category | flops | bytes accessed | tf_op | source)
XLA Modules:
  0.0 140.0 jit_solution(10890152530831503316)
XLA Ops:
  0.1 1.6 %copy-done = f32[512,1024]{1,0:T(8,128)S(1)} copy-done((f32[512,1024]{1,0:T(8,128)S(1)}, f32[512,1024]{1,0:T(8,128)}, u32[]{:S(2)}) %copy-start) | copy-done | bytes 2097176
  1.7 0.8 copy-done.2
  2.5 1.1 pick.4
  3.6 0.9 collective-permute-start.2
  4.5 2.4 %collective-permute-start = (bf16[64,1024]{1,0:T(8,128)(2,1)S(1)}, bf16[64,1024]{1,0:T(8,128)(2,1)S(1)}, u32[]{:S(2)}, u32[]{:S(2)}) collective-permute-start(bf16[64,1024]{1,0:T(8,128)(2,1)S(1)} %get-tuple-element.76), channel_id=1, source_target_pairs={{0,1},{1,2},{2,3},{3,0},{4,5},{5,6},{6,7},{7,4},{8,9},{9,10},{10,1... | collective-permute-start | bytes 393224 | tf_op jit(solution)/shard_map/ppermute | solution.py:242
  6.9 0.5 collective-permute-start.1
  7.5 1.9 %setup.1 = (f32[64,1]{1,0:T(8,128)S(1)}, f32[64,1]{1,0:T(8,128)S(1)}, f32[64,1]{1,0:T(8,128)S(1)}, f32[64,1]{1,0:T(8,128)S(1)}, f32[64,1]{1,0:T(8,128)S(1)}, /*i...) custom-call(s32[64,256]{1,0:T(8,128)S(1)} %copy-done.3, ...), custom_call_target="tpu_custom_call" | custom-call | flops 1000000 | bytes 202268 | tf_op jit(solution)/shard_map/setup/pallas_call | solution.py:25
  9.4 2.4 %pick.5 = (f32[64,1024]{1,0:T(8,128)S(1)}, f32[64,1024]{1,0:T(8,128)S(1)}, f32[64,1024]{1,0:T(8,128)S(1)}, f32[64,1024]{1,0:T(8,128)S(1)}) custom-call(f32[512,1024]{1,0:T(8,128)S(1)} %copy-done.1, s32[64,256]{1,0:T(8,128)S(1)} %copy-done.3, s32[1,3]{1,0:T(1,128)S(1)} %add_bitcast_fusion.place), custom_call_target="tpu_custom_call" | custom-call | flops 805306368 | bytes 3211276 | tf_op jit(solution)/shard_map/pick/pallas_call | solution.py:25
  11.8 0.5 collective-permute-done.refs_1_
  12.2 1.2 collective-permute-done.1.refs_2_
  13.4 6.1 %collective-permute-start.3 = (bf16[80,1024]{1,0:T(8,128)(2,1)S(1)}, bf16[80,1024]{1,0:T(8,128)(2,1)S(1)}, u32[]{:S(2)}, u32[]{:S(2)}) collective-permute-start(bf16[80,1024]{1,0:T(8,128)(2,1)S(1)} %start.1.refs_0_), channel_id=1, source_target_pairs={{252,4},{253,5},{254,6},{255,7},{0,252},{1,253},{2,254},{3,255},{4... | collective-permute-start | bytes 491528 | tf_op jit(solution)/shard_map/ppermute | solution.py:242
  19.6 2.4 %pick.6 = (f32[64,1024]{1,0:T(8,128)S(1)}, f32[64,1024]{1,0:T(8,128)S(1)}, f32[64,1024]{1,0:T(8,128)S(1)}, f32[64,1024]{1,0:T(8,128)S(1)}) custom-call(f32[512,1024]{1,0:T(8,128)S(1)} %copy-done.1, s32[64,256]{1,0:T(8,128)S(1)} %copy-done.3, s32[1,3]{1,0:T(1,128)S(1)} %add_bitcast_fusion.place), custom_call_target="tpu_custom_call" | custom-call | flops 805306368 | bytes 3211276 | tf_op jit(solution)/shard_map/pick/pallas_call | solution.py:25
  21.9 2.4 %pick.7 = (f32[64,1024]{1,0:T(8,128)S(1)}, f32[64,1024]{1,0:T(8,128)S(1)}, f32[64,1024]{1,0:T(8,128)S(1)}, f32[64,1024]{1,0:T(8,128)S(1)}) custom-call(f32[512,1024]{1,0:T(8,128)S(1)} %copy-done.1, s32[64,256]{1,0:T(8,128)S(1)} %copy-done.3, s32[1,3]{1,0:T(1,128)S(1)} %add_bitcast_fusion.place), custom_call_target="tpu_custom_call" | custom-call | flops 805306368 | bytes 3211276 | tf_op jit(solution)/shard_map/pick/pallas_call | solution.py:25
  24.3 3.3 %collective-permute-done.4.refs_1_ = bf16[80,1024]{1,0:T(8,128)(2,1)S(1)} collective-permute-done((bf16[80,1024]{1,0:T(8,128)(2,1)S(1)}, bf16[80,1024]{1,0:T(8,128)(2,1)S(1)}, u32[]{:S(2)}, u32[]{:S(2)}) %collective-permute-start.4) | collective-permute-done | bytes 163872 | tf_op jit(solution)/shard_map/ppermute | solution.py:242
  27.6 2.2 %collective-permute-start.8 = (bf16[64,1024]{1,0:T(8,128)(2,1)S(1)}, bf16[64,1024]{1,0:T(8,128)(2,1)S(1)}, u32[]{:S(2)}, u32[]{:S(2)}) collective-permute-start(bf16[64,1024]{1,0:T(8,128)(2,1)S(1)} %get-tuple-element.106.refs_0_), channel_id=1, source_target_pairs={{0,1},{1,2},{2,3},{3,0},{4,5},{5,6},{6,7},{7,4},{8,9},{9,10},{10,1... | collective-permute-start | bytes 393224 | tf_op jit(solution)/shard_map/ppermute | solution.py:242
  29.9 1.3 collective-permute-start.9
  31.1 0.4 collective-permute-start.10
  31.5 2.9 %collective-permute-start.5 = (f32[64,1024]{1,0:T(8,128)S(1)}, f32[64,1024]{1,0:T(8,128)S(1)}, u32[]{:S(2)}, u32[]{:S(2)}) collective-permute-start(f32[64,1024]{1,0:T(8,128)S(1)} %get-tuple-element.108), channel_id=1, source_target_pairs={{0,1},{1,2},{2,3},{3,0},{4,5},{5,6},{6,7},{7,4},{8,9},{9,10},{10,1... | collective-permute-start | bytes 786440 | tf_op jit(solution)/shard_map/ppermute | solution.py:242
  34.4 1.0 collective-permute-start.6
  35.4 2.4 %collective-permute-done.9.refs_2_ = bf16[64,1024]{1,0:T(8,128)(2,1)S(1)} collective-permute-done((bf16[64,1024]{1,0:T(8,128)(2,1)S(1)}, bf16[64,1024]{1,0:T(8,128)(2,1)S(1)}, u32[]{:S(2)}, u32[]{:S(2)}) %collective-permute-start.9) | collective-permute-done | bytes 131104 | tf_op jit(solution)/shard_map/ppermute | solution.py:242
  37.8 4.4 %collective-permute-done.10.refs_3_ = bf16[64,1024]{1,0:T(8,128)(2,1)S(1)} collective-permute-done((bf16[64,1024]{1,0:T(8,128)(2,1)S(1)}, bf16[64,1024]{1,0:T(8,128)(2,1)S(1)}, u32[]{:S(2)}, u32[]{:S(2)}) %collective-permute-start.10) | collective-permute-done | bytes 131104 | tf_op jit(solution)/shard_map/ppermute | solution.py:242
  42.2 8.2 %root.4.refs_4_.transformed = bf16[256,1024]{1,0:T(8,128)(2,1)S(1)} custom-call(bf16[64,1024]{1,0:T(8,128)(2,1)S(1)} %get-tuple-element.106.refs_0_, bf16[64,1024]{1,0:T(8,128)(2,1)S(1)} %collective-permute-done.8.refs_1_, bf16[64,1024]{1,0:T(8,128)(2,1)S(1)} %collective-permute-done.9.refs_2_, bf16[64,1024]{1,0:T(8,128)(2,1)S(1)} %collective-permute-done.10.refs_3_, ...), custom_call_target="tpu_custom_call" | custom-call | flops 8000000000 | bytes 1049600 | tf_op jit(solution)/shard_map/root/pallas_call | solution.py:25
  50.4 0.6 rows.3.refs_0_
  51.0 0.3 collective-permute-start.12
  51.3 0.5 collective-permute-start.11
  51.8 2.3 %tile.4.state = f32[512,1024]{1,0:T(8,128)S(1)} custom-call(f32[512,1024]{1,0:T(8,128)S(1)} %copy-done.1, bf16[256,1024]{1,0:T(8,128)(2,1)S(1)} %root.4.refs_4_.transformed, f32[1,1]{1,0:T(1,128)} %get-tuple-element.114.factor), custom_call_target="tpu_custom_call" | custom-call | flops 536870912 | bytes 4194304 | tf_op jit(solution)/shard_map/tile/pallas_call | solution.py:301
  54.0 1.6 %collective-permute-done.12.refs_2_ = bf16[80,1024]{1,0:T(8,128)(2,1)S(1)} collective-permute-done((bf16[80,1024]{1,0:T(8,128)(2,1)S(1)}, bf16[80,1024]{1,0:T(8,128)(2,1)S(1)}, u32[]{:S(2)}, u32[]{:S(2)}) %collective-permute-start.12) | collective-permute-done | bytes 163872 | tf_op jit(solution)/shard_map/ppermute | solution.py:242
  55.7 1.0 collective-permute-done.11.refs_1_
  56.8 0.8 collective-permute-start.17
  57.6 1.3 collective-permute-start.18
  59.0 2.5 %collective-permute-start.13 = (f32[64,1024]{1,0:T(8,128)S(1)}, f32[64,1024]{1,0:T(8,128)S(1)}, u32[]{:S(2)}, u32[]{:S(2)}) collective-permute-start(f32[64,1024]{1,0:T(8,128)S(1)} %get-tuple-element.118), channel_id=1, source_target_pairs={{0,1},{1,2},{2,3},{3,0},{4,5},{5,6},{6,7},{7,4},{8,9},{9,10},{10,1... | collective-permute-start | bytes 786440 | tf_op jit(solution)/shard_map/ppermute | solution.py:242
  61.5 1.5 %collective-permute-start.14 = (f32[64,1024]{1,0:T(8,128)S(1)}, f32[64,1024]{1,0:T(8,128)S(1)}, u32[]{:S(2)}, u32[]{:S(2)}) collective-permute-start(f32[64,1024]{1,0:T(8,128)S(1)} %get-tuple-element.119), channel_id=1, source_target_pairs={{0,2},{1,3},{2,0},{3,1},{4,6},{5,7},{6,4},{7,5},{8,10},{9,11},{10,... | collective-permute-start | bytes 786440 | tf_op jit(solution)/shard_map/ppermute | solution.py:242
  63.0 0.3 collective-permute-done.16.refs_1_
  63.2 1.2 collective-permute-start.15
  64.4 0.4 collective-permute-done.17.refs_2_
  64.8 5.9 %collective-permute-done.18.refs_3_ = bf16[64,1024]{1,0:T(8,128)(2,1)S(1)} collective-permute-done((bf16[64,1024]{1,0:T(8,128)(2,1)S(1)}, bf16[64,1024]{1,0:T(8,128)(2,1)S(1)}, u32[]{:S(2)}, u32[]{:S(2)}) %collective-permute-start.18) | collective-permute-done | bytes 131104 | tf_op jit(solution)/shard_map/ppermute | solution.py:242
  70.7 8.2 %root.5.refs_6_.transformed = bf16[256,1024]{1,0:T(8,128)(2,1)S(1)} custom-call(bf16[64,1024]{1,0:T(8,128)(2,1)S(1)} %get-tuple-element.116.refs_0_, bf16[64,1024]{1,0:T(8,128)(2,1)S(1)} %collective-permute-done.16.refs_1_, bf16[64,1024]{1,0:T(8,128)(2,1)S(1)} %collective-permute-done.17.refs_2_, bf16[64,1024]{1,0:T(8,128)(2,1)S(1)} %collective-permute-done.18.refs_3_, ...), custom_call_target="tpu_custom_call" | custom-call | flops 8000000000 | bytes 1049600 | tf_op jit(solution)/shard_map/root/pallas_call | solution.py:25
  78.9 1.2 rows.4.refs_0_
  80.2 2.0 %collective-permute-start.19 = (bf16[80,1024]{1,0:T(8,128)(2,1)S(1)}, bf16[80,1024]{1,0:T(8,128)(2,1)S(1)}, u32[]{:S(2)}, u32[]{:S(2)}) collective-permute-start(bf16[80,1024]{1,0:T(8,128)(2,1)S(1)} %rows.4.refs_0_), channel_id=1, source_target_pairs={{4,8},{5,9},{6,10},{7,11},{8,12},{9,13},{10,14},{11,15},{12,4},{13... | collective-permute-start | bytes 491528 | tf_op jit(solution)/shard_map/ppermute | solution.py:242
  82.2 2.1 %tile.5.state = f32[512,1024]{1,0:T(8,128)S(1)} custom-call(f32[512,1024]{1,0:T(8,128)S(1)} %tile.4.state, bf16[256,1024]{1,0:T(8,128)(2,1)S(1)} %root.5.refs_6_.transformed, f32[1,1]{1,0:T(1,128)} %get-tuple-element.126.factor), custom_call_target="tpu_custom_call" | custom-call | flops 536870912 | bytes 4194304 | tf_op jit(solution)/shard_map/tile/pallas_call | solution.py:301
  84.3 1.1 collective-permute-done.20.refs_2_
  85.5 2.9 %collective-permute-done.19.refs_1_ = bf16[80,1024]{1,0:T(8,128)(2,1)S(1)} collective-permute-done((bf16[80,1024]{1,0:T(8,128)(2,1)S(1)}, bf16[80,1024]{1,0:T(8,128)(2,1)S(1)}, u32[]{:S(2)}, u32[]{:S(2)}) %collective-permute-start.19) | collective-permute-done | bytes 163872 | tf_op jit(solution)/shard_map/ppermute | solution.py:242
  88.5 1.9 %collective-permute-start.25 = (bf16[64,1024]{1,0:T(8,128)(2,1)S(1)}, bf16[64,1024]{1,0:T(8,128)(2,1)S(1)}, u32[]{:S(2)}, u32[]{:S(2)}) collective-permute-start(bf16[64,1024]{1,0:T(8,128)(2,1)S(1)} %get-tuple-element.128.refs_0_), channel_id=1, source_target_pairs={{0,2},{1,3},{2,0},{3,1},{4,6},{5,7},{6,4},{7,5},{8,10},{9,11},{10,... | collective-permute-start | bytes 393224 | tf_op jit(solution)/shard_map/ppermute | solution.py:242
  90.4 1.0 collective-permute-start.26
  91.4 2.2 %collective-permute-start.21 = (f32[64,1024]{1,0:T(8,128)S(1)}, f32[64,1024]{1,0:T(8,128)S(1)}, u32[]{:S(2)}, u32[]{:S(2)}) collective-permute-start(f32[64,1024]{1,0:T(8,128)S(1)} %get-tuple-element.130), channel_id=1, source_target_pairs={{0,1},{1,2},{2,3},{3,0},{4,5},{5,6},{6,7},{7,4},{8,9},{9,10},{10,1... | collective-permute-start | bytes 786440 | tf_op jit(solution)/shard_map/ppermute | solution.py:242
  93.6 1.0 collective-permute-start.22
  94.6 0.3 collective-permute-done.24.refs_1_
  94.9 1.2 collective-permute-start.23
  96.0 0.5 collective-permute-done.25.refs_2_
  96.5 2.1 %collective-permute-done.26.refs_3_ = bf16[64,1024]{1,0:T(8,128)(2,1)S(1)} collective-permute-done((bf16[64,1024]{1,0:T(8,128)(2,1)S(1)}, bf16[64,1024]{1,0:T(8,128)(2,1)S(1)}, u32[]{:S(2)}, u32[]{:S(2)}) %collective-permute-start.26) | collective-permute-done | bytes 131104 | tf_op jit(solution)/shard_map/ppermute | solution.py:242
  98.6 8.2 %root.6.refs_8_.transformed = bf16[256,1024]{1,0:T(8,128)(2,1)S(1)} custom-call(bf16[64,1024]{1,0:T(8,128)(2,1)S(1)} %get-tuple-element.128.refs_0_, bf16[64,1024]{1,0:T(8,128)(2,1)S(1)} %collective-permute-done.24.refs_1_, bf16[64,1024]{1,0:T(8,128)(2,1)S(1)} %collective-permute-done.25.refs_2_, bf16[64,1024]{1,0:T(8,128)(2,1)S(1)} %collective-permute-done.26.refs_3_, ...), custom_call_target="tpu_custom_call" | custom-call | flops 8000000000 | bytes 1049600 | tf_op jit(solution)/shard_map/root/pallas_call | solution.py:25
  106.9 1.6 %rows.5.refs_0_ = bf16[80,1024]{1,0:T(8,128)(2,1)S(1)} custom-call(f32[64,1024]{1,0:T(8,128)S(1)} %get-tuple-element.129.refs_0_, f32[64,1024]{1,0:T(8,128)S(1)} %collective-permute-done.21.refs_1_, f32[64,1024]{1,0:T(8,128)S(1)} %collective-permute-done.22.refs_2_, f32[64,1024]{1,0:T(8,128)S(1)} %collective-permute-done.23.refs_3_, ...), custom_call_target="tpu_custom_call" | custom-call | flops 201326592 | bytes 2818816 | tf_op jit(solution)/shard_map/rows/pallas_call | solution.py:25
  108.5 2.5 %collective-permute-start.27 = (bf16[80,1024]{1,0:T(8,128)(2,1)S(1)}, bf16[80,1024]{1,0:T(8,128)(2,1)S(1)}, u32[]{:S(2)}, u32[]{:S(2)}) collective-permute-start(bf16[80,1024]{1,0:T(8,128)(2,1)S(1)} %rows.5.refs_0_), channel_id=1, source_target_pairs={{8,16},{9,17},{10,18},{11,19},{12,8},{13,9},{14,10},{15,11},{16,12... | collective-permute-start | bytes 491528 | tf_op jit(solution)/shard_map/ppermute | solution.py:242
  110.9 3.0 %collective-permute-start.28 = (bf16[80,1024]{1,0:T(8,128)(2,1)S(1)}, bf16[80,1024]{1,0:T(8,128)(2,1)S(1)}, u32[]{:S(2)}, u32[]{:S(2)}) collective-permute-start(bf16[80,1024]{1,0:T(8,128)(2,1)S(1)} %rows.5.refs_0_), channel_id=1, source_target_pairs={{8,12},{9,13},{10,14},{11,15},{12,16},{13,17},{14,18},{15,19},{16,... | collective-permute-start | bytes 491528 | tf_op jit(solution)/shard_map/ppermute | solution.py:242
  114.0 2.2 %tile.6.state = f32[512,1024]{1,0:T(8,128)S(1)} custom-call(f32[512,1024]{1,0:T(8,128)S(1)} %tile.5.state, bf16[256,1024]{1,0:T(8,128)(2,1)S(1)} %root.6.refs_8_.transformed, f32[1,1]{1,0:T(1,128)} %get-tuple-element.139.factor), custom_call_target="tpu_custom_call" | custom-call | flops 536870912 | bytes 4194304 | tf_op jit(solution)/shard_map/tile/pallas_call | solution.py:301
  116.2 1.0 collective-permute-done.27.refs_2_
  117.2 1.8 %collective-permute-done.28.refs_1_ = bf16[80,1024]{1,0:T(8,128)(2,1)S(1)} collective-permute-done((bf16[80,1024]{1,0:T(8,128)(2,1)S(1)}, bf16[80,1024]{1,0:T(8,128)(2,1)S(1)}, u32[]{:S(2)}, u32[]{:S(2)}) %collective-permute-start.28) | collective-permute-done | bytes 163872 | tf_op jit(solution)/shard_map/ppermute | solution.py:242
  119.0 1.8 %collective-permute-start.29 = (bf16[64,1024]{1,0:T(8,128)(2,1)S(1)}, bf16[64,1024]{1,0:T(8,128)(2,1)S(1)}, u32[]{:S(2)}, u32[]{:S(2)}) collective-permute-start(bf16[64,1024]{1,0:T(8,128)(2,1)S(1)} %get-tuple-element.142.refs_0_), channel_id=1, source_target_pairs={{0,1},{1,2},{2,3},{3,0},{4,5},{5,6},{6,7},{7,4},{8,9},{9,10},{10,1... | collective-permute-start | bytes 393224 | tf_op jit(solution)/shard_map/ppermute | solution.py:242
  120.9 0.8 collective-permute-start.30
  121.8 2.9 %collective-permute-done.29.refs_1_ = bf16[64,1024]{1,0:T(8,128)(2,1)S(1)} collective-permute-done((bf16[64,1024]{1,0:T(8,128)(2,1)S(1)}, bf16[64,1024]{1,0:T(8,128)(2,1)S(1)}, u32[]{:S(2)}, u32[]{:S(2)}) %collective-permute-start.29) | collective-permute-done | bytes 131104 | tf_op jit(solution)/shard_map/ppermute | solution.py:242
  124.8 2.6 %collective-permute-done.30.refs_2_ = bf16[64,1024]{1,0:T(8,128)(2,1)S(1)} collective-permute-done((bf16[64,1024]{1,0:T(8,128)(2,1)S(1)}, bf16[64,1024]{1,0:T(8,128)(2,1)S(1)}, u32[]{:S(2)}, u32[]{:S(2)}) %collective-permute-start.30) | collective-permute-done | bytes 131104 | tf_op jit(solution)/shard_map/ppermute | solution.py:242
  127.4 1.3 collective-permute-done.31.refs_3_
  128.7 8.2 %root.7.transformed = bf16[256,1024]{1,0:T(8,128)(2,1)S(1)} custom-call(bf16[64,1024]{1,0:T(8,128)(2,1)S(1)} %get-tuple-element.142.refs_0_, bf16[64,1024]{1,0:T(8,128)(2,1)S(1)} %collective-permute-done.29.refs_1_, bf16[64,1024]{1,0:T(8,128)(2,1)S(1)} %collective-permute-done.30.refs_2_, bf16[64,1024]{1,0:T(8,128)(2,1)S(1)} %collective-permute-done.31.refs_3_, ...), custom_call_target="tpu_custom_call" | custom-call | flops 8000000000 | bytes 1049600 | tf_op jit(solution)/shard_map/root/pallas_call | solution.py:25
  136.9 3.1 %tile.7 = f32[512,1024]{1,0:T(8,128)} custom-call(f32[512,1024]{1,0:T(8,128)S(1)} %tile.6.state, bf16[256,1024]{1,0:T(8,128)(2,1)S(1)} %root.7.transformed, f32[1,1]{1,0:T(1,128)} %get-tuple-element.144.factor), custom_call_target="tpu_custom_call" | custom-call | flops 536870912 | bytes 4194304 | tf_op jit(solution)/shard_map/tile/pallas_call | solution.py:301
  (36 shorter events, 0.8 us)
Async XLA Ops:
  0.0 7.4 %copy-start.5 = (s32[64,3,4]{0,2,1:T(4,128)S(1)}, s32[64,3,4]{0,2,1:T(4,128)}, u32[]{:S(2)}) copy-start(s32[64,3,4]{0,2,1:T(4,128)} %param.7) | copy-start | bytes 9220
  0.0 7.5 %copy-start.4 = (f32[1,256]{1,0:T(1,128)S(1)}, f32[1,256]{1,0:T(1,128)}, u32[]{:S(2)}) copy-start(f32[1,256]{1,0:T(1,128)} %own.1) | copy-start | bytes 3076
  0.1 1.6 %copy-start = (f32[512,1024]{1,0:T(8,128)S(1)}, f32[512,1024]{1,0:T(8,128)}, u32[]{:S(2)}) copy-start(f32[512,1024]{1,0:T(8,128)} %state.9) | copy-start | bytes 6291460
  1.7 0.8 copy-start.2
  2.5 5.0 %copy-start.3 = (s32[64,256]{1,0:T(8,128)S(1)}, s32[64,256]{1,0:T(8,128)}, u32[]{:S(2)}) copy-start(s32[64,256]{1,0:T(8,128)} %obs.9) | copy-start | bytes 196612
  2.5 6.9 %copy-start.1 = (f32[512,1024]{1,0:T(8,128)S(1)}, f32[512,1024]{1,0:T(8,128)}, u32[]{:S(2)}) copy-start(f32[512,1024]{1,0:T(8,128)} %state.9) | copy-start | bytes 6291460
  3.6 8.2 %collective-permute-start.2 = (bf16[64,1024]{1,0:T(8,128)(2,1)S(1)}, bf16[64,1024]{1,0:T(8,128)(2,1)S(1)}, u32[]{:S(2)}, u32[]{:S(2)}) collective-permute-start(bf16[64,1024]{1,0:T(8,128)(2,1)S(1)} %get-tuple-element.78), channel_id=1, source_target_pairs={{0,3},{1,0},{2,1},{3,2},{4,7},{5,4},{6,5},{7,6},{8,11},{9,8},{10,9... | collective-permute-start | bytes 393224 | tf_op jit(solution)/shard_map/ppermute | solution.py:242
  4.5 7.7 %collective-permute-start = (bf16[64,1024]{1,0:T(8,128)(2,1)S(1)}, bf16[64,1024]{1,0:T(8,128)(2,1)S(1)}, u32[]{:S(2)}, u32[]{:S(2)}) collective-permute-start(bf16[64,1024]{1,0:T(8,128)(2,1)S(1)} %get-tuple-element.76), channel_id=1, source_target_pairs={{0,1},{1,2},{2,3},{3,0},{4,5},{5,6},{6,7},{7,4},{8,9},{9,10},{10,1... | collective-permute-start | bytes 393224 | tf_op jit(solution)/shard_map/ppermute | solution.py:242
  6.9 6.5 %collective-permute-start.1 = (bf16[64,1024]{1,0:T(8,128)(2,1)S(1)}, bf16[64,1024]{1,0:T(8,128)(2,1)S(1)}, u32[]{:S(2)}, u32[]{:S(2)}) collective-permute-start(bf16[64,1024]{1,0:T(8,128)(2,1)S(1)} %get-tuple-element.77), channel_id=1, source_target_pairs={{0,2},{1,3},{2,0},{3,1},{4,6},{5,7},{6,4},{7,5},{8,10},{9,11},{10,... | collective-permute-start | bytes 393224 | tf_op jit(solution)/shard_map/ppermute | solution.py:242
  13.4 10.9 %collective-permute-start.3 = (bf16[80,1024]{1,0:T(8,128)(2,1)S(1)}, bf16[80,1024]{1,0:T(8,128)(2,1)S(1)}, u32[]{:S(2)}, u32[]{:S(2)}) collective-permute-start(bf16[80,1024]{1,0:T(8,128)(2,1)S(1)} %start.1.refs_0_), channel_id=1, source_target_pairs={{252,4},{253,5},{254,6},{255,7},{0,252},{1,253},{2,254},{3,255},{4... | collective-permute-start | bytes 491528 | tf_op jit(solution)/shard_map/ppermute | solution.py:242
  19.5 8.1 %collective-permute-start.4 = (bf16[80,1024]{1,0:T(8,128)(2,1)S(1)}, bf16[80,1024]{1,0:T(8,128)(2,1)S(1)}, u32[]{:S(2)}, u32[]{:S(2)}) collective-permute-start(bf16[80,1024]{1,0:T(8,128)(2,1)S(1)} %start.1.refs_0_), channel_id=1, source_target_pairs={{252,0},{253,1},{254,2},{255,3},{0,4},{1,5},{2,6},{3,7},{4,252},{5... | collective-permute-start | bytes 491528 | tf_op jit(solution)/shard_map/ppermute | solution.py:242
  27.6 7.8 %collective-permute-start.8 = (bf16[64,1024]{1,0:T(8,128)(2,1)S(1)}, bf16[64,1024]{1,0:T(8,128)(2,1)S(1)}, u32[]{:S(2)}, u32[]{:S(2)}) collective-permute-start(bf16[64,1024]{1,0:T(8,128)(2,1)S(1)} %get-tuple-element.106.refs_0_), channel_id=1, source_target_pairs={{0,1},{1,2},{2,3},{3,0},{4,5},{5,6},{6,7},{7,4},{8,9},{9,10},{10,1... | collective-permute-start | bytes 393224 | tf_op jit(solution)/shard_map/ppermute | solution.py:242
  29.9 7.9 %collective-permute-start.9 = (bf16[64,1024]{1,0:T(8,128)(2,1)S(1)}, bf16[64,1024]{1,0:T(8,128)(2,1)S(1)}, u32[]{:S(2)}, u32[]{:S(2)}) collective-permute-start(bf16[64,1024]{1,0:T(8,128)(2,1)S(1)} %get-tuple-element.106.refs_0_), channel_id=1, source_target_pairs={{0,2},{1,3},{2,0},{3,1},{4,6},{5,7},{6,4},{7,5},{8,10},{9,11},{10,... | collective-permute-start | bytes 393224 | tf_op jit(solution)/shard_map/ppermute | solution.py:242
  31.1 11.1 %collective-permute-start.10 = (bf16[64,1024]{1,0:T(8,128)(2,1)S(1)}, bf16[64,1024]{1,0:T(8,128)(2,1)S(1)}, u32[]{:S(2)}, u32[]{:S(2)}) collective-permute-start(bf16[64,1024]{1,0:T(8,128)(2,1)S(1)} %get-tuple-element.106.refs_0_), channel_id=1, source_target_pairs={{0,3},{1,0},{2,1},{3,2},{4,7},{5,4},{6,5},{7,6},{8,11},{9,8},{10,9... | collective-permute-start | bytes 393224 | tf_op jit(solution)/shard_map/ppermute | solution.py:242
  31.5 18.9 %collective-permute-start.5 = (f32[64,1024]{1,0:T(8,128)S(1)}, f32[64,1024]{1,0:T(8,128)S(1)}, u32[]{:S(2)}, u32[]{:S(2)}) collective-permute-start(f32[64,1024]{1,0:T(8,128)S(1)} %get-tuple-element.108), channel_id=1, source_target_pairs={{0,1},{1,2},{2,3},{3,0},{4,5},{5,6},{6,7},{7,4},{8,9},{9,10},{10,1... | collective-permute-start | bytes 786440 | tf_op jit(solution)/shard_map/ppermute | solution.py:242
  34.4 16.0 %collective-permute-start.6 = (f32[64,1024]{1,0:T(8,128)S(1)}, f32[64,1024]{1,0:T(8,128)S(1)}, u32[]{:S(2)}, u32[]{:S(2)}) collective-permute-start(f32[64,1024]{1,0:T(8,128)S(1)} %get-tuple-element.109), channel_id=1, source_target_pairs={{0,2},{1,3},{2,0},{3,1},{4,6},{5,7},{6,4},{7,5},{8,10},{9,11},{10,... | collective-permute-start | bytes 786440 | tf_op jit(solution)/shard_map/ppermute | solution.py:242
  35.4 15.0 %collective-permute-start.7 = (f32[64,1024]{1,0:T(8,128)S(1)}, f32[64,1024]{1,0:T(8,128)S(1)}, u32[]{:S(2)}, u32[]{:S(2)}) collective-permute-start(f32[64,1024]{1,0:T(8,128)S(1)} %get-tuple-element.110), channel_id=1, source_target_pairs={{0,3},{1,0},{2,1},{3,2},{4,7},{5,4},{6,5},{7,6},{8,11},{9,8},{10,9... | collective-permute-start | bytes 786440 | tf_op jit(solution)/shard_map/ppermute | solution.py:242
  51.0 4.7 %collective-permute-start.12 = (bf16[80,1024]{1,0:T(8,128)(2,1)S(1)}, bf16[80,1024]{1,0:T(8,128)(2,1)S(1)}, u32[]{:S(2)}, u32[]{:S(2)}) collective-permute-start(bf16[80,1024]{1,0:T(8,128)(2,1)S(1)} %rows.3.refs_0_), channel_id=1, source_target_pairs={{0,8},{1,9},{2,10},{3,11},{4,0},{5,1},{6,2},{7,3},{8,4},{9,5},{10,... | collective-permute-start | bytes 491528 | tf_op jit(solution)/shard_map/ppermute | solution.py:242
  51.3 5.4 %collective-permute-start.11 = (bf16[80,1024]{1,0:T(8,128)(2,1)S(1)}, bf16[80,1024]{1,0:T(8,128)(2,1)S(1)}, u32[]{:S(2)}, u32[]{:S(2)}) collective-permute-start(bf16[80,1024]{1,0:T(8,128)(2,1)S(1)} %rows.3.refs_0_), channel_id=1, source_target_pairs={{0,4},{1,5},{2,6},{3,7},{4,8},{5,9},{6,10},{7,11},{8,0},{9,1},{10,... | collective-permute-start | bytes 491528 | tf_op jit(solution)/shard_map/ppermute | solution.py:242
  56.7 6.5 %collective-permute-start.16 = (bf16[64,1024]{1,0:T(8,128)(2,1)S(1)}, bf16[64,1024]{1,0:T(8,128)(2,1)S(1)}, u32[]{:S(2)}, u32[]{:S(2)}) collective-permute-start(bf16[64,1024]{1,0:T(8,128)(2,1)S(1)} %get-tuple-element.116.refs_0_), channel_id=1, source_target_pairs={{0,1},{1,2},{2,3},{3,0},{4,5},{5,6},{6,7},{7,4},{8,9},{9,10},{10,1... | collective-permute-start | bytes 393224 | tf_op jit(solution)/shard_map/ppermute | solution.py:242
  56.8 8.0 %collective-permute-start.17 = (bf16[64,1024]{1,0:T(8,128)(2,1)S(1)}, bf16[64,1024]{1,0:T(8,128)(2,1)S(1)}, u32[]{:S(2)}, u32[]{:S(2)}) collective-permute-start(bf16[64,1024]{1,0:T(8,128)(2,1)S(1)} %get-tuple-element.116.refs_0_), channel_id=1, source_target_pairs={{0,2},{1,3},{2,0},{3,1},{4,6},{5,7},{6,4},{7,5},{8,10},{9,11},{10,... | collective-permute-start | bytes 393224 | tf_op jit(solution)/shard_map/ppermute | solution.py:242
  57.6 13.1 %collective-permute-start.18 = (bf16[64,1024]{1,0:T(8,128)(2,1)S(1)}, bf16[64,1024]{1,0:T(8,128)(2,1)S(1)}, u32[]{:S(2)}, u32[]{:S(2)}) collective-permute-start(bf16[64,1024]{1,0:T(8,128)(2,1)S(1)} %get-tuple-element.116.refs_0_), channel_id=1, source_target_pairs={{0,3},{1,0},{2,1},{3,2},{4,7},{5,4},{6,5},{7,6},{8,11},{9,8},{10,9... | collective-permute-start | bytes 393224 | tf_op jit(solution)/shard_map/ppermute | solution.py:242
  59.0 19.9 %collective-permute-start.13 = (f32[64,1024]{1,0:T(8,128)S(1)}, f32[64,1024]{1,0:T(8,128)S(1)}, u32[]{:S(2)}, u32[]{:S(2)}) collective-permute-start(f32[64,1024]{1,0:T(8,128)S(1)} %get-tuple-element.118), channel_id=1, source_target_pairs={{0,1},{1,2},{2,3},{3,0},{4,5},{5,6},{6,7},{7,4},{8,9},{9,10},{10,1... | collective-permute-start | bytes 786440 | tf_op jit(solution)/shard_map/ppermute | solution.py:242
  61.5 17.4 %collective-permute-start.14 = (f32[64,1024]{1,0:T(8,128)S(1)}, f32[64,1024]{1,0:T(8,128)S(1)}, u32[]{:S(2)}, u32[]{:S(2)}) collective-permute-start(f32[64,1024]{1,0:T(8,128)S(1)} %get-tuple-element.119), channel_id=1, source_target_pairs={{0,2},{1,3},{2,0},{3,1},{4,6},{5,7},{6,4},{7,5},{8,10},{9,11},{10,... | collective-permute-start | bytes 786440 | tf_op jit(solution)/shard_map/ppermute | solution.py:242
  63.2 15.7 %collective-permute-start.15 = (f32[64,1024]{1,0:T(8,128)S(1)}, f32[64,1024]{1,0:T(8,128)S(1)}, u32[]{:S(2)}, u32[]{:S(2)}) collective-permute-start(f32[64,1024]{1,0:T(8,128)S(1)} %get-tuple-element.120), channel_id=1, source_target_pairs={{0,3},{1,0},{2,1},{3,2},{4,7},{5,4},{6,5},{7,6},{8,11},{9,8},{10,9... | collective-permute-start | bytes 786440 | tf_op jit(solution)/shard_map/ppermute | solution.py:242
  80.1 5.4 %collective-permute-start.20 = (bf16[80,1024]{1,0:T(8,128)(2,1)S(1)}, bf16[80,1024]{1,0:T(8,128)(2,1)S(1)}, u32[]{:S(2)}, u32[]{:S(2)}) collective-permute-start(bf16[80,1024]{1,0:T(8,128)(2,1)S(1)} %rows.4.refs_0_), channel_id=1, source_target_pairs={{4,12},{5,13},{6,14},{7,15},{8,4},{9,5},{10,6},{11,7},{12,8},{13,9... | collective-permute-start | bytes 491528 | tf_op jit(solution)/shard_map/ppermute | solution.py:242
  80.2 8.2 %collective-permute-start.19 = (bf16[80,1024]{1,0:T(8,128)(2,1)S(1)}, bf16[80,1024]{1,0:T(8,128)(2,1)S(1)}, u32[]{:S(2)}, u32[]{:S(2)}) collective-permute-start(bf16[80,1024]{1,0:T(8,128)(2,1)S(1)} %rows.4.refs_0_), channel_id=1, source_target_pairs={{4,8},{5,9},{6,10},{7,11},{8,12},{9,13},{10,14},{11,15},{12,4},{13... | collective-permute-start | bytes 491528 | tf_op jit(solution)/shard_map/ppermute | solution.py:242
  88.4 6.5 %collective-permute-start.24 = (bf16[64,1024]{1,0:T(8,128)(2,1)S(1)}, bf16[64,1024]{1,0:T(8,128)(2,1)S(1)}, u32[]{:S(2)}, u32[]{:S(2)}) collective-permute-start(bf16[64,1024]{1,0:T(8,128)(2,1)S(1)} %get-tuple-element.128.refs_0_), channel_id=1, source_target_pairs={{0,1},{1,2},{2,3},{3,0},{4,5},{5,6},{6,7},{7,4},{8,9},{9,10},{10,1... | collective-permute-start | bytes 393224 | tf_op jit(solution)/shard_map/ppermute | solution.py:242
  88.5 8.1 %collective-permute-start.25 = (bf16[64,1024]{1,0:T(8,128)(2,1)S(1)}, bf16[64,1024]{1,0:T(8,128)(2,1)S(1)}, u32[]{:S(2)}, u32[]{:S(2)}) collective-permute-start(bf16[64,1024]{1,0:T(8,128)(2,1)S(1)} %get-tuple-element.128.refs_0_), channel_id=1, source_target_pairs={{0,2},{1,3},{2,0},{3,1},{4,6},{5,7},{6,4},{7,5},{8,10},{9,11},{10,... | collective-permute-start | bytes 393224 | tf_op jit(solution)/shard_map/ppermute | solution.py:242
  90.4 8.3 %collective-permute-start.26 = (bf16[64,1024]{1,0:T(8,128)(2,1)S(1)}, bf16[64,1024]{1,0:T(8,128)(2,1)S(1)}, u32[]{:S(2)}, u32[]{:S(2)}) collective-permute-start(bf16[64,1024]{1,0:T(8,128)(2,1)S(1)} %get-tuple-element.128.refs_0_), channel_id=1, source_target_pairs={{0,3},{1,0},{2,1},{3,2},{4,7},{5,4},{6,5},{7,6},{8,11},{9,8},{10,9... | collective-permute-start | bytes 393224 | tf_op jit(solution)/shard_map/ppermute | solution.py:242
  91.4 15.5 %collective-permute-start.21 = (f32[64,1024]{1,0:T(8,128)S(1)}, f32[64,1024]{1,0:T(8,128)S(1)}, u32[]{:S(2)}, u32[]{:S(2)}) collective-permute-start(f32[64,1024]{1,0:T(8,128)S(1)} %get-tuple-element.130), channel_id=1, source_target_pairs={{0,1},{1,2},{2,3},{3,0},{4,5},{5,6},{6,7},{7,4},{8,9},{9,10},{10,1... | collective-permute-start | bytes 786440 | tf_op jit(solution)/shard_map/ppermute | solution.py:242
  93.6 13.2 %collective-permute-start.22 = (f32[64,1024]{1,0:T(8,128)S(1)}, f32[64,1024]{1,0:T(8,128)S(1)}, u32[]{:S(2)}, u32[]{:S(2)}) collective-permute-start(f32[64,1024]{1,0:T(8,128)S(1)} %get-tuple-element.131), channel_id=1, source_target_pairs={{0,2},{1,3},{2,0},{3,1},{4,6},{5,7},{6,4},{7,5},{8,10},{9,11},{10,... | collective-permute-start | bytes 786440 | tf_op jit(solution)/shard_map/ppermute | solution.py:242
  94.9 12.0 %collective-permute-start.23 = (f32[64,1024]{1,0:T(8,128)S(1)}, f32[64,1024]{1,0:T(8,128)S(1)}, u32[]{:S(2)}, u32[]{:S(2)}) collective-permute-start(f32[64,1024]{1,0:T(8,128)S(1)} %get-tuple-element.132), channel_id=1, source_target_pairs={{0,3},{1,0},{2,1},{3,2},{4,7},{5,4},{6,5},{7,6},{8,11},{9,8},{10,9... | collective-permute-start | bytes 786440 | tf_op jit(solution)/shard_map/ppermute | solution.py:242
  108.5 8.7 %collective-permute-start.27 = (bf16[80,1024]{1,0:T(8,128)(2,1)S(1)}, bf16[80,1024]{1,0:T(8,128)(2,1)S(1)}, u32[]{:S(2)}, u32[]{:S(2)}) collective-permute-start(bf16[80,1024]{1,0:T(8,128)(2,1)S(1)} %rows.5.refs_0_), channel_id=1, source_target_pairs={{8,16},{9,17},{10,18},{11,19},{12,8},{13,9},{14,10},{15,11},{16,12... | collective-permute-start | bytes 491528 | tf_op jit(solution)/shard_map/ppermute | solution.py:242
  110.9 8.1 %collective-permute-start.28 = (bf16[80,1024]{1,0:T(8,128)(2,1)S(1)}, bf16[80,1024]{1,0:T(8,128)(2,1)S(1)}, u32[]{:S(2)}, u32[]{:S(2)}) collective-permute-start(bf16[80,1024]{1,0:T(8,128)(2,1)S(1)} %rows.5.refs_0_), channel_id=1, source_target_pairs={{8,12},{9,13},{10,14},{11,15},{12,16},{13,17},{14,18},{15,19},{16,... | collective-permute-start | bytes 491528 | tf_op jit(solution)/shard_map/ppermute | solution.py:242
  119.0 5.8 %collective-permute-start.29 = (bf16[64,1024]{1,0:T(8,128)(2,1)S(1)}, bf16[64,1024]{1,0:T(8,128)(2,1)S(1)}, u32[]{:S(2)}, u32[]{:S(2)}) collective-permute-start(bf16[64,1024]{1,0:T(8,128)(2,1)S(1)} %get-tuple-element.142.refs_0_), channel_id=1, source_target_pairs={{0,1},{1,2},{2,3},{3,0},{4,5},{5,6},{6,7},{7,4},{8,9},{9,10},{10,1... | collective-permute-start | bytes 393224 | tf_op jit(solution)/shard_map/ppermute | solution.py:242
  120.9 6.6 %collective-permute-start.30 = (bf16[64,1024]{1,0:T(8,128)(2,1)S(1)}, bf16[64,1024]{1,0:T(8,128)(2,1)S(1)}, u32[]{:S(2)}, u32[]{:S(2)}) collective-permute-start(bf16[64,1024]{1,0:T(8,128)(2,1)S(1)} %get-tuple-element.142.refs_0_), channel_id=1, source_target_pairs={{0,2},{1,3},{2,0},{3,1},{4,6},{5,7},{6,4},{7,5},{8,10},{9,11},{10,... | collective-permute-start | bytes 393224 | tf_op jit(solution)/shard_map/ppermute | solution.py:242
  121.7 7.0 %collective-permute-start.31 = (bf16[64,1024]{1,0:T(8,128)(2,1)S(1)}, bf16[64,1024]{1,0:T(8,128)(2,1)S(1)}, u32[]{:S(2)}, u32[]{:S(2)}) collective-permute-start(bf16[64,1024]{1,0:T(8,128)(2,1)S(1)} %get-tuple-element.142.refs_0_), channel_id=1, source_target_pairs={{0,3},{1,0},{2,1},{3,2},{4,7},{5,4},{6,5},{7,6},{8,11},{9,8},{10,9... | collective-permute-start | bytes 393224 | tf_op jit(solution)/shard_map/ppermute | solution.py:242

commit v6 on v5

--- a/solution.py
+++ b/solution.py
@@ -344,7 +344,7 @@
     row_factor = {(t[0], source): out for (t, source), out in zip(pairs, prepared)}
     tile_factor = prepared[len(pairs) : len(pairs) + NCOL]
     extra = prepared[len(pairs) + NCOL :]
-    parts[-1], picked[1] = lax.optimization_barrier((parts[-1], picked[1]))
+    parts[-1], picked[1:3] = lax.optimization_barrier((parts[-1], picked[1:3]))
     rows = kernel_call(
         start_kernel,
         jax.ShapeDtypeStruct((share + EXTRA, members), BF16),
@@ -357,7 +357,7 @@
     done = []
     for colour in range(NCOL):
         if colour == 0:
-            whole, variance, picked[2:] = joined(rows, colour, picked[2:])
+            whole, variance, picked[3:] = joined(rows, colour, picked[3:])
         else:
             whole, variance, state = joined(rows, colour, state)
         pieces = spread(whole)

time: 142 us -> 142 us (level); the launches traced: 140 us -> 142 us
  starting transfers between devices: 43.6 us -> 45.2 us
    ppermute x32, starting transfers between devices: 43.6 us -> 45.2 us  [hop(): return lax.ppermute(value, AXES, flat)]
  transfers between devices with their start and end apart: 32 -> 32, of which waited for: 20 -> 19; matrix products, arithmetic and copies ran while one was open for 0% -> 0% of each run, Pallas kernels for 29% -> 28%
where the time goes in v6:
time: 142 us
  Pallas kernels  56 us (39%)
  starting transfers between devices  45.2 us (32%)
  waiting for transfers between devices  37.5 us (26%)
  local copies, waits for them, and re-layouts  2.55 us (2%)
    pallas_call x17, Pallas kernels, kernel_call(): pl.pallas_call(body, out_shape=out, in_specs=[scalar if n in smem else wh...  46.3 us
    ppermute x32, starting transfers between devices, hop(): return lax.ppermute(value, AXES, flat)  45.2 us
    ppermute x32, waiting for transfers between devices, hop(): return lax.ppermute(value, AXES, flat)  37.5 us
    pallas_call x4, Pallas kernels, move_tile(): pl.pallas_call(tile_kernel, out_shape=jax.ShapeDtypeStruct(state.shape, F...  9.74 us
  transfers between devices with their start and end apart: 32, of which 19 were waited for; matrix products, arithmetic and copies ran while one was open for 0% of the time, Pallas kernels for 28%

profile of v6, /device:TPU:6, one launch (start us, length us, event | category | flops | bytes accessed | tf_op | source)
XLA Modules:
  0.0 141.6 jit_solution(7936876666532093328)
XLA Ops:
  0.1 1.6 %copy-done = f32[512,1024]{1,0:T(8,128)S(1)} copy-done((f32[512,1024]{1,0:T(8,128)S(1)}, f32[512,1024]{1,0:T(8,128)}, u32[]{:S(2)}) %copy-start) | copy-done | bytes 2097176
  1.7 0.8 copy-done.2
  2.5 1.1 pick.4
  3.6 2.3 %collective-permute-start = (bf16[64,1024]{1,0:T(8,128)(2,1)S(1)}, bf16[64,1024]{1,0:T(8,128)(2,1)S(1)}, u32[]{:S(2)}, u32[]{:S(2)}) collective-permute-start(bf16[64,1024]{1,0:T(8,128)(2,1)S(1)} %get-tuple-element.76), channel_id=1, source_target_pairs={{0,1},{1,2},{2,3},{3,0},{4,5},{5,6},{6,7},{7,4},{8,9},{9,10},{10,1... | collective-permute-start | bytes 393224 | tf_op jit(solution)/shard_map/ppermute | solution.py:242
  5.9 0.7 collective-permute-start.1
  6.6 0.3 collective-permute-start.2
  7.0 1.9 %setup.1 = (f32[64,1]{1,0:T(8,128)S(1)}, f32[64,1]{1,0:T(8,128)S(1)}, f32[64,1]{1,0:T(8,128)S(1)}, f32[64,1]{1,0:T(8,128)S(1)}, f32[64,1]{1,0:T(8,128)S(1)}, /*i...) custom-call(s32[64,256]{1,0:T(8,128)S(1)} %copy-done.3, ...), custom_call_target="tpu_custom_call" | custom-call | flops 1000000 | bytes 202268 | tf_op jit(solution)/shard_map/setup/pallas_call | solution.py:25
  8.9 2.4 %pick.5 = (f32[64,1024]{1,0:T(8,128)S(1)}, f32[64,1024]{1,0:T(8,128)S(1)}, f32[64,1024]{1,0:T(8,128)S(1)}, f32[64,1024]{1,0:T(8,128)S(1)}) custom-call(f32[512,1024]{1,0:T(8,128)S(1)} %copy-done.1, s32[64,256]{1,0:T(8,128)S(1)} %copy-done.3, s32[1,3]{1,0:T(1,128)S(1)} %add_bitcast_fusion.place), custom_call_target="tpu_custom_call" | custom-call | flops 805306368 | bytes 3211276 | tf_op jit(solution)/shard_map/pick/pallas_call | solution.py:25
  11.3 2.4 %pick.6 = (f32[64,1024]{1,0:T(8,128)S(1)}, f32[64,1024]{1,0:T(8,128)S(1)}, f32[64,1024]{1,0:T(8,128)S(1)}, f32[64,1024]{1,0:T(8,128)S(1)}) custom-call(f32[512,1024]{1,0:T(8,128)S(1)} %copy-done.1, s32[64,256]{1,0:T(8,128)S(1)} %copy-done.3, s32[1,3]{1,0:T(1,128)S(1)} %add_bitcast_fusion.place), custom_call_target="tpu_custom_call" | custom-call | flops 805306368 | bytes 3211276 | tf_op jit(solution)/shard_map/pick/pallas_call | solution.py:25
  13.7 0.3 collective-permute-done.2.refs_3_
  13.9 6.8 %collective-permute-start.3 = (bf16[80,1024]{1,0:T(8,128)(2,1)S(1)}, bf16[80,1024]{1,0:T(8,128)(2,1)S(1)}, u32[]{:S(2)}, u32[]{:S(2)}) collective-permute-start(bf16[80,1024]{1,0:T(8,128)(2,1)S(1)} %start.1.refs_0_), channel_id=1, source_target_pairs={{252,4},{253,5},{254,6},{255,7},{0,252},{1,253},{2,254},{3,255},{4... | collective-permute-start | bytes 491528 | tf_op jit(solution)/shard_map/ppermute | solution.py:242
  20.7 2.4 %pick.7 = (f32[64,1024]{1,0:T(8,128)S(1)}, f32[64,1024]{1,0:T(8,128)S(1)}, f32[64,1024]{1,0:T(8,128)S(1)}, f32[64,1024]{1,0:T(8,128)S(1)}) custom-call(f32[512,1024]{1,0:T(8,128)S(1)} %copy-done.1, s32[64,256]{1,0:T(8,128)S(1)} %copy-done.3, s32[1,3]{1,0:T(1,128)S(1)} %add_bitcast_fusion.place), custom_call_target="tpu_custom_call" | custom-call | flops 805306368 | bytes 3211276 | tf_op jit(solution)/shard_map/pick/pallas_call | solution.py:25
  23.1 1.7 %collective-permute-done.3.refs_2_ = bf16[80,1024]{1,0:T(8,128)(2,1)S(1)} collective-permute-done((bf16[80,1024]{1,0:T(8,128)(2,1)S(1)}, bf16[80,1024]{1,0:T(8,128)(2,1)S(1)}, u32[]{:S(2)}, u32[]{:S(2)}) %collective-permute-start.3) | collective-permute-done | bytes 163872 | tf_op jit(solution)/shard_map/ppermute | solution.py:242
  24.8 4.0 %collective-permute-done.4.refs_1_ = bf16[80,1024]{1,0:T(8,128)(2,1)S(1)} collective-permute-done((bf16[80,1024]{1,0:T(8,128)(2,1)S(1)}, bf16[80,1024]{1,0:T(8,128)(2,1)S(1)}, u32[]{:S(2)}, u32[]{:S(2)}) %collective-permute-start.4) | collective-permute-done | bytes 163872 | tf_op jit(solution)/shard_map/ppermute | solution.py:242
  28.8 3.0 %collective-permute-start.8 = (bf16[64,1024]{1,0:T(8,128)(2,1)S(1)}, bf16[64,1024]{1,0:T(8,128)(2,1)S(1)}, u32[]{:S(2)}, u32[]{:S(2)}) collective-permute-start(bf16[64,1024]{1,0:T(8,128)(2,1)S(1)} %get-tuple-element.106.refs_0_), channel_id=1, source_target_pairs={{0,1},{1,2},{2,3},{3,0},{4,5},{5,6},{6,7},{7,4},{8,9},{9,10},{10,1... | collective-permute-start | bytes 393224 | tf_op jit(solution)/shard_map/ppermute | solution.py:242
  32.0 1.3 collective-permute-start.10
  33.3 1.9 %collective-permute-start.5 = (f32[64,1024]{1,0:T(8,128)S(1)}, f32[64,1024]{1,0:T(8,128)S(1)}, u32[]{:S(2)}, u32[]{:S(2)}) collective-permute-start(f32[64,1024]{1,0:T(8,128)S(1)} %get-tuple-element.108), channel_id=1, source_target_pairs={{0,1},{1,2},{2,3},{3,0},{4,5},{5,6},{6,7},{7,4},{8,9},{9,10},{10,1... | collective-permute-start | bytes 786440 | tf_op jit(solution)/shard_map/ppermute | solution.py:242
  35.2 2.2 %collective-permute-start.6 = (f32[64,1024]{1,0:T(8,128)S(1)}, f32[64,1024]{1,0:T(8,128)S(1)}, u32[]{:S(2)}, u32[]{:S(2)}) collective-permute-start(f32[64,1024]{1,0:T(8,128)S(1)} %get-tuple-element.109), channel_id=1, source_target_pairs={{0,2},{1,3},{2,0},{3,1},{4,6},{5,7},{6,4},{7,5},{8,10},{9,11},{10,... | collective-permute-start | bytes 786440 | tf_op jit(solution)/shard_map/ppermute | solution.py:242
  37.4 0.4 collective-permute-done.8.refs_1_
  37.8 2.0 %collective-permute-done.9.refs_2_ = bf16[64,1024]{1,0:T(8,128)(2,1)S(1)} collective-permute-done((bf16[64,1024]{1,0:T(8,128)(2,1)S(1)}, bf16[64,1024]{1,0:T(8,128)(2,1)S(1)}, u32[]{:S(2)}, u32[]{:S(2)}) %collective-permute-start.9) | collective-permute-done | bytes 131104 | tf_op jit(solution)/shard_map/ppermute | solution.py:242
  39.8 1.6 %collective-permute-done.10.refs_3_ = bf16[64,1024]{1,0:T(8,128)(2,1)S(1)} collective-permute-done((bf16[64,1024]{1,0:T(8,128)(2,1)S(1)}, bf16[64,1024]{1,0:T(8,128)(2,1)S(1)}, u32[]{:S(2)}, u32[]{:S(2)}) %collective-permute-start.10) | collective-permute-done | bytes 131104 | tf_op jit(solution)/shard_map/ppermute | solution.py:242
  41.4 8.2 %root.4.refs_4_.transformed = bf16[256,1024]{1,0:T(8,128)(2,1)S(1)} custom-call(bf16[64,1024]{1,0:T(8,128)(2,1)S(1)} %get-tuple-element.106.refs_0_, bf16[64,1024]{1,0:T(8,128)(2,1)S(1)} %collective-permute-done.8.refs_1_, bf16[64,1024]{1,0:T(8,128)(2,1)S(1)} %collective-permute-done.9.refs_2_, bf16[64,1024]{1,0:T(8,128)(2,1)S(1)} %collective-permute-done.10.refs_3_, ...), custom_call_target="tpu_custom_call" | custom-call | flops 8000000000 | bytes 1049600 | tf_op jit(solution)/shard_map/root/pallas_call | solution.py:25
  49.6 0.6 rows.3.refs_0_
  50.2 0.3 collective-permute-start.12
  50.5 0.5 collective-permute-start.11
  51.0 2.2 %tile.4.state = f32[512,1024]{1,0:T(8,128)S(1)} custom-call(f32[512,1024]{1,0:T(8,128)S(1)} %copy-done.1, bf16[256,1024]{1,0:T(8,128)(2,1)S(1)} %root.4.refs_4_.transformed, f32[1,1]{1,0:T(1,128)} %get-tuple-element.114.factor), custom_call_target="tpu_custom_call" | custom-call | flops 536870912 | bytes 4194304 | tf_op jit(solution)/shard_map/tile/pallas_call | solution.py:301
  53.2 1.6 %collective-permute-done.12.refs_2_ = bf16[80,1024]{1,0:T(8,128)(2,1)S(1)} collective-permute-done((bf16[80,1024]{1,0:T(8,128)(2,1)S(1)}, bf16[80,1024]{1,0:T(8,128)(2,1)S(1)}, u32[]{:S(2)}, u32[]{:S(2)}) %collective-permute-start.12) | collective-permute-done | bytes 163872 | tf_op jit(solution)/shard_map/ppermute | solution.py:242
  54.9 1.0 collective-permute-done.11.refs_1_
  55.9 1.9 %collective-permute-start.16 = (bf16[64,1024]{1,0:T(8,128)(2,1)S(1)}, bf16[64,1024]{1,0:T(8,128)(2,1)S(1)}, u32[]{:S(2)}, u32[]{:S(2)}) collective-permute-start(bf16[64,1024]{1,0:T(8,128)(2,1)S(1)} %get-tuple-element.116.refs_0_), channel_id=1, source_target_pairs={{0,1},{1,2},{2,3},{3,0},{4,5},{5,6},{6,7},{7,4},{8,9},{9,10},{10,1... | collective-permute-start | bytes 393224 | tf_op jit(solution)/shard_map/ppermute | solution.py:242
  57.8 0.8 collective-permute-start.17
  58.5 1.3 collective-permute-start.18
  59.8 1.9 %collective-permute-start.13 = (f32[64,1024]{1,0:T(8,128)S(1)}, f32[64,1024]{1,0:T(8,128)S(1)}, u32[]{:S(2)}, u32[]{:S(2)}) collective-permute-start(f32[64,1024]{1,0:T(8,128)S(1)} %get-tuple-element.118), channel_id=1, source_target_pairs={{0,1},{1,2},{2,3},{3,0},{4,5},{5,6},{6,7},{7,4},{8,9},{9,10},{10,1... | collective-permute-start | bytes 786440 | tf_op jit(solution)/shard_map/ppermute | solution.py:242
  61.8 1.6 %collective-permute-start.14 = (f32[64,1024]{1,0:T(8,128)S(1)}, f32[64,1024]{1,0:T(8,128)S(1)}, u32[]{:S(2)}, u32[]{:S(2)}) collective-permute-start(f32[64,1024]{1,0:T(8,128)S(1)} %get-tuple-element.119), channel_id=1, source_target_pairs={{0,2},{1,3},{2,0},{3,1},{4,6},{5,7},{6,4},{7,5},{8,10},{9,11},{10,... | collective-permute-start | bytes 786440 | tf_op jit(solution)/shard_map/ppermute | solution.py:242
  63.3 0.2 collective-permute-start.15
  63.6 2.0 %collective-permute-done.17.refs_2_ = bf16[64,1024]{1,0:T(8,128)(2,1)S(1)} collective-permute-done((bf16[64,1024]{1,0:T(8,128)(2,1)S(1)}, bf16[64,1024]{1,0:T(8,128)(2,1)S(1)}, u32[]{:S(2)}, u32[]{:S(2)}) %collective-permute-start.17) | collective-permute-done | bytes 131104 | tf_op jit(solution)/shard_map/ppermute | solution.py:242
  65.5 6.5 %collective-permute-done.18.refs_3_ = bf16[64,1024]{1,0:T(8,128)(2,1)S(1)} collective-permute-done((bf16[64,1024]{1,0:T(8,128)(2,1)S(1)}, bf16[64,1024]{1,0:T(8,128)(2,1)S(1)}, u32[]{:S(2)}, u32[]{:S(2)}) %collective-permute-start.18) | collective-permute-done | bytes 131104 | tf_op jit(solution)/shard_map/ppermute | solution.py:242
  72.1 8.2 %root.5.refs_6_.transformed = bf16[256,1024]{1,0:T(8,128)(2,1)S(1)} custom-call(bf16[64,1024]{1,0:T(8,128)(2,1)S(1)} %get-tuple-element.116.refs_0_, bf16[64,1024]{1,0:T(8,128)(2,1)S(1)} %collective-permute-done.16.refs_1_, bf16[64,1024]{1,0:T(8,128)(2,1)S(1)} %collective-permute-done.17.refs_2_, bf16[64,1024]{1,0:T(8,128)(2,1)S(1)} %collective-permute-done.18.refs_3_, ...), custom_call_target="tpu_custom_call" | custom-call | flops 8000000000 | bytes 1049600 | tf_op jit(solution)/shard_map/root/pallas_call | solution.py:25
  80.3 1.2 rows.4.refs_0_
  81.5 2.0 %collective-permute-start.19 = (bf16[80,1024]{1,0:T(8,128)(2,1)S(1)}, bf16[80,1024]{1,0:T(8,128)(2,1)S(1)}, u32[]{:S(2)}, u32[]{:S(2)}) collective-permute-start(bf16[80,1024]{1,0:T(8,128)(2,1)S(1)} %rows.4.refs_0_), channel_id=1, source_target_pairs={{4,8},{5,9},{6,10},{7,11},{8,12},{9,13},{10,14},{11,15},{12,4},{13... | collective-permute-start | bytes 491528 | tf_op jit(solution)/shard_map/ppermute | solution.py:242
  83.5 2.1 %tile.5.state = f32[512,1024]{1,0:T(8,128)S(1)} custom-call(f32[512,1024]{1,0:T(8,128)S(1)} %tile.4.state, bf16[256,1024]{1,0:T(8,128)(2,1)S(1)} %root.5.refs_6_.transformed, f32[1,1]{1,0:T(1,128)} %get-tuple-element.126.factor), custom_call_target="tpu_custom_call" | custom-call | flops 536870912 | bytes 4194304 | tf_op jit(solution)/shard_map/tile/pallas_call | solution.py:301
  85.7 1.8 %collective-permute-done.20.refs_2_ = bf16[80,1024]{1,0:T(8,128)(2,1)S(1)} collective-permute-done((bf16[80,1024]{1,0:T(8,128)(2,1)S(1)}, bf16[80,1024]{1,0:T(8,128)(2,1)S(1)}, u32[]{:S(2)}, u32[]{:S(2)}) %collective-permute-start.20) | collective-permute-done | bytes 163872 | tf_op jit(solution)/shard_map/ppermute | solution.py:242
  87.5 3.5 %collective-permute-done.19.refs_1_ = bf16[80,1024]{1,0:T(8,128)(2,1)S(1)} collective-permute-done((bf16[80,1024]{1,0:T(8,128)(2,1)S(1)}, bf16[80,1024]{1,0:T(8,128)(2,1)S(1)}, u32[]{:S(2)}, u32[]{:S(2)}) %collective-permute-start.19) | collective-permute-done | bytes 163872 | tf_op jit(solution)/shard_map/ppermute | solution.py:242
  91.1 1.7 %collective-permute-start.25 = (bf16[64,1024]{1,0:T(8,128)(2,1)S(1)}, bf16[64,1024]{1,0:T(8,128)(2,1)S(1)}, u32[]{:S(2)}, u32[]{:S(2)}) collective-permute-start(bf16[64,1024]{1,0:T(8,128)(2,1)S(1)} %get-tuple-element.128.refs_0_), channel_id=1, source_target_pairs={{0,2},{1,3},{2,0},{3,1},{4,6},{5,7},{6,4},{7,5},{8,10},{9,11},{10,... | collective-permute-start | bytes 393224 | tf_op jit(solution)/shard_map/ppermute | solution.py:242
  92.8 1.3 collective-permute-start.26
  94.1 1.9 %collective-permute-start.21 = (f32[64,1024]{1,0:T(8,128)S(1)}, f32[64,1024]{1,0:T(8,128)S(1)}, u32[]{:S(2)}, u32[]{:S(2)}) collective-permute-start(f32[64,1024]{1,0:T(8,128)S(1)} %get-tuple-element.130), channel_id=1, source_target_pairs={{0,1},{1,2},{2,3},{3,0},{4,5},{5,6},{6,7},{7,4},{8,9},{9,10},{10,1... | collective-permute-start | bytes 786440 | tf_op jit(solution)/shard_map/ppermute | solution.py:242
  96.0 1.2 collective-permute-start.22
  97.3 0.3 collective-permute-done.24.refs_1_
  97.5 1.2 collective-permute-start.23
  98.7 1.3 collective-permute-done.26.refs_3_
  100.0 8.2 %root.6.refs_8_.transformed = bf16[256,1024]{1,0:T(8,128)(2,1)S(1)} custom-call(bf16[64,1024]{1,0:T(8,128)(2,1)S(1)} %get-tuple-element.128.refs_0_, bf16[64,1024]{1,0:T(8,128)(2,1)S(1)} %collective-permute-done.24.refs_1_, bf16[64,1024]{1,0:T(8,128)(2,1)S(1)} %collective-permute-done.25.refs_2_, bf16[64,1024]{1,0:T(8,128)(2,1)S(1)} %collective-permute-done.26.refs_3_, ...), custom_call_target="tpu_custom_call" | custom-call | flops 8000000000 | bytes 1049600 | tf_op jit(solution)/shard_map/root/pallas_call | solution.py:25
  108.2 1.6 %rows.5.refs_0_ = bf16[80,1024]{1,0:T(8,128)(2,1)S(1)} custom-call(f32[64,1024]{1,0:T(8,128)S(1)} %get-tuple-element.129.refs_0_, f32[64,1024]{1,0:T(8,128)S(1)} %collective-permute-done.21.refs_1_, f32[64,1024]{1,0:T(8,128)S(1)} %collective-permute-done.22.refs_2_, f32[64,1024]{1,0:T(8,128)S(1)} %collective-permute-done.23.refs_3_, ...), custom_call_target="tpu_custom_call" | custom-call | flops 201326592 | bytes 2818816 | tf_op jit(solution)/shard_map/rows/pallas_call | solution.py:25
  109.8 2.5 %collective-permute-start.27 = (bf16[80,1024]{1,0:T(8,128)(2,1)S(1)}, bf16[80,1024]{1,0:T(8,128)(2,1)S(1)}, u32[]{:S(2)}, u32[]{:S(2)}) collective-permute-start(bf16[80,1024]{1,0:T(8,128)(2,1)S(1)} %rows.5.refs_0_), channel_id=1, source_target_pairs={{8,16},{9,17},{10,18},{11,19},{12,8},{13,9},{14,10},{15,11},{16,12... | collective-permute-start | bytes 491528 | tf_op jit(solution)/shard_map/ppermute | solution.py:242
  112.3 3.2 %collective-permute-start.28 = (bf16[80,1024]{1,0:T(8,128)(2,1)S(1)}, bf16[80,1024]{1,0:T(8,128)(2,1)S(1)}, u32[]{:S(2)}, u32[]{:S(2)}) collective-permute-start(bf16[80,1024]{1,0:T(8,128)(2,1)S(1)} %rows.5.refs_0_), channel_id=1, source_target_pairs={{8,12},{9,13},{10,14},{11,15},{12,16},{13,17},{14,18},{15,19},{16,... | collective-permute-start | bytes 491528 | tf_op jit(solution)/shard_map/ppermute | solution.py:242
  115.5 2.2 %tile.6.state = f32[512,1024]{1,0:T(8,128)S(1)} custom-call(f32[512,1024]{1,0:T(8,128)S(1)} %tile.5.state, bf16[256,1024]{1,0:T(8,128)(2,1)S(1)} %root.6.refs_8_.transformed, f32[1,1]{1,0:T(1,128)} %get-tuple-element.139.factor), custom_call_target="tpu_custom_call" | custom-call | flops 536870912 | bytes 4194304 | tf_op jit(solution)/shard_map/tile/pallas_call | solution.py:301
  117.7 1.0 collective-permute-done.27.refs_2_
  118.7 1.7 %collective-permute-done.28.refs_1_ = bf16[80,1024]{1,0:T(8,128)(2,1)S(1)} collective-permute-done((bf16[80,1024]{1,0:T(8,128)(2,1)S(1)}, bf16[80,1024]{1,0:T(8,128)(2,1)S(1)}, u32[]{:S(2)}, u32[]{:S(2)}) %collective-permute-start.28) | collective-permute-done | bytes 163872 | tf_op jit(solution)/shard_map/ppermute | solution.py:242
  120.5 2.0 %collective-permute-start.29 = (bf16[64,1024]{1,0:T(8,128)(2,1)S(1)}, bf16[64,1024]{1,0:T(8,128)(2,1)S(1)}, u32[]{:S(2)}, u32[]{:S(2)}) collective-permute-start(bf16[64,1024]{1,0:T(8,128)(2,1)S(1)} %get-tuple-element.142.refs_0_), channel_id=1, source_target_pairs={{0,1},{1,2},{2,3},{3,0},{4,5},{5,6},{6,7},{7,4},{8,9},{9,10},{10,1... | collective-permute-start | bytes 393224 | tf_op jit(solution)/shard_map/ppermute | solution.py:242
  122.5 0.2 collective-permute-start.30
  122.7 0.8 collective-permute-start.31
  123.5 3.0 %collective-permute-done.29.refs_1_ = bf16[64,1024]{1,0:T(8,128)(2,1)S(1)} collective-permute-done((bf16[64,1024]{1,0:T(8,128)(2,1)S(1)}, bf16[64,1024]{1,0:T(8,128)(2,1)S(1)}, u32[]{:S(2)}, u32[]{:S(2)}) %collective-permute-start.29) | collective-permute-done | bytes 131104 | tf_op jit(solution)/shard_map/ppermute | solution.py:242
  126.4 2.7 %collective-permute-done.30.refs_2_ = bf16[64,1024]{1,0:T(8,128)(2,1)S(1)} collective-permute-done((bf16[64,1024]{1,0:T(8,128)(2,1)S(1)}, bf16[64,1024]{1,0:T(8,128)(2,1)S(1)}, u32[]{:S(2)}, u32[]{:S(2)}) %collective-permute-start.30) | collective-permute-done | bytes 131104 | tf_op jit(solution)/shard_map/ppermute | solution.py:242
  129.1 1.2 collective-permute-done.31.refs_3_
  130.3 8.2 %root.7.transformed = bf16[256,1024]{1,0:T(8,128)(2,1)S(1)} custom-call(bf16[64,1024]{1,0:T(8,128)(2,1)S(1)} %get-tuple-element.142.refs_0_, bf16[64,1024]{1,0:T(8,128)(2,1)S(1)} %collective-permute-done.29.refs_1_, bf16[64,1024]{1,0:T(8,128)(2,1)S(1)} %collective-permute-done.30.refs_2_, bf16[64,1024]{1,0:T(8,128)(2,1)S(1)} %collective-permute-done.31.refs_3_, ...), custom_call_target="tpu_custom_call" | custom-call | flops 8000000000 | bytes 1049600 | tf_op jit(solution)/shard_map/root/pallas_call | solution.py:25
  138.4 3.1 %tile.7 = f32[512,1024]{1,0:T(8,128)} custom-call(f32[512,1024]{1,0:T(8,128)S(1)} %tile.6.state, bf16[256,1024]{1,0:T(8,128)(2,1)S(1)} %root.7.transformed, f32[1,1]{1,0:T(1,128)} %get-tuple-element.144.factor), custom_call_target="tpu_custom_call" | custom-call | flops 536870912 | bytes 4194304 | tf_op jit(solution)/shard_map/tile/pallas_call | solution.py:301
  (36 shorter events, 0.7 us)
Async XLA Ops:
  0.0 6.9 %copy-start.5 = (s32[64,3,4]{0,2,1:T(4,128)S(1)}, s32[64,3,4]{0,2,1:T(4,128)}, u32[]{:S(2)}) copy-start(s32[64,3,4]{0,2,1:T(4,128)} %param.7) | copy-start | bytes 9220
  0.0 7.0 %copy-start.4 = (f32[1,256]{1,0:T(1,128)S(1)}, f32[1,256]{1,0:T(1,128)}, u32[]{:S(2)}) copy-start(f32[1,256]{1,0:T(1,128)} %own.1) | copy-start | bytes 3076
  0.1 1.6 %copy-start = (f32[512,1024]{1,0:T(8,128)S(1)}, f32[512,1024]{1,0:T(8,128)}, u32[]{:S(2)}) copy-start(f32[512,1024]{1,0:T(8,128)} %state.9) | copy-start | bytes 6291460
  1.7 0.8 copy-start.2
  2.5 4.5 %copy-start.3 = (s32[64,256]{1,0:T(8,128)S(1)}, s32[64,256]{1,0:T(8,128)}, u32[]{:S(2)}) copy-start(s32[64,256]{1,0:T(8,128)} %obs.9) | copy-start | bytes 196612
  2.5 6.4 %copy-start.1 = (f32[512,1024]{1,0:T(8,128)S(1)}, f32[512,1024]{1,0:T(8,128)}, u32[]{:S(2)}) copy-start(f32[512,1024]{1,0:T(8,128)} %state.9) | copy-start | bytes 6291460
  3.6 10.3 %collective-permute-start = (bf16[64,1024]{1,0:T(8,128)(2,1)S(1)}, bf16[64,1024]{1,0:T(8,128)(2,1)S(1)}, u32[]{:S(2)}, u32[]{:S(2)}) collective-permute-start(bf16[64,1024]{1,0:T(8,128)(2,1)S(1)} %get-tuple-element.76), channel_id=1, source_target_pairs={{0,1},{1,2},{2,3},{3,0},{4,5},{5,6},{6,7},{7,4},{8,9},{9,10},{10,1... | collective-permute-start | bytes 393224 | tf_op jit(solution)/shard_map/ppermute | solution.py:242
  5.9 8.0 %collective-permute-start.1 = (bf16[64,1024]{1,0:T(8,128)(2,1)S(1)}, bf16[64,1024]{1,0:T(8,128)(2,1)S(1)}, u32[]{:S(2)}, u32[]{:S(2)}) collective-permute-start(bf16[64,1024]{1,0:T(8,128)(2,1)S(1)} %get-tuple-element.77), channel_id=1, source_target_pairs={{0,2},{1,3},{2,0},{3,1},{4,6},{5,7},{6,4},{7,5},{8,10},{9,11},{10,... | collective-permute-start | bytes 393224 | tf_op jit(solution)/shard_map/ppermute | solution.py:242
  6.6 7.3 %collective-permute-start.2 = (bf16[64,1024]{1,0:T(8,128)(2,1)S(1)}, bf16[64,1024]{1,0:T(8,128)(2,1)S(1)}, u32[]{:S(2)}, u32[]{:S(2)}) collective-permute-start(bf16[64,1024]{1,0:T(8,128)(2,1)S(1)} %get-tuple-element.78), channel_id=1, source_target_pairs={{0,3},{1,0},{2,1},{3,2},{4,7},{5,4},{6,5},{7,6},{8,11},{9,8},{10,9... | collective-permute-start | bytes 393224 | tf_op jit(solution)/shard_map/ppermute | solution.py:242
  13.9 10.9 %collective-permute-start.3 = (bf16[80,1024]{1,0:T(8,128)(2,1)S(1)}, bf16[80,1024]{1,0:T(8,128)(2,1)S(1)}, u32[]{:S(2)}, u32[]{:S(2)}) collective-permute-start(bf16[80,1024]{1,0:T(8,128)(2,1)S(1)} %start.1.refs_0_), channel_id=1, source_target_pairs={{252,4},{253,5},{254,6},{255,7},{0,252},{1,253},{2,254},{3,255},{4... | collective-permute-start | bytes 491528 | tf_op jit(solution)/shard_map/ppermute | solution.py:242
  20.7 8.1 %collective-permute-start.4 = (bf16[80,1024]{1,0:T(8,128)(2,1)S(1)}, bf16[80,1024]{1,0:T(8,128)(2,1)S(1)}, u32[]{:S(2)}, u32[]{:S(2)}) collective-permute-start(bf16[80,1024]{1,0:T(8,128)(2,1)S(1)} %start.1.refs_0_), channel_id=1, source_target_pairs={{252,0},{253,1},{254,2},{255,3},{0,4},{1,5},{2,6},{3,7},{4,252},{5... | collective-permute-start | bytes 491528 | tf_op jit(solution)/shard_map/ppermute | solution.py:242
  28.8 9.0 %collective-permute-start.8 = (bf16[64,1024]{1,0:T(8,128)(2,1)S(1)}, bf16[64,1024]{1,0:T(8,128)(2,1)S(1)}, u32[]{:S(2)}, u32[]{:S(2)}) collective-permute-start(bf16[64,1024]{1,0:T(8,128)(2,1)S(1)} %get-tuple-element.106.refs_0_), channel_id=1, source_target_pairs={{0,1},{1,2},{2,3},{3,0},{4,5},{5,6},{6,7},{7,4},{8,9},{9,10},{10,1... | collective-permute-start | bytes 393224 | tf_op jit(solution)/shard_map/ppermute | solution.py:242
  31.8 8.0 %collective-permute-start.9 = (bf16[64,1024]{1,0:T(8,128)(2,1)S(1)}, bf16[64,1024]{1,0:T(8,128)(2,1)S(1)}, u32[]{:S(2)}, u32[]{:S(2)}) collective-permute-start(bf16[64,1024]{1,0:T(8,128)(2,1)S(1)} %get-tuple-element.106.refs_0_), channel_id=1, source_target_pairs={{0,2},{1,3},{2,0},{3,1},{4,6},{5,7},{6,4},{7,5},{8,10},{9,11},{10,... | collective-permute-start | bytes 393224 | tf_op jit(solution)/shard_map/ppermute | solution.py:242
  32.0 9.4 %collective-permute-start.10 = (bf16[64,1024]{1,0:T(8,128)(2,1)S(1)}, bf16[64,1024]{1,0:T(8,128)(2,1)S(1)}, u32[]{:S(2)}, u32[]{:S(2)}) collective-permute-start(bf16[64,1024]{1,0:T(8,128)(2,1)S(1)} %get-tuple-element.106.refs_0_), channel_id=1, source_target_pairs={{0,3},{1,0},{2,1},{3,2},{4,7},{5,4},{6,5},{7,6},{8,11},{9,8},{10,9... | collective-permute-start | bytes 393224 | tf_op jit(solution)/shard_map/ppermute | solution.py:242
  33.3 16.3 %collective-permute-start.5 = (f32[64,1024]{1,0:T(8,128)S(1)}, f32[64,1024]{1,0:T(8,128)S(1)}, u32[]{:S(2)}, u32[]{:S(2)}) collective-permute-start(f32[64,1024]{1,0:T(8,128)S(1)} %get-tuple-element.108), channel_id=1, source_target_pairs={{0,1},{1,2},{2,3},{3,0},{4,5},{5,6},{6,7},{7,4},{8,9},{9,10},{10,1... | collective-permute-start | bytes 786440 | tf_op jit(solution)/shard_map/ppermute | solution.py:242
  35.2 14.4 %collective-permute-start.6 = (f32[64,1024]{1,0:T(8,128)S(1)}, f32[64,1024]{1,0:T(8,128)S(1)}, u32[]{:S(2)}, u32[]{:S(2)}) collective-permute-start(f32[64,1024]{1,0:T(8,128)S(1)} %get-tuple-element.109), channel_id=1, source_target_pairs={{0,2},{1,3},{2,0},{3,1},{4,6},{5,7},{6,4},{7,5},{8,10},{9,11},{10,... | collective-permute-start | bytes 786440 | tf_op jit(solution)/shard_map/ppermute | solution.py:242
  37.8 11.8 %collective-permute-start.7 = (f32[64,1024]{1,0:T(8,128)S(1)}, f32[64,1024]{1,0:T(8,128)S(1)}, u32[]{:S(2)}, u32[]{:S(2)}) collective-permute-start(f32[64,1024]{1,0:T(8,128)S(1)} %get-tuple-element.110), channel_id=1, source_target_pairs={{0,3},{1,0},{2,1},{3,2},{4,7},{5,4},{6,5},{7,6},{8,11},{9,8},{10,9... | collective-permute-start | bytes 786440 | tf_op jit(solution)/shard_map/ppermute | solution.py:242
  50.2 4.7 %collective-permute-start.12 = (bf16[80,1024]{1,0:T(8,128)(2,1)S(1)}, bf16[80,1024]{1,0:T(8,128)(2,1)S(1)}, u32[]{:S(2)}, u32[]{:S(2)}) collective-permute-start(bf16[80,1024]{1,0:T(8,128)(2,1)S(1)} %rows.3.refs_0_), channel_id=1, source_target_pairs={{0,8},{1,9},{2,10},{3,11},{4,0},{5,1},{6,2},{7,3},{8,4},{9,5},{10,... | collective-permute-start | bytes 491528 | tf_op jit(solution)/shard_map/ppermute | solution.py:242
  50.5 5.4 %collective-permute-start.11 = (bf16[80,1024]{1,0:T(8,128)(2,1)S(1)}, bf16[80,1024]{1,0:T(8,128)(2,1)S(1)}, u32[]{:S(2)}, u32[]{:S(2)}) collective-permute-start(bf16[80,1024]{1,0:T(8,128)(2,1)S(1)} %rows.3.refs_0_), channel_id=1, source_target_pairs={{0,4},{1,5},{2,6},{3,7},{4,8},{5,9},{6,10},{7,11},{8,0},{9,1},{10,... | collective-permute-start | bytes 491528 | tf_op jit(solution)/shard_map/ppermute | solution.py:242
  55.9 7.4 %collective-permute-start.16 = (bf16[64,1024]{1,0:T(8,128)(2,1)S(1)}, bf16[64,1024]{1,0:T(8,128)(2,1)S(1)}, u32[]{:S(2)}, u32[]{:S(2)}) collective-permute-start(bf16[64,1024]{1,0:T(8,128)(2,1)S(1)} %get-tuple-element.116.refs_0_), channel_id=1, source_target_pairs={{0,1},{1,2},{2,3},{3,0},{4,5},{5,6},{6,7},{7,4},{8,9},{9,10},{10,1... | collective-permute-start | bytes 393224 | tf_op jit(solution)/shard_map/ppermute | solution.py:242
  57.8 7.8 %collective-permute-start.17 = (bf16[64,1024]{1,0:T(8,128)(2,1)S(1)}, bf16[64,1024]{1,0:T(8,128)(2,1)S(1)}, u32[]{:S(2)}, u32[]{:S(2)}) collective-permute-start(bf16[64,1024]{1,0:T(8,128)(2,1)S(1)} %get-tuple-element.116.refs_0_), channel_id=1, source_target_pairs={{0,2},{1,3},{2,0},{3,1},{4,6},{5,7},{6,4},{7,5},{8,10},{9,11},{10,... | collective-permute-start | bytes 393224 | tf_op jit(solution)/shard_map/ppermute | solution.py:242
  58.5 13.5 %collective-permute-start.18 = (bf16[64,1024]{1,0:T(8,128)(2,1)S(1)}, bf16[64,1024]{1,0:T(8,128)(2,1)S(1)}, u32[]{:S(2)}, u32[]{:S(2)}) collective-permute-start(bf16[64,1024]{1,0:T(8,128)(2,1)S(1)} %get-tuple-element.116.refs_0_), channel_id=1, source_target_pairs={{0,3},{1,0},{2,1},{3,2},{4,7},{5,4},{6,5},{7,6},{8,11},{9,8},{10,9... | collective-permute-start | bytes 393224 | tf_op jit(solution)/shard_map/ppermute | solution.py:242
  59.8 20.4 %collective-permute-start.13 = (f32[64,1024]{1,0:T(8,128)S(1)}, f32[64,1024]{1,0:T(8,128)S(1)}, u32[]{:S(2)}, u32[]{:S(2)}) collective-permute-start(f32[64,1024]{1,0:T(8,128)S(1)} %get-tuple-element.118), channel_id=1, source_target_pairs={{0,1},{1,2},{2,3},{3,0},{4,5},{5,6},{6,7},{7,4},{8,9},{9,10},{10,1... | collective-permute-start | bytes 786440 | tf_op jit(solution)/shard_map/ppermute | solution.py:242
  61.8 18.5 %collective-permute-start.14 = (f32[64,1024]{1,0:T(8,128)S(1)}, f32[64,1024]{1,0:T(8,128)S(1)}, u32[]{:S(2)}, u32[]{:S(2)}) collective-permute-start(f32[64,1024]{1,0:T(8,128)S(1)} %get-tuple-element.119), channel_id=1, source_target_pairs={{0,2},{1,3},{2,0},{3,1},{4,6},{5,7},{6,4},{7,5},{8,10},{9,11},{10,... | collective-permute-start | bytes 786440 | tf_op jit(solution)/shard_map/ppermute | solution.py:242
  63.3 17.0 %collective-permute-start.15 = (f32[64,1024]{1,0:T(8,128)S(1)}, f32[64,1024]{1,0:T(8,128)S(1)}, u32[]{:S(2)}, u32[]{:S(2)}) collective-permute-start(f32[64,1024]{1,0:T(8,128)S(1)} %get-tuple-element.120), channel_id=1, source_target_pairs={{0,3},{1,0},{2,1},{3,2},{4,7},{5,4},{6,5},{7,6},{8,11},{9,8},{10,9... | collective-permute-start | bytes 786440 | tf_op jit(solution)/shard_map/ppermute | solution.py:242
  81.4 6.0 %collective-permute-start.20 = (bf16[80,1024]{1,0:T(8,128)(2,1)S(1)}, bf16[80,1024]{1,0:T(8,128)(2,1)S(1)}, u32[]{:S(2)}, u32[]{:S(2)}) collective-permute-start(bf16[80,1024]{1,0:T(8,128)(2,1)S(1)} %rows.4.refs_0_), channel_id=1, source_target_pairs={{4,12},{5,13},{6,14},{7,15},{8,4},{9,5},{10,6},{11,7},{12,8},{13,9... | collective-permute-start | bytes 491528 | tf_op jit(solution)/shard_map/ppermute | solution.py:242
  81.5 9.4 %collective-permute-start.19 = (bf16[80,1024]{1,0:T(8,128)(2,1)S(1)}, bf16[80,1024]{1,0:T(8,128)(2,1)S(1)}, u32[]{:S(2)}, u32[]{:S(2)}) collective-permute-start(bf16[80,1024]{1,0:T(8,128)(2,1)S(1)} %rows.4.refs_0_), channel_id=1, source_target_pairs={{4,8},{5,9},{6,10},{7,11},{8,12},{9,13},{10,14},{11,15},{12,4},{13... | collective-permute-start | bytes 491528 | tf_op jit(solution)/shard_map/ppermute | solution.py:242
  91.0 6.5 %collective-permute-start.24 = (bf16[64,1024]{1,0:T(8,128)(2,1)S(1)}, bf16[64,1024]{1,0:T(8,128)(2,1)S(1)}, u32[]{:S(2)}, u32[]{:S(2)}) collective-permute-start(bf16[64,1024]{1,0:T(8,128)(2,1)S(1)} %get-tuple-element.128.refs_0_), channel_id=1, source_target_pairs={{0,1},{1,2},{2,3},{3,0},{4,5},{5,6},{6,7},{7,4},{8,9},{9,10},{10,1... | collective-permute-start | bytes 393224 | tf_op jit(solution)/shard_map/ppermute | solution.py:242
  91.1 7.6 %collective-permute-start.25 = (bf16[64,1024]{1,0:T(8,128)(2,1)S(1)}, bf16[64,1024]{1,0:T(8,128)(2,1)S(1)}, u32[]{:S(2)}, u32[]{:S(2)}) collective-permute-start(bf16[64,1024]{1,0:T(8,128)(2,1)S(1)} %get-tuple-element.128.refs_0_), channel_id=1, source_target_pairs={{0,2},{1,3},{2,0},{3,1},{4,6},{5,7},{6,4},{7,5},{8,10},{9,11},{10,... | collective-permute-start | bytes 393224 | tf_op jit(solution)/shard_map/ppermute | solution.py:242
  92.8 7.2 %collective-permute-start.26 = (bf16[64,1024]{1,0:T(8,128)(2,1)S(1)}, bf16[64,1024]{1,0:T(8,128)(2,1)S(1)}, u32[]{:S(2)}, u32[]{:S(2)}) collective-permute-start(bf16[64,1024]{1,0:T(8,128)(2,1)S(1)} %get-tuple-element.128.refs_0_), channel_id=1, source_target_pairs={{0,3},{1,0},{2,1},{3,2},{4,7},{5,4},{6,5},{7,6},{8,11},{9,8},{10,9... | collective-permute-start | bytes 393224 | tf_op jit(solution)/shard_map/ppermute | solution.py:242
  94.1 14.0 %collective-permute-start.21 = (f32[64,1024]{1,0:T(8,128)S(1)}, f32[64,1024]{1,0:T(8,128)S(1)}, u32[]{:S(2)}, u32[]{:S(2)}) collective-permute-start(f32[64,1024]{1,0:T(8,128)S(1)} %get-tuple-element.130), channel_id=1, source_target_pairs={{0,1},{1,2},{2,3},{3,0},{4,5},{5,6},{6,7},{7,4},{8,9},{9,10},{10,1... | collective-permute-start | bytes 786440 | tf_op jit(solution)/shard_map/ppermute | solution.py:242
  96.0 12.1 %collective-permute-start.22 = (f32[64,1024]{1,0:T(8,128)S(1)}, f32[64,1024]{1,0:T(8,128)S(1)}, u32[]{:S(2)}, u32[]{:S(2)}) collective-permute-start(f32[64,1024]{1,0:T(8,128)S(1)} %get-tuple-element.131), channel_id=1, source_target_pairs={{0,2},{1,3},{2,0},{3,1},{4,6},{5,7},{6,4},{7,5},{8,10},{9,11},{10,... | collective-permute-start | bytes 786440 | tf_op jit(solution)/shard_map/ppermute | solution.py:242
  97.5 10.7 %collective-permute-start.23 = (f32[64,1024]{1,0:T(8,128)S(1)}, f32[64,1024]{1,0:T(8,128)S(1)}, u32[]{:S(2)}, u32[]{:S(2)}) collective-permute-start(f32[64,1024]{1,0:T(8,128)S(1)} %get-tuple-element.132), channel_id=1, source_target_pairs={{0,3},{1,0},{2,1},{3,2},{4,7},{5,4},{6,5},{7,6},{8,11},{9,8},{10,9... | collective-permute-start | bytes 786440 | tf_op jit(solution)/shard_map/ppermute | solution.py:242
  109.8 8.9 %collective-permute-start.27 = (bf16[80,1024]{1,0:T(8,128)(2,1)S(1)}, bf16[80,1024]{1,0:T(8,128)(2,1)S(1)}, u32[]{:S(2)}, u32[]{:S(2)}) collective-permute-start(bf16[80,1024]{1,0:T(8,128)(2,1)S(1)} %rows.5.refs_0_), channel_id=1, source_target_pairs={{8,16},{9,17},{10,18},{11,19},{12,8},{13,9},{14,10},{15,11},{16,12... | collective-permute-start | bytes 491528 | tf_op jit(solution)/shard_map/ppermute | solution.py:242
  112.3 8.2 %collective-permute-start.28 = (bf16[80,1024]{1,0:T(8,128)(2,1)S(1)}, bf16[80,1024]{1,0:T(8,128)(2,1)S(1)}, u32[]{:S(2)}, u32[]{:S(2)}) collective-permute-start(bf16[80,1024]{1,0:T(8,128)(2,1)S(1)} %rows.5.refs_0_), channel_id=1, source_target_pairs={{8,12},{9,13},{10,14},{11,15},{12,16},{13,17},{14,18},{15,19},{16,... | collective-permute-start | bytes 491528 | tf_op jit(solution)/shard_map/ppermute | solution.py:242
  120.5 5.9 %collective-permute-start.29 = (bf16[64,1024]{1,0:T(8,128)(2,1)S(1)}, bf16[64,1024]{1,0:T(8,128)(2,1)S(1)}, u32[]{:S(2)}, u32[]{:S(2)}) collective-permute-start(bf16[64,1024]{1,0:T(8,128)(2,1)S(1)} %get-tuple-element.142.refs_0_), channel_id=1, source_target_pairs={{0,1},{1,2},{2,3},{3,0},{4,5},{5,6},{6,7},{7,4},{8,9},{9,10},{10,1... | collective-permute-start | bytes 393224 | tf_op jit(solution)/shard_map/ppermute | solution.py:242
  122.5 6.6 %collective-permute-start.30 = (bf16[64,1024]{1,0:T(8,128)(2,1)S(1)}, bf16[64,1024]{1,0:T(8,128)(2,1)S(1)}, u32[]{:S(2)}, u32[]{:S(2)}) collective-permute-start(bf16[64,1024]{1,0:T(8,128)(2,1)S(1)} %get-tuple-element.142.refs_0_), channel_id=1, source_target_pairs={{0,2},{1,3},{2,0},{3,1},{4,6},{5,7},{6,4},{7,5},{8,10},{9,11},{10,... | collective-permute-start | bytes 393224 | tf_op jit(solution)/shard_map/ppermute | solution.py:242
  122.7 7.6 %collective-permute-start.31 = (bf16[64,1024]{1,0:T(8,128)(2,1)S(1)}, bf16[64,1024]{1,0:T(8,128)(2,1)S(1)}, u32[]{:S(2)}, u32[]{:S(2)}) collective-permute-start(bf16[64,1024]{1,0:T(8,128)(2,1)S(1)} %get-tuple-element.142.refs_0_), channel_id=1, source_target_pairs={{0,3},{1,0},{2,1},{3,2},{4,7},{5,4},{6,5},{7,6},{8,11},{9,8},{10,9... | collective-permute-start | bytes 393224 | tf_op jit(solution)/shard_map/ppermute | solution.py:242
